TPU v7x, 128 devices: a whole 4x4x4 slice. The times are simulated.
128 devices in a mesh: expert: 32 (over x, y, core), tensor: 4 (over z).
Axes of the slice: x: 4, y: 4, z: 4, core: 2. Of those that a mesh axis runs over, the one named last changes fastest.
Arguments:
- tokens: bfloat16 [65536, 512], P(('expert', 'tensor')), may hold values from -6 to 6
- first_gain: float32 [512], replicated, may hold values from 0.5 to 1.5
- second_gain: float32 [512], replicated, may hold values from 0.5 to 1.5
- query_weight: bfloat16 [512, 512], P(None, 'tensor'), may hold values from -0.25 to 0.25
- key_weight: bfloat16 [512, 512], P(None, 'tensor'), may hold values from -0.25 to 0.25
- value_weight: bfloat16 [512, 512], P(None, 'tensor'), may hold values from -0.25 to 0.25
- output_weight: bfloat16 [512, 512], P('tensor'), may hold values from -2 to 2
- router_weight: bfloat16 [512, 32], replicated, may hold values from -0.125 to 0.125
- expert_in: bfloat16 [32, 512, 2048], P('expert', None, 'tensor'), may hold values from -0.5 to 0.5
- expert_out: bfloat16 [32, 2048, 512], P('expert', 'tensor'), may hold values from -0.5 to 0.5
- cotangent: float32 [65536, 512], P(('expert', 'tensor')), may hold values from -6 to 6
- routes: int32 [65536, 4], P(('expert', 'tensor')), may hold values from 0 to 31, all different within a row
- priority: int32 [2048, 32], P(('expert', 'tensor')), may hold values from 0 to 31, each once within a row
- prefix_len: int32 [32], P('expert'), may hold values from 204 to 1024
Outputs:
- layer_output: bfloat16 [65536, 512], P(('expert', 'tensor'))
- tokens_grad: float32 [65536, 512], P(('expert', 'tensor'))
- first_gain_grad: float32 [512], replicated
- second_gain_grad: float32 [512], replicated
- query_grad: float32 [512, 512], P(None, 'tensor')
- key_grad: float32 [512, 512], P(None, 'tensor')
- value_grad: float32 [512, 512], P(None, 'tensor')
- output_grad: float32 [512, 512], P('tensor')
- router_grad: float32 [512, 32], replicated
- expert_in_grad: float32 [32, 512, 2048], P('expert', None, 'tensor')
- expert_out_grad: float32 [32, 2048, 512], P('expert', 'tensor')
Inputs may be any that keep to these rules, and one draw needn't show every extreme that they name: `routes`: each row names 4 different experts, and every expert is named by some row. `priority`: each row holds every number of 0 to 31 once.
All inputs are finite; a program needn't handle non-finite values.
Results may differ from a plain program's by a relative error of at most 0.028.
Values may be sent and summed in bfloat16 or wider, within the bound.
A program may use at most 128 MiB of HBM per device.

v0:
```python
import jax
import jax.numpy as jnp
from jax import lax
from jax.sharding import PartitionSpec as P

HEAD_DIM = 64
GROUP = 32
TOP = 4


EPS = 1e-05
NEG = -1e30


def norm_rows(values, gain_vec):
    center = values - jnp.mean(values, axis=-1, keepdims=True)
    spread = lax.rsqrt(jnp.mean(center * center, axis=-1, keepdims=True) + EPS)
    scaled = center * spread
    return (scaled, spread, scaled * gain_vec)


def norm_back(grad_in, scaled, spread, gain_vec):
    grad_scaled = grad_in * gain_vec
    centered = grad_scaled - jnp.mean(grad_scaled, axis=-1, keepdims=True)
    return spread * (centered - scaled * jnp.mean(grad_scaled * scaled, axis=-1, keepdims=True))


def block_scores(queries, key_rows, start_row, block_rows, prefix):
    query_blk = lax.dynamic_slice_in_dim(queries, start_row, block_rows, 0)
    scores = jnp.einsum(
        "qhd,khd->hqk", query_blk, key_rows, preferred_element_type=jnp.float32
    ) * HEAD_DIM ** (-0.5)
    row_ids = start_row + jnp.arange(block_rows, dtype=jnp.int32)
    col_ids = jnp.arange(key_rows.shape[0], dtype=jnp.int32)
    allowed = (col_ids[None, :] <= row_ids[:, None]) | (col_ids[None, :] < prefix)
    return (query_blk, jnp.where(allowed[None], scores, NEG))


def attend_forward(queries, key_rows, value_rows, prefix, block_rows):
    length = key_rows.shape[0]

    def one_block(start_row):
        query_blk, scores = block_scores(queries, key_rows, start_row, block_rows, prefix)
        row_peak = jnp.max(scores, axis=-1, keepdims=True)
        exp_scores = jnp.exp(scores - row_peak)
        exp_total = jnp.sum(exp_scores, axis=-1, keepdims=True)
        soft_rows = (exp_scores / exp_total).astype(jnp.bfloat16)
        context = jnp.einsum(
            "hqk,khd->qhd", soft_rows, value_rows, preferred_element_type=jnp.float32
        )
        return (context.astype(jnp.bfloat16), (row_peak + jnp.log(exp_total))[..., 0])

    starts = jnp.arange(length // block_rows, dtype=jnp.int32) * block_rows
    context, log_total = lax.map(one_block, starts)
    return (context.reshape(length, queries.shape[1] * queries.shape[2]), log_total)


def attend_backward(queries, key_rows, value_rows, grad_context, log_total, prefix, block_rows):
    length = key_rows.shape[0]
    score_scale = HEAD_DIM ** (-0.5)

    def one_block(carried, inputs):
        grad_keys, grad_values = carried
        start_row, block_log = inputs
        query_blk, scores = block_scores(queries, key_rows, start_row, block_rows, prefix)
        soft_rows = jnp.exp(scores - block_log[..., None])
        grad_blk = lax.dynamic_slice_in_dim(grad_context, start_row, block_rows, 0)
        grad_soft = jnp.einsum(
            "qhd,khd->hqk", grad_blk, value_rows, preferred_element_type=jnp.float32
        )
        inner_sum = jnp.sum(soft_rows * grad_soft, axis=-1, keepdims=True)
        grad_scores = (soft_rows * (grad_soft - inner_sum)).astype(jnp.bfloat16)
        grad_values = grad_values + jnp.einsum(
            "hqk,qhd->khd",
            soft_rows.astype(jnp.bfloat16),
            grad_blk,
            preferred_element_type=jnp.float32,
        )
        grad_keys = grad_keys + score_scale * jnp.einsum(
            "hqk,qhd->khd", grad_scores, query_blk, preferred_element_type=jnp.float32
        )
        grad_query = score_scale * jnp.einsum(
            "hqk,khd->qhd", grad_scores, key_rows, preferred_element_type=jnp.float32
        )
        return ((grad_keys, grad_values), grad_query)

    empty_rows = jnp.zeros(key_rows.shape, jnp.float32)
    starts = jnp.arange(length // block_rows, dtype=jnp.int32) * block_rows
    (grad_keys, grad_values), grad_query = lax.scan(
        one_block, (empty_rows, empty_rows), (starts, log_total)
    )
    return (
        grad_query.reshape(length, -1),
        grad_keys.reshape(length, -1),
        grad_values.reshape(length, -1),
    )


def to_homes(part_out, expert_size):
    local_experts, row_total, width = part_out.shape
    moved = part_out.reshape(local_experts, expert_size, -1, width).transpose(1, 0, 2, 3)
    return moved.reshape(expert_size * local_experts, -1, width)


def body(
    tokens,
    first_gain,
    second_gain,
    query_weight,
    key_weight,
    value_weight,
    output_weight,
    router_weight,
    expert_in,
    expert_out,
    cotangent,
    routes,
    priority,
    prefix_len,
):
    row_count, width = tokens.shape
    tensor_size = lax.axis_size("tensor")
    expert_size = lax.axis_size("expert")
    length = row_count * tensor_size
    block_rows = min(512, length)
    head_count = query_weight.shape[1] // HEAD_DIM
    experts = router_weight.shape[1]
    groups = row_count // GROUP
    capacity = (5 * GROUP * TOP + 4 * experts - 1) // (4 * experts)
    prefix = prefix_len[0]
    stream = tokens.astype(jnp.float32)
    scaled_one, spread_one, normed_one = norm_rows(stream, first_gain)
    sequence = lax.all_gather(normed_one.astype(jnp.bfloat16), "tensor", axis=0, tiled=True)
    queries = jnp.dot(sequence, query_weight, preferred_element_type=jnp.float32).astype(
        jnp.bfloat16
    )
    key_rows = jnp.dot(sequence, key_weight, preferred_element_type=jnp.float32).astype(
        jnp.bfloat16
    )
    value_rows = jnp.dot(sequence, value_weight, preferred_element_type=jnp.float32).astype(
        jnp.bfloat16
    )
    query_heads = queries.reshape(length, head_count, HEAD_DIM)
    key_heads = key_rows.reshape(length, head_count, HEAD_DIM)
    value_heads = value_rows.reshape(length, head_count, HEAD_DIM)
    context, log_total = attend_forward(query_heads, key_heads, value_heads, prefix, block_rows)
    attended = lax.psum_scatter(
        jnp.dot(context, output_weight, preferred_element_type=jnp.float32).astype(jnp.bfloat16),
        "tensor",
        scatter_dimension=0,
        tiled=True,
    ).astype(jnp.float32)
    residual = stream + attended
    scaled_two, spread_two, normed_two = norm_rows(residual, second_gain)
    mixer_in = normed_two.astype(jnp.bfloat16)
    logits = jnp.dot(mixer_in, router_weight, preferred_element_type=jnp.float32)
    member = jnp.sum(
        (routes[:, :, None] == jnp.arange(experts, dtype=jnp.int32)).astype(jnp.float32), axis=1
    )
    member = member.reshape(groups, GROUP, experts)
    earlier = (priority[:, :, None] < priority[:, None, :]).astype(jnp.float32)
    order_rank = jnp.einsum("gst,gse->gte", earlier, member)
    kept_pairs = member * (order_rank < capacity).astype(jnp.float32)
    exp_terms = kept_pairs * jnp.exp(logits.reshape(groups, GROUP, experts))
    exp_total = jnp.sum(exp_terms, axis=1, keepdims=True)
    kept_count = jnp.sum(kept_pairs, axis=1, keepdims=True)
    weights = exp_terms / jnp.where(kept_count > 0, exp_total, 1.0)
    weights_low = weights.astype(jnp.bfloat16)
    grouped = mixer_in.reshape(groups, GROUP, width)
    mixed_rows = jnp.einsum(
        "gte,gtd->egd", weights_low, grouped, preferred_element_type=jnp.float32
    ).astype(jnp.bfloat16)
    sequence_mix = lax.all_gather(mixed_rows, "tensor", axis=1, tiled=True)
    owner_rows = lax.all_to_all(sequence_mix, "expert", split_axis=0, concat_axis=1, tiled=True)
    hidden_pre = jnp.einsum(
        "erd,edf->erf", owner_rows, expert_in, preferred_element_type=jnp.float32
    )
    sigma_pre = jax.nn.sigmoid(hidden_pre)
    hidden = (hidden_pre * sigma_pre).astype(jnp.bfloat16)
    part_out = jnp.einsum("erf,efd->erd", hidden, expert_out, preferred_element_type=jnp.float32)
    arrived = lax.all_to_all(
        to_homes(part_out, expert_size).astype(jnp.bfloat16),
        "expert",
        split_axis=0,
        concat_axis=0,
        tiled=True,
    )
    summed = lax.psum_scatter(arrived, "tensor", scatter_dimension=1, tiled=True).astype(
        jnp.float32
    )
    returned = summed.astype(jnp.bfloat16)
    mixed_back = jnp.einsum(
        "gte,egd->gtd", weights_low, returned, preferred_element_type=jnp.float32
    ).reshape(row_count, width)
    layer_output = (residual + mixed_back).astype(jnp.bfloat16)
    grad_mix = cotangent.astype(jnp.bfloat16).reshape(groups, GROUP, width)
    grad_returned = jnp.einsum(
        "gte,gtd->egd", weights_low, grad_mix, preferred_element_type=jnp.float32
    ).astype(jnp.bfloat16)
    grad_weights = jnp.einsum(
        "gtd,egd->gte", grad_mix, returned, preferred_element_type=jnp.float32
    )
    sequence_grad = lax.all_gather(grad_returned, "tensor", axis=1, tiled=True)
    grad_owner = lax.all_to_all(sequence_grad, "expert", split_axis=0, concat_axis=1, tiled=True)
    grad_hidden = jnp.einsum(
        "erd,efd->erf", grad_owner, expert_out, preferred_element_type=jnp.float32
    )
    slope = sigma_pre * (1.0 + hidden_pre * (1.0 - sigma_pre))
    grad_pre = (grad_hidden * slope).astype(jnp.bfloat16)
    expert_out_grad = jnp.einsum(
        "erf,erd->efd", hidden, grad_owner, preferred_element_type=jnp.float32
    )
    expert_in_grad = jnp.einsum(
        "erd,erf->edf", owner_rows, grad_pre, preferred_element_type=jnp.float32
    )
    grad_part = jnp.einsum("erf,edf->erd", grad_pre, expert_in, preferred_element_type=jnp.float32)
    grad_arrived = lax.all_to_all(
        to_homes(grad_part, expert_size).astype(jnp.bfloat16),
        "expert",
        split_axis=0,
        concat_axis=0,
        tiled=True,
    )
    grad_summed = lax.psum_scatter(grad_arrived, "tensor", scatter_dimension=1, tiled=True).astype(
        jnp.float32
    )
    grad_mixed = grad_summed.astype(jnp.bfloat16)
    grad_grouped = jnp.einsum(
        "gte,egd->gtd", weights_low, grad_mixed, preferred_element_type=jnp.float32
    )
    grad_weights = grad_weights + jnp.einsum(
        "egd,gtd->gte", grad_mixed, grouped, preferred_element_type=jnp.float32
    )
    inner_sum = jnp.sum(weights * grad_weights, axis=1, keepdims=True)
    grad_logits = (
        (weights * (grad_weights - inner_sum)).reshape(row_count, experts).astype(jnp.bfloat16)
    )
    router_part = jnp.einsum("td,te->de", mixer_in, grad_logits, preferred_element_type=jnp.float32)
    grad_mixer = grad_grouped.reshape(row_count, width) + jnp.einsum(
        "te,de->td", grad_logits, router_weight, preferred_element_type=jnp.float32
    )
    second_part = jnp.sum(grad_mixer * scaled_two, axis=0)
    grad_residual = cotangent + norm_back(grad_mixer, scaled_two, spread_two, second_gain)
    grad_sequence = lax.all_gather(grad_residual.astype(jnp.bfloat16), "tensor", axis=0, tiled=True)
    output_part = jnp.einsum(
        "lc,ld->cd", context, grad_sequence, preferred_element_type=jnp.float32
    )
    grad_context = jnp.einsum(
        "ld,cd->lc", grad_sequence, output_weight, preferred_element_type=jnp.float32
    ).astype(jnp.bfloat16)
    grad_query, grad_keys, grad_values = attend_backward(
        query_heads,
        key_heads,
        value_heads,
        grad_context.reshape(length, head_count, HEAD_DIM),
        log_total,
        prefix,
        block_rows,
    )
    grad_query = grad_query.astype(jnp.bfloat16)
    grad_keys = grad_keys.astype(jnp.bfloat16)
    grad_values = grad_values.astype(jnp.bfloat16)
    query_part = jnp.einsum("ld,lc->dc", sequence, grad_query, preferred_element_type=jnp.float32)
    key_part = jnp.einsum("ld,lc->dc", sequence, grad_keys, preferred_element_type=jnp.float32)
    value_part = jnp.einsum("ld,lc->dc", sequence, grad_values, preferred_element_type=jnp.float32)
    total_grad = jnp.einsum(
        "lc,dc->ld", grad_query, query_weight, preferred_element_type=jnp.float32
    )
    total_grad = total_grad + jnp.einsum(
        "lc,dc->ld", grad_keys, key_weight, preferred_element_type=jnp.float32
    )
    grad_normed = lax.psum_scatter(
        (
            total_grad
            + jnp.einsum("lc,dc->ld", grad_values, value_weight, preferred_element_type=jnp.float32)
        ).astype(jnp.bfloat16),
        "tensor",
        scatter_dimension=0,
        tiled=True,
    ).astype(jnp.float32)
    first_part = jnp.sum(grad_normed * scaled_one, axis=0)
    tokens_grad = grad_residual + norm_back(grad_normed, scaled_one, spread_one, first_gain)
    query_grad, key_grad, value_grad, output_grad = (
        lax.psum(query_part.astype(jnp.bfloat16), "expert").astype(jnp.float32),
        lax.psum(key_part.astype(jnp.bfloat16), "expert").astype(jnp.float32),
        lax.psum(value_part.astype(jnp.bfloat16), "expert").astype(jnp.float32),
        lax.psum(output_part.astype(jnp.bfloat16), "expert").astype(jnp.float32),
    )
    first_gain_grad, second_gain_grad, router_grad = lax.psum(
        (first_part, second_part, router_part), ("expert", "tensor")
    )
    return (
        layer_output,
        tokens_grad,
        first_gain_grad,
        second_gain_grad,
        query_grad,
        key_grad,
        value_grad,
        output_grad,
        router_grad,
        expert_in_grad,
        expert_out_grad,
    )


def solution(mesh):
    in_specs = (
        P(("expert", "tensor"), None),
        P(),
        P(),
        P(None, "tensor"),
        P(None, "tensor"),
        P(None, "tensor"),
        P("tensor", None),
        P(),
        P("expert", None, "tensor"),
        P("expert", "tensor", None),
        P(("expert", "tensor"), None),
        P(("expert", "tensor"), None),
        P(("expert", "tensor"), None),
        P("expert"),
    )
    out_specs = (
        P(("expert", "tensor"), None),
        P(("expert", "tensor"), None),
        P(),
        P(),
        P(None, "tensor"),
        P(None, "tensor"),
        P(None, "tensor"),
        P("tensor", None),
        P(),
        P("expert", None, "tensor"),
        P("expert", "tensor", None),
    )
    return jax.shard_map(body, mesh=mesh, in_specs=in_specs, out_specs=out_specs, check_vma=False)
```

profile of v0, /device:TPU:1, one launch (start us, length us, event | category | flops | bytes accessed | tf_op | source)
XLA Modules:
  0.0 777.5 jit_solution(236218361544068434)
XLA Ops:
  12.6 33.8 %all-gather.5.cloned.1.call-done = bf16[2048,512]{1,0:T(8,128)(2,1)} async-done(((bf16[512,512]{1,0:T(8,128)(2,1)}), bf16[2048,512]{1,0:T(8,128)(2,1)}) %all-gather.5.cloned.1.call-update) | async-done | bytes 2097168 | tf_op jit(solution)/shard_map/all_gather | solution.py:133
  46.4 2.6 convolution_convert_fusion.2
  49.0 2.4 convolution_convert_fusion.3
  53.1 56.4 %while.27 = (s32[]{:T(128)}, bf16[4,512,2,64]{1,3,2,0:T(8,128)(2,1)S(1)}, f32[4,2,512]{2,1,0:T(2,128)}, s32[4]{0:T(128)}, s32[]{:T(128)}, /*index=5*/bf16[2048,2...) while((s32[]{:T(128)}, ...), condition=%wide.region_5.6_spmd, body=%wide.region_2.5_spmd.sunk | while | flops 564200960 | bytes 30711992 | solution.py:54
  58.4 3.1 fusion.162
  61.4 2.5 fusion.163
  63.9 2.7 fusion.164
  72.5 3.1 fusion.162
  75.5 2.5 fusion.163
  78.0 2.7 fusion.164
  86.6 3.0 fusion.162
  89.6 2.5 fusion.163
  92.1 2.7 fusion.164
  100.7 3.0 fusion.162
  103.7 2.5 fusion.163
  106.2 2.7 fusion.164
  113.2 29.8 %reduce-scatter.5.cloned.1.call-done = bf16[512,512]{1,0:T(8,128)(2,1)} async-done(((bf16[2048,512]{1,0:T(8,128)(2,1)}), bf16[512,512]{1,0:T(8,128)(2,1)}) %reduce-scatter.5.cloned.1.call-update) | async-done | bytes 524304 | tf_op jit(solution)/shard_map/reduce_scatter | solution.py:147
  151.3 28.2 %all-gather.7.cloned.1.call-done = bf16[32,64,512]{2,0,1:T(8,128)(2,1)} async-done(((bf16[32,16,512]{2,0,1:T(8,128)(2,1)}), bf16[32,64,512]{2,0,1:T(8,128)(2,1)}) %all-gather.7.cloned.1.call-update) | async-done | bytes 2097168 | tf_op jit(solution)/shard_map/all_gather | solution.py:173
  179.5 4.1 copy.64
  183.6 7.8 all-to-all-start
  191.4 21.3 %all-gather.9.cloned.1.call-done = bf16[32,64,512]{2,0,1:T(8,128)(2,1)} async-done(((bf16[32,16,512]{2,0,1:T(8,128)(2,1)}), bf16[32,64,512]{2,0,1:T(8,128)(2,1)}) %all-gather.9.cloned.1.call-update) | async-done | bytes 2097168 | tf_op jit(solution)/shard_map/all_gather | solution.py:203
  212.7 4.1 copy.67
  216.8 2.9 all-to-all-done
  219.7 5.2 all-to-all-start.2
  225.0 6.0 multiply_convert_fusion.2
  230.9 22.4 %all-to-all-done.2 = bf16[32,64,512]{2,1,0:T(8,128)(2,1)} async-done(((bf16[32,64,512]{2,1,0:T(8,128)(2,1)}), bf16[32,64,512]{2,1,0:T(8,128)(2,1)}, u32[]{:S(2)}, u32[]{:S(2)}) %all-to-all-start.2) | async-done | bytes 2097184 | tf_op jit(solution)/shard_map/all_to_all | solution.py:204
  253.4 5.2 multiply_convert_fusion.1
  261.3 32.6 %all_to_all.28 = bf16[32,64,512]{2,1,0:T(8,128)(2,1)} all-to-all(bf16[32,64,512]{2,1,0:T(8,128)(2,1)S(1)} %convolution_convert_fusion.5), channel_id=1, replica_groups=mesh['expert'=32,'tensor'=4] {'expert'}, dimensions={0} | all-to-all | bytes 4194304 | tf_op jit(solution)/shard_map/all_to_all | solution.py:217
  294.0 2.8 convolution_convert_fusion.6
  296.8 32.0 %all_to_all.29 = bf16[32,64,512]{2,1,0:T(8,128)(2,1)} all-to-all(bf16[32,64,512]{2,1,0:T(8,128)(2,1)S(1)} %convolution_convert_fusion.6), channel_id=1, replica_groups=mesh['expert'=32,'tensor'=4] {'expert'}, dimensions={0} | all-to-all | bytes 4194304 | tf_op jit(solution)/shard_map/all_to_all | solution.py:181
  328.9 2.2 fusion.68
  331.2 24.1 %reduce-scatter.7.cloned.1.call-done = bf16[32,16,512]{2,1,0:T(8,128)(2,1)} async-done(((bf16[32,64,512]{2,1,0:T(8,128)(2,1)}), bf16[32,16,512]{2,1,0:T(8,128)(2,1)}) %reduce-scatter.7.cloned.1.call-update) | async-done | bytes 524304 | tf_op jit(solution)/shard_map/reduce_scatter | solution.py:188
  362.7 30.5 %all-gather.11.cloned.1.call-done = bf16[2048,512]{1,0:T(8,128)(2,1)} async-done(((bf16[512,512]{1,0:T(8,128)(2,1)}), bf16[2048,512]{1,0:T(8,128)(2,1)}) %all-gather.11.cloned.1.call-update) | async-done | bytes 2097168 | tf_op jit(solution)/shard_map/all_gather | solution.py:244
  393.1 2.4 convolution_convert_fusion.1
  395.5 81.8 %while.28 = (s32[]{:T(128)}, f32[2048,2,64]{0,2,1:T(8,128)S(1)}, f32[2048,2,64]{0,2,1:T(8,128)}, bf16[4,512,2,64]{1,3,2,0:T(8,128)(2,1)}, s32[4]{0:T(128)}, /*in...) while((s32[]{:T(128)}, f32[2048,2,64]{0,2,1:T(8,128)S(1)}, ...), condition=%wide.region_19.20_spmd.clone, body=%wide.region_17.19_spmd.clone.sunk | while | flops 1377109504 | bytes 86282592 | solution.py:89
  401.5 2.4 fusion.174
  403.9 2.6 fusion.177
  406.5 3.2 multiply_reduce_fusion.7
  409.8 2.6 multiply_convert_fusion.5
  413.8 2.1 fusion.176
  421.9 2.4 fusion.174
  424.3 2.6 fusion.177
  426.9 3.2 multiply_reduce_fusion.7
  430.2 2.6 multiply_convert_fusion.5
  434.2 2.1 fusion.176
  442.3 2.4 fusion.174
  444.7 2.6 fusion.177
  447.3 3.2 multiply_reduce_fusion.7
  450.6 2.6 multiply_convert_fusion.5
  454.6 2.1 fusion.176
  462.7 2.4 fusion.174
  465.1 2.6 fusion.177
  467.7 3.2 multiply_reduce_fusion.7
  471.0 2.6 multiply_convert_fusion.5
  479.2 2.7 fusion.83
  481.9 2.7 fusion.82
  490.0 5.5 add_convert_fusion
  495.6 4.6 convolution_bitcast_fusion
  500.3 4.0 convolution_bitcast_fusion.1
  505.2 88.3 %all-reduce.7.cloned.1.call-done = (bf16[512,128]{1,0:T(8,128)(2,1)}, bf16[512,128]{1,0:T(8,128)(2,1)}, bf16[512,128]{1,0:T(8,128)(2,1)}, bf16[128,512]{1,0:T(8,128)(2,1)}) async-done(((bf16[512,128]{1,0:T(8,128)(2,1)}, bf16[512,128]{1,0:T(8,128)(2,1)}, bf16[512,128]{1,0:T(8,128)(2,1)}, bf16[128,512]{1,0:T(8,128)(2,1)}), (bf16[512,128]{1,0:T(8,128)(2,1)}, bf16[512,128]{1,0:T(8,128)(2,1)}, ...) | async-done | bytes 524304 | tf_op jit(solution)/shard_map/psum | solution.py:284
  600.0 25.5 %reduce-scatter.11.cloned.1.call-done = bf16[512,512]{1,0:T(8,128)(2,1)} async-done(((bf16[2048,512]{1,0:T(8,128)(2,1)}), bf16[512,512]{1,0:T(8,128)(2,1)}) %reduce-scatter.11.cloned.1.call-update) | async-done | bytes 524304 | tf_op jit(solution)/shard_map/reduce_scatter | solution.py:272
  627.2 2.4 fusion.57
  629.6 64.7 %all-reduce = (f32[512]{0:T(512)}, f32[512]{0:T(512)}) all-reduce(f32[512]{0:T(512)S(1)} %get-tuple-element.156, f32[512]{0:T(512)S(1)} %get-tuple-element.154), channel_id=1, replica_groups=mesh['expert'=32,'tensor'=4] {'expert','tensor'}, use_global_device_ids=true, to_apply=%region_24.25 | all-reduce | flops 1024 | bytes 8192 | tf_op jit(solution)/shard_map/psum | solution.py:289
  694.3 74.4 %all-reduce.5.cloned.1.call-done = f32[512,32]{0,1:T(8,128)} async-done(((f32[512,32]{0,1:T(8,128)}), f32[512,32]{0,1:T(8,128)}) %all-reduce.5.cloned.1.call-update) | async-done | bytes 65552 | tf_op jit(solution)/shard_map/psum | solution.py:289
  (229 shorter events, 86.0 us)
Async XLA Ops:
  7.2 217.8 %copy-start = (bf16[1,512,512]{2,1,0:T(8,128)(2,1)S(1)}, bf16[1,512,512]{2,1,0:T(8,128)(2,1)}, u32[]{:S(2)}) copy-start(bf16[1,512,512]{2,1,0:T(8,128)(2,1)} %param.26) | copy-start | bytes 1572868
  7.2 41.8 %copy-start.22 = (bf16[512,128]{1,0:T(8,128)(2,1)S(1)}, bf16[512,128]{1,0:T(8,128)(2,1)}, u32[]{:S(2)}) copy-start(bf16[512,128]{1,0:T(8,128)(2,1)} %param.22) | copy-start | bytes 393220
  7.2 44.2 %copy-start.24 = (bf16[512,128]{1,0:T(8,128)(2,1)S(1)}, bf16[512,128]{1,0:T(8,128)(2,1)}, u32[]{:S(2)}) copy-start(bf16[512,128]{1,0:T(8,128)(2,1)} %param.21) | copy-start | bytes 393220
  7.2 39.2 %all-gather.5.cloned.1.call-start = ((), (), s32[]{:S(2)}) async-start(), calls=%async_computation.8 | async-start | bytes 2621440 | tf_op jit(solution)/shard_map/all_gather | solution.py:133
  8.5 44.5 %copy-start.30 = (f32[512]{0:T(512)}, f32[512]{0:T(512)S(1)}, u32[]{:S(2)}) copy-start(f32[512]{0:T(512)S(1)} %broadcast_multiply_fusion.5) | copy-start | bytes 6148
  9.9 43.2 %copy-start.33 = (f32[512]{0:T(512)}, f32[512]{0:T(512)S(1)}, u32[]{:S(2)}) copy-start(f32[512]{0:T(512)S(1)} %add_rsqrt_fusion.1) | copy-start | bytes 6148
  12.0 130.9 %reduce-scatter.5.cloned.1.call-start = ((), (), s32[]{:S(2)}) async-start(), calls=%async_computation.9 | async-start | bytes 2621440 | tf_op jit(solution)/shard_map/reduce_scatter | solution.py:147
  46.4 5.0 copy-start.2
  53.1 57.8 %copy-start.26 = (bf16[128,512]{1,0:T(8,128)(2,1)S(1)}, bf16[128,512]{1,0:T(8,128)(2,1)}, u32[]{:S(2)}) copy-start(bf16[128,512]{1,0:T(8,128)(2,1)} %param.24) | copy-start | bytes 393220
  109.5 3.5 copy-start.38
  109.5 33.4 %copy-start.4 = (bf16[512,512]{1,0:T(8,128)(2,1)S(1)}, bf16[512,512]{1,0:T(8,128)(2,1)}, u32[]{:S(2)}) copy-start(bf16[512,512]{1,0:T(8,128)(2,1)} %param.18) | copy-start | bytes 1572868
  109.9 35.6 %copy-start.35 = (f32[512]{0:T(512)S(1)}, f32[512]{0:T(512)}, u32[]{:S(2)}) copy-start(f32[512]{0:T(512)} %param.20) | copy-start | bytes 6148
  110.9 36.0 %copy-start.28 = (bf16[512,32]{0,1:T(8,128)(2,1)S(1)}, bf16[512,32]{0,1:T(8,128)(2,1)}, u32[]{:S(2)}) copy-start(bf16[512,32]{0,1:T(8,128)(2,1)} %param.25) | copy-start | bytes 98308
  112.9 34.3 %copy-start.32 = (s32[16,32]{1,0:T(8,128)S(1)}, s32[16,32]{1,0:T(8,128)}, u32[]{:S(2)}) copy-start(s32[16,32]{1,0:T(8,128)} %param.30) | copy-start | bytes 6148
  113.0 66.5 %all-gather.7.cloned.1.call-start = ((), (), s32[]{:S(2)}) async-start(), calls=%async_computation.10 | async-start | bytes 2621440 | tf_op jit(solution)/shard_map/all_gather | solution.py:173
  146.9 182.1 %copy-start.5 = (bf16[512,512]{1,0:T(8,128)(2,1)}, bf16[512,512]{1,0:T(8,128)(2,1)S(1)}, u32[]{:S(2)}) copy-start(bf16[512,512]{1,0:T(8,128)(2,1)S(1)} %multiply_convert_fusion.3) | copy-start | bytes 1572868
  148.8 63.9 %all-gather.9.cloned.1.call-start = ((), (), s32[]{:S(2)}) async-start(), calls=%async_computation.12 | async-start | bytes 2621440 | tf_op jit(solution)/shard_map/all_gather | solution.py:203
  183.6 36.1 %all-to-all-start = ((bf16[32,64,512]{2,1,0:T(8,128)(2,1)}), bf16[32,64,512]{2,1,0:T(8,128)(2,1)}, u32[]{:S(2)}, u32[]{:S(2)}) async-start(bf16[32,64,512]{2,1,0:T(8,128)(2,1)} %copy.64), calls=%async_computation.1 | async-start | bytes 4194304 | tf_op jit(solution)/shard_map/all_to_all | solution.py:174
  219.7 33.7 %all-to-all-start.2 = ((bf16[32,64,512]{2,1,0:T(8,128)(2,1)}), bf16[32,64,512]{2,1,0:T(8,128)(2,1)}, u32[]{:S(2)}, u32[]{:S(2)}) async-start(bf16[32,64,512]{2,1,0:T(8,128)(2,1)} %copy.67), calls=%async_computation.4 | async-start | bytes 4194304 | tf_op jit(solution)/shard_map/all_to_all | solution.py:204
  224.9 104.0 %reduce-scatter.9.cloned.1.call-start = ((), (), s32[]{:S(2)}) async-start(), calls=%async_computation.13 | async-start | bytes 2621440 | tf_op jit(solution)/shard_map/reduce_scatter | solution.py:224
  261.3 32.7 %copy-start.39 = (bf16[1,512,512]{2,1,0:T(8,128)(2,1)S(1)}, bf16[1,512,512]{2,1,0:T(8,128)(2,1)}, u32[]{:S(2)}) copy-start(bf16[1,512,512]{2,1,0:T(8,128)(2,1)} %param.27) | copy-start | bytes 1572868
  293.9 61.3 %reduce-scatter.7.cloned.1.call-start = ((), (), s32[]{:S(2)}) async-start(), calls=%async_computation.11 | async-start | bytes 2621440 | tf_op jit(solution)/shard_map/reduce_scatter | solution.py:188
  328.8 29.8 %copy-start.7 = (bf16[512,512]{1,0:T(8,128)(2,1)S(1)}, bf16[512,512]{1,0:T(8,128)(2,1)}, u32[]{:S(2)}) copy-start(bf16[512,512]{1,0:T(8,128)(2,1)} %reduce-scatter.5.cloned.1.call-done) | copy-start | bytes 1572868
  328.8 64.3 %all-gather.11.cloned.1.call-start = ((), (), s32[]{:S(2)}) async-start(), calls=%async_computation.14 | async-start | bytes 2621440 | tf_op jit(solution)/shard_map/all_gather | solution.py:244
  331.2 27.5 %copy-start.29 = (bf16[512,32]{0,1:T(8,128)(2,1)S(1)}, bf16[512,32]{0,1:T(8,128)(2,1)}, u32[]{:S(2)}) copy-start(bf16[512,32]{0,1:T(8,128)(2,1)} %param.25) | copy-start | bytes 98308
  355.2 4.7 copy-start.13
  356.9 3.6 copy-start.11
  356.9 3.6 copy-start.36
  357.0 3.5 copy-start.20
  360.0 33.1 %copy-start.27 = (bf16[128,512]{1,0:T(8,128)(2,1)S(1)}, bf16[128,512]{1,0:T(8,128)(2,1)}, u32[]{:S(2)}) copy-start(bf16[128,512]{1,0:T(8,128)(2,1)} %param.24) | copy-start | bytes 393220
  362.4 231.1 %all-reduce.7.cloned.1.call-start = ((), (), s32[]{:S(2)}) async-start(), calls=%async_computation.17 | async-start | bytes 1048576 | tf_op jit(solution)/shard_map/psum | solution.py:284
  401.5 2.4 copy-start.14
  406.5 3.3 copy-start.15
  409.8 2.6 copy-start.18
  413.8 2.1 copy-start.19
  421.9 2.4 copy-start.14
  426.9 3.3 copy-start.15
  430.2 2.6 copy-start.18
  434.2 2.1 copy-start.19
  442.3 2.4 copy-start.14
  447.3 3.3 copy-start.15
  450.6 2.6 copy-start.18
  454.6 2.1 copy-start.19
  462.7 2.4 copy-start.14
  467.7 3.3 copy-start.15
  471.0 2.6 copy-start.18
  474.9 2.1 copy-start.19
  477.3 1.8 copy-start.16
  477.3 1.8 copy-start.23
  479.0 2.9 copy-start.25
  479.1 5.4 copy-start.8
  479.2 5.4 copy-start.10
  481.9 3.8 copy-start.3
  485.7 4.3 copy-start.17
  490.0 135.5 %reduce-scatter.11.cloned.1.call-start = ((), (), s32[]{:S(2)}) async-start(), calls=%async_computation.15 | async-start | bytes 2621440 | tf_op jit(solution)/shard_map/reduce_scatter | solution.py:272
  495.6 273.1 %all-reduce.5.cloned.1.call-start = ((), (), s32[]{:S(2)}) async-start(), calls=%async_computation.16 | async-start | bytes 131072 | tf_op jit(solution)/shard_map/psum | solution.py:289
  495.6 4.6 copy-start.41
  500.3 4.1 copy-start.6
  500.3 4.1 copy-start.21
  500.3 125.2 %copy-start.31 = (f32[512]{0:T(512)S(1)}, f32[512]{0:T(512)}, u32[]{:S(2)}) copy-start(f32[512]{0:T(512)} %copy-done.30) | copy-start | bytes 6148
  500.3 125.2 %copy-start.34 = (f32[512]{0:T(512)S(1)}, f32[512]{0:T(512)}, u32[]{:S(2)}) copy-start(f32[512]{0:T(512)} %copy-done.33) | copy-start | bytes 6148
  500.3 125.2 %copy-start.37 = (f32[512]{0:T(512)S(1)}, f32[512]{0:T(512)}, u32[]{:S(2)}) copy-start(f32[512]{0:T(512)} %param.19) | copy-start | bytes 6148
  500.3 126.9 %copy-start.12 = (f32[512,512]{1,0:T(8,128)S(1)}, f32[512,512]{1,0:T(8,128)}, u32[]{:S(2)}) copy-start(f32[512,512]{1,0:T(8,128)} %get-tuple-element.205) | copy-start | bytes 3145732
  500.3 269.9 %copy-start.1 = (bf16[1,512,512]{2,1,0:T(8,128)(2,1)S(1)}, bf16[1,512,512]{2,1,0:T(8,128)(2,1)}, u32[]{:S(2)}) copy-start(bf16[1,512,512]{2,1,0:T(8,128)(2,1)} %param.26) | copy-start | bytes 1572868
  (2 other events, 2.2 us)
Sparse Core Ops, SparseCore 0:
  12.1 34.2 all-gather.4
  113.1 29.8 reduce-scatter.4
  148.9 30.5 all-gather.6
  181.7 30.9 all-gather.8
  294.0 26.2 reduce-scatter.8
  329.0 26.2 reduce-scatter.6
  362.5 30.5 all-gather.10
  490.1 103.3 all-reduce.6
  595.9 29.5 reduce-scatter.10
  631.4 137.2 all-reduce.4
where the time goes:
time: 788 us; the launch traced here: 777 us
  waiting for transfers between devices  381 us (48%)
  matrix products  132 us (17%)
  blocking collectives  129 us (16%)
  other arithmetic  62.2 us (8%)
  local copies, waits for them, and re-layouts  27.2 us (3%)
  loops' own time  16.4 us (2%)
  between operations  15.3 us (2%)
  starting transfers between devices  13.6 us (2%)
    psum x1, waiting for transfers between devices, body(): lax.psum(query_part.astype(jnp.bfloat16), 'expert').astype(jnp.float32)  88.3 us
    psum x1, waiting for transfers between devices, body(): lax.psum((first_part, second_part, router_part), ('expert', 'tensor'))  74.4 us
    psum x1, blocking collectives, body(): lax.psum((first_part, second_part, router_part), ('expert', 'tensor'))  64.7 us
    all_gather x1, waiting for transfers between devices, body(): lax.all_gather(normed_one.astype(jnp.bfloat16), 'tensor', axis=0, tiled=T...  33.8 us
    all_to_all x1, blocking collectives, body(): lax.all_to_all(to_homes(grad_part, expert_size).astype(jnp.bfloat16), 'ex...  32.6 us
    all_to_all x1, blocking collectives, body(): lax.all_to_all(to_homes(part_out, expert_size).astype(jnp.bfloat16), 'exp...  32 us
    all_gather x1, waiting for transfers between devices, body(): lax.all_gather(grad_residual.astype(jnp.bfloat16), 'tensor', axis=0, tile...  30.5 us
    reduce_scatter x1, waiting for transfers between devices, body(): lax.psum_scatter(jnp.dot(context, output_weight, preferred_element_type=j...  29.8 us
  transfers between devices with their start and end apart: 12, of which 11 were waited for; matrix products, arithmetic and copies ran while one was open for 6% of the time, Pallas kernels for 0%

commit v1 on v0

v1 whole, which is shorter than its diff:
```python
import functools
import math

import jax
import jax.numpy as jnp
from jax import lax
from jax.experimental import pallas as pl
from jax.experimental.pallas import tpu as pltpu
from jax.sharding import PartitionSpec as P

HEAD_DIM = 64
GROUP = 32
TOP = 4
EPS = 1e-05
NEG = -1e30
SCORE_SCALE = HEAD_DIM**-0.5
SCORE_LOG2 = SCORE_SCALE * math.log2(math.e)
MESH = pl.DeviceIdType.MESH
VM = pl.BlockSpec(memory_space=pltpu.VMEM)
SM = pl.BlockSpec(memory_space=pltpu.SMEM)
TENSOR = 4
VMEM_BYTES = 48 << 20
BF16 = jnp.bfloat16
F32 = jnp.float32


def dotf(left, right, dims=((1,), (0,)), precision=None):
    return lax.dot_general(
        left, right, (dims, ((), ())), preferred_element_type=F32, precision=precision
    )


def iota(shape, axis):
    return lax.broadcasted_iota(jnp.int32, shape, axis)


def norm_parts(values):
    center = values - jnp.mean(values, axis=1, keepdims=True)
    spread = lax.rsqrt(jnp.mean(center * center, axis=1, keepdims=True) + EPS)
    return center * spread, spread


def remote(src, dst, send_sem, recv_sem, axis, to):
    return pltpu.make_async_remote_copy(
        src_ref=src,
        dst_ref=dst,
        send_sem=send_sem,
        recv_sem=recv_sem,
        device_id={axis: to},
        device_id_type=MESH,
    )


def greet(axis, size):
    barrier = pltpu.get_barrier_semaphore()
    me = lax.axis_index(axis)

    def one(off, _):
        pl.semaphore_signal(
            barrier, inc=1, device_id={axis: lax.rem(me + off, size)}, device_id_type=MESH
        )
        return 0

    lax.fori_loop(1, size, one, 0)


def project_kernel(
    tok_ref,
    gain_ref,
    wq_ref,
    wk_ref,
    wv_ref,
    routes_ref,
    prio_ref,
    seq_ref,
    q_ref,
    k_ref,
    v_ref,
    kept_ref,
    w_s,
    send_sem,
    recv_sem,
    *,
    experts,
    capacity,
):
    place = lax.axis_index("tensor")
    right, left = lax.rem(place + 1, TENSOR), lax.rem(place + TENSOR - 1, TENSOR)
    far = lax.rem(place + 2, TENSOR)
    barrier = pltpu.get_barrier_semaphore()
    for neighbour in (right, left):
        pl.semaphore_signal(
            barrier, inc=1, device_id={"tensor": neighbour}, device_id_type=MESH
        )
    rows, width = tok_ref.shape
    half = rows // 2

    def start_of(owner, part):
        return pl.multiple_of(owner * rows + part * half, half)

    def send(slot, owner, part, to):
        block = seq_ref.at[pl.ds(start_of(owner, part), half), :]
        return remote(block, block, send_sem.at[slot], recv_sem.at[slot], "tensor", to)

    for part in range(2):
        scaled, _ = norm_parts(tok_ref[part * half : (part + 1) * half, :].astype(F32))
        seq_ref[pl.ds(start_of(place, part), half), :] = (scaled * gain_ref[...]).astype(BF16)
    pl.semaphore_wait(barrier, 2)
    right_low, left_high = send(0, place, 0, right), send(1, place, 1, left)
    right_high, left_low = send(2, place, 1, right), send(3, place, 0, left)
    for copy in (right_low, left_high, right_high, left_low):
        copy.start()
    head_cols = wq_ref.shape[1]
    w_s[:, 0:head_cols] = wq_ref[...]
    w_s[:, head_cols : 2 * head_cols] = wk_ref[...]
    w_s[:, 2 * head_cols : 3 * head_cols] = wv_ref[...]

    def project(owner, part):
        start = start_of(owner, part)
        out = dotf(seq_ref[pl.ds(start, half), :], w_s[...]).astype(BF16)
        q_ref[pl.ds(start, half), :] = out[:, 0:head_cols]
        k_ref[pl.ds(start, half), :] = out[:, head_cols : 2 * head_cols]
        v_ref[pl.ds(start, half), :] = out[:, 2 * head_cols : 3 * head_cols]

    project(place, 0)
    project(place, 1)
    right_low.wait_recv()
    right_on = send(4, left, 0, right)
    right_on.start()
    left_high.wait_recv()
    left_on = send(5, right, 1, left)
    left_on.start()

    groups, size = prio_ref.shape
    wide = experts * groups
    prio = prio_ref[...].astype(F32).astype(BF16)
    tok_group = (iota((rows, groups), 0) // size) == iota((rows, groups), 1)
    spread_rows = dotf(jnp.where(tok_group, 1.0, 0.0).astype(BF16), prio)
    at_col = (iota((rows, size), 0) % size) == iota((rows, size), 1)
    prio_col = jnp.sum(jnp.where(at_col, spread_rows, 0.0), axis=1, keepdims=True)
    group_tok = (iota((groups, rows), 1) // size) == iota((groups, rows), 0)
    spread_cols = dotf(prio, jnp.where(group_tok, 1.0, 0.0).astype(BF16), ((0,), (0,)))
    at_row = (iota((size, rows), 1) % size) == iota((size, rows), 0)
    prio_row = jnp.sum(jnp.where(at_row, spread_cols, 0.0), axis=0, keepdims=True)
    col = iota((rows, wide), 1)
    own_group = (iota((rows, wide), 0) // size) == (col % groups)
    col_expert = col // groups
    named = routes_ref[:, 0:1] == col_expert
    for pick in range(1, TOP):
        named = named | (routes_ref[:, pick : pick + 1] == col_expert)
    member = jnp.where(named & own_group, 1.0, 0.0)
    earlier = jnp.where(prio_row < prio_col, 1.0, 0.0).astype(BF16)
    rank = dotf(earlier, member.astype(BF16))
    kept_ref[...] = jnp.where(rank < capacity, member, 0.0).astype(BF16)

    right_high.wait_recv()
    project(left, 0)
    project(left, 1)
    left_low.wait_recv()
    project(right, 0)
    project(right, 1)
    right_on.wait_recv()
    project(far, 0)
    left_on.wait_recv()
    project(far, 1)
    for copy in (right_low, left_high, right_high, left_low, right_on, left_on):
        copy.wait_send()


def project_rows(tokens, gain, wq, wk, wv, routes, priority, experts, capacity):
    rows, width = tokens.shape
    head_cols = wq.shape[1]
    heads = jax.ShapeDtypeStruct((TENSOR * rows, head_cols), BF16)
    return pl.pallas_call(
        functools.partial(project_kernel, experts=experts, capacity=float(capacity)),
        out_shape=(
            jax.ShapeDtypeStruct((TENSOR * rows, width), BF16),
            heads,
            heads,
            heads,
            jax.ShapeDtypeStruct((rows, experts * priority.shape[0]), BF16),
        ),
        in_specs=[VM] * 7,
        out_specs=(VM,) * 5,
        scratch_shapes=[
            pltpu.VMEM((width, 3 * head_cols), BF16),
            pltpu.SemaphoreType.DMA((6,)),
            pltpu.SemaphoreType.DMA((6,)),
        ],
        compiler_params=pltpu.CompilerParams(
            collective_id=0, has_side_effects=True, vmem_limit_bytes=VMEM_BYTES
        ),
        name="project",
    )(tokens, gain, wq, wk, wv, routes, priority)


def pick_head(values, head):
    lane = iota(values.shape, 1)
    inside = (lane >= head * HEAD_DIM) & (lane < (head + 1) * HEAD_DIM)
    return jnp.where(inside, values, jnp.zeros_like(values))


def attend_kernel(bq, bk, prefix_ref, q_ref, k_ref, v_ref, ctx_ref, lse_ref):
    length, cols = q_ref.shape
    heads = cols // HEAD_DIM
    prefix = prefix_ref[0]

    @pl.loop(0, length // bq)
    def _(blk):
        row0 = pl.multiple_of(blk * bq, bq)
        q = q_ref[pl.ds(row0, bq), :]
        q_heads = [pick_head(q, head) for head in range(heads)]
        n_full = jnp.maximum(prefix // bk, (row0 + 1) // bk)
        n_seen = jnp.maximum((prefix + bk - 1) // bk, (row0 + bq + bk - 1) // bk)

        def step(kb, carry, masked):
            col0 = pl.multiple_of(kb * bk, bk)
            keys = k_ref[pl.ds(col0, bk), :]
            vals = v_ref[pl.ds(col0, bk), :]
            out = []
            if masked:
                row_ids = iota((bq, bk), 0) + row0
                col_ids = iota((bq, bk), 1) + col0
                seen = (col_ids <= row_ids) | (col_ids < prefix)
            for head in range(heads):
                peak, total, acc = carry[3 * head : 3 * head + 3]
                scores = dotf(q_heads[head], keys, ((1,), (1,)))
                if masked:
                    scores = jnp.where(seen, scores, NEG)
                new_peak = jnp.maximum(peak, jnp.max(scores, axis=1, keepdims=True))
                soft = jnp.exp2((scores - new_peak) * SCORE_LOG2)
                shrink = jnp.exp2((peak - new_peak) * SCORE_LOG2)
                total = shrink * total + jnp.sum(soft, axis=1, keepdims=True)
                acc = shrink * acc + dotf(soft.astype(BF16), vals)
                out += [new_peak, total, acc]
            return tuple(out)

        init = (
            jnp.full((bq, 1), NEG, F32),
            jnp.zeros((bq, 1), F32),
            jnp.zeros((bq, cols), F32),
        ) * heads
        carry = lax.fori_loop(0, n_full, functools.partial(step, masked=False), init)
        carry = lax.fori_loop(n_full, n_seen, functools.partial(step, masked=True), carry)
        merged = jnp.zeros((bq, cols), F32)
        for head in range(heads):
            peak, total, acc = carry[3 * head : 3 * head + 3]
            merged = merged + pick_head(acc * (1.0 / total), head)
            lse = peak * SCORE_LOG2 + jnp.log2(total)
            lse_ref[pl.ds(8 * head, 8), pl.ds(row0, bq)] = jnp.transpose(
                jnp.broadcast_to(lse, (bq, 128))
            )[:8]
        ctx_ref[pl.ds(row0, bq), :] = merged.astype(BF16)


def attend(q, k, v, prefix):
    length, cols = q.shape
    heads = cols // HEAD_DIM
    block = min(512, length)
    return pl.pallas_call(
        functools.partial(attend_kernel, block, block),
        out_shape=(
            jax.ShapeDtypeStruct((length, cols), BF16),
            jax.ShapeDtypeStruct((8 * heads, length), F32),
        ),
        in_specs=[SM, VM, VM, VM],
        out_specs=(VM, VM),
        compiler_params=pltpu.CompilerParams(vmem_limit_bytes=VMEM_BYTES),
        name="attend",
    )(prefix, q, k, v)


def attend_back_kernel(
    bq,
    bk,
    prefix_ref,
    q_ref,
    k_ref,
    v_ref,
    grad_ref,
    ctx_ref,
    lse_ref,
    dq_ref,
    dk_ref,
    dv_ref,
    dq_acc,
    dk_acc,
    dv_acc,
    inner,
):
    length, cols = q_ref.shape
    heads = cols // HEAD_DIM
    prefix = prefix_ref[0]
    dq_acc[...] = jnp.zeros_like(dq_acc)
    ones = [pick_head(jnp.ones((8, cols), F32), head) for head in range(heads)]

    @pl.loop(0, length // bq)
    def _(blk):
        rows = pl.ds(pl.multiple_of(blk * bq, bq), bq)
        product = grad_ref[rows, :].astype(F32) * ctx_ref[rows, :].astype(F32)
        for head in range(heads):
            inner[pl.ds(8 * head, 8), rows] = dotf(
                ones[head], product, ((1,), (1,)), lax.Precision.HIGHEST
            )

    @pl.loop(0, length // bk)
    def _(kb):
        col0 = pl.multiple_of(kb * bk, bk)
        keys = k_ref[pl.ds(col0, bk), :]
        vals = v_ref[pl.ds(col0, bk), :]
        key_heads = [pick_head(keys, head) for head in range(heads)]
        dk_acc[...] = jnp.zeros_like(dk_acc)
        dv_acc[...] = jnp.zeros_like(dv_acc)
        first = jnp.where(col0 < prefix, 0, col0 // bq)
        full = jnp.where(col0 + bk <= prefix, 0, (col0 + bk + bq - 2) // bq)
        full = jnp.maximum(first, full)

        def step(blk, _, masked):
            row0 = pl.multiple_of(blk * bq, bq)
            rows = pl.ds(row0, bq)
            q = q_ref[rows, :]
            grad = grad_ref[rows, :]
            if masked:
                key_ids = iota((bk, bq), 0) + col0
                row_ids = iota((bk, bq), 1) + row0
                seen = (key_ids <= row_ids) | (key_ids < prefix)
            dq = dq_acc[rows, :]
            dk = dk_acc[...]
            dv = dv_acc[...]
            for head in range(heads):
                q_head = pick_head(q, head)
                grad_head = pick_head(grad, head)
                soft = jnp.exp2(
                    dotf(keys, q_head, ((1,), (1,))) * SCORE_LOG2 - lse_ref[pl.ds(8 * head, 1), rows]
                )
                if masked:
                    soft = jnp.where(seen, soft, 0.0)
                grad_soft = dotf(vals, grad_head, ((1,), (1,)))
                grad_scores = (soft * (grad_soft - inner[pl.ds(8 * head, 1), rows])).astype(BF16)
                dv += dotf(soft.astype(BF16), grad_head)
                dk += dotf(grad_scores, q_head)
                dq += dotf(grad_scores, key_heads[head], ((0,), (0,)))
            dq_acc[rows, :] = dq
            dk_acc[...] = dk
            dv_acc[...] = dv
            return 0

        lax.fori_loop(first, full, functools.partial(step, masked=True), 0)
        lax.fori_loop(full, length // bq, functools.partial(step, masked=False), 0)
        dk_ref[pl.ds(col0, bk), :] = (dk_acc[...] * SCORE_SCALE).astype(BF16)
        dv_ref[pl.ds(col0, bk), :] = dv_acc[...].astype(BF16)

    dq_ref[...] = (dq_acc[...] * SCORE_SCALE).astype(BF16)


def attend_back(q, k, v, grad, ctx, lse, prefix):
    length, cols = q.shape
    block = min(512, length)
    out = jax.ShapeDtypeStruct((length, cols), BF16)
    return pl.pallas_call(
        functools.partial(attend_back_kernel, block, block),
        out_shape=(out, out, out),
        in_specs=[SM] + [VM] * 6,
        out_specs=(VM, VM, VM),
        scratch_shapes=[
            pltpu.VMEM((length, cols), F32),
            pltpu.VMEM((block, cols), F32),
            pltpu.VMEM((block, cols), F32),
            pltpu.VMEM(lse.shape, F32),
        ],
        compiler_params=pltpu.CompilerParams(vmem_limit_bytes=VMEM_BYTES),
        name="attend_back",
    )(prefix, q, k, v, grad, ctx, lse)


def middle_kernel(
    ctx_ref,
    tok_ref,
    gain_ref,
    wo_ref,
    router_ref,
    kept_ref,
    cot_ref,
    win_ref,
    wout_ref,
    out_ref,
    gres_ref,
    gctx_ref,
    dwin_ref,
    dwout_ref,
    dwo_ref,
    drouter_ref,
    dgain_ref,
    ctx_s,
    wide_router,
    res_s,
    scaled_s,
    spread_s,
    mixer_s,
    gmix_s,
    weight_s,
    low_s,
    out_s,
    in_s,
    done_s,
    ret_s,
    hidden_s,
    gpre_s,
    gctx_s,
    glog_s,
    gatt_s,
    ctx_sems,
    mix_sems,
    ret_sems,
    back_sems,
    *,
    experts,
):
    rows, width = tok_ref.shape
    place = lax.axis_index("tensor")
    me = lax.axis_index("expert")
    groups = rows // GROUP
    wide = experts * groups
    hcols = ctx_ref.shape[1]
    step_rows = 128
    steps = rows // step_rows
    peers = experts
    barrier = pltpu.get_barrier_semaphore()
    greet("tensor", TENSOR)
    greet("expert", peers)
    pl.semaphore_wait(barrier, TENSOR - 1 + peers - 1)

    def ctx_copy(off):
        to = lax.rem(place + off, TENSOR)
        block = ctx_ref.at[pl.ds(pl.multiple_of(to * rows, rows), rows), :]
        return remote(
            block, ctx_s.at[place], ctx_sems.at[0, off], ctx_sems.at[1, off], "tensor", to
        )

    ctx_copies = [ctx_copy(off) for off in (2, 1, 3)]
    for copy in ctx_copies:
        copy.start()
    ctx_s[place] = ctx_ref[pl.ds(pl.multiple_of(place * rows, rows), rows), :]
    to_wide = jnp.where(iota((experts, wide), 0) == iota((experts, wide), 1) // groups, 1.0, 0.0)
    to_wide = to_wide.astype(BF16)
    wide_router[...] = dotf(router_ref[...], to_wide).astype(BF16)
    gmix_s[...] = cot_ref[...].astype(BF16)
    for copy in ctx_copies:
        copy.wait_recv()

    @pl.loop(0, steps)
    def _(step):
        part = pl.ds(pl.multiple_of(step * step_rows, step_rows), step_rows)
        ctx = jnp.concatenate([ctx_s[at, part, :] for at in range(TENSOR)], axis=1)
        residual = tok_ref[part, :].astype(F32) + dotf(ctx, wo_ref[...])
        res_s[part, :] = residual
        scaled, spread = norm_parts(residual)
        scaled_s[part, :] = scaled
        spread_s[part, :] = jnp.broadcast_to(spread, (step_rows, 128))
        mixer = (scaled * gain_ref[...]).astype(BF16)
        mixer_s[part, :] = mixer
        logits = dotf(mixer, wide_router[...])
        kept = kept_ref[part, :].astype(F32)
        terms = jnp.where(kept > 0.0, jnp.exp(logits), 0.0)
        total = jnp.sum(terms, axis=0, keepdims=True)
        count = jnp.sum(kept, axis=0, keepdims=True)
        weight = terms / jnp.where(count > 0.0, total, 1.0)
        weight_s[part, :] = weight
        low_s[part, :] = weight.astype(BF16)

    def mix_to(src_ref, kind):
        @pl.loop(0, wide // 128)
        def _(blk):
            cols = pl.ds(pl.multiple_of(blk * 128, 128), 128)
            mixed = dotf(low_s[:, cols], src_ref[...], ((0,), (0,))).astype(BF16)
            count = 128 // groups
            out_s[pl.ds(blk * count, count), kind] = mixed.reshape(count, groups, width)

    mix_to(mixer_s, 0)
    mix_to(gmix_s, 1)

    def mix_copy(off):
        to = lax.rem(me + off, peers)
        return remote(
            out_s.at[to], in_s.at[off], mix_sems.at[0, off], mix_sems.at[1, off], "expert", to
        )

    def start_mix(off, _):
        mix_copy(off).start()
        return 0

    lax.fori_loop(1, peers, start_mix, 0)
    in_s[0] = out_s[me]

    def ret_copy(off):
        to = lax.rem(me + peers - off, peers)
        return remote(
            done_s.at[off], ret_s.at[me], ret_sems.at[0, off], ret_sems.at[1, off], "expert", to
        )

    batch = 128 // groups
    slices, _, fcols = win_ref.shape

    @pl.loop(0, peers // batch)
    def _(chunk):
        def wait_mix(off, _):
            mix_copy(off).wait_recv()
            return 0

        begin = chunk * batch
        lax.fori_loop(jnp.maximum(begin, 1), begin + batch, wait_mix, 0)
        slots = pl.ds(begin, batch)
        part = pl.ds(pl.multiple_of(chunk * 128, 128), 128)
        mixed = in_s[slots, 0].reshape(128, width)
        grad = in_s[slots, 1].reshape(128, width)

        def one_slice(at, carry):
            returned, grad_mixed = carry
            pre = dotf(mixed, win_ref[at])
            sigma = 1.0 / (1.0 + jnp.exp(-pre))
            hidden = (pre * sigma).astype(BF16)
            grad_hidden = dotf(grad, wout_ref[at], ((1,), (1,)))
            grad_pre = (grad_hidden * (sigma * (1.0 + pre * (1.0 - sigma)))).astype(BF16)
            hidden_s[at, part, :] = hidden
            gpre_s[at, part, :] = grad_pre
            returned = returned + dotf(hidden, wout_ref[at])
            grad_mixed = grad_mixed + dotf(grad_pre, win_ref[at], ((1,), (1,)))
            return returned, grad_mixed

        zero = jnp.zeros((128, width), F32)
        returned, grad_mixed = lax.fori_loop(0, slices, one_slice, (zero, zero))
        done_s[slots, 0] = returned.astype(BF16).reshape(batch, groups, width)
        done_s[slots, 1] = grad_mixed.astype(BF16).reshape(batch, groups, width)

        def start_ret(off, _):
            ret_copy(off).start()
            return 0

        lax.fori_loop(jnp.maximum(begin, 1), begin + batch, start_ret, 0)

    ret_s[me] = done_s[0]

    @pl.loop(0, slices)
    def _(at):
        mixed = in_s[:, 0].reshape(wide, width)
        grad = in_s[:, 1].reshape(wide, width)
        dwin_ref[at] = dotf(mixed, gpre_s[at], ((0,), (0,))).astype(BF16)
        dwout_ref[at] = dotf(hidden_s[at], grad, ((0,), (0,))).astype(BF16)

    def wait_ret(off, _):
        ret_copy(off).wait_recv()
        return 0

    lax.fori_loop(1, peers, wait_ret, 0)

    dgain_ref[...] = jnp.zeros_like(dgain_ref)
    from_wide = jnp.where(iota((wide, experts), 0) // groups == iota((wide, experts), 1), 1.0, 0.0)
    from_wide = from_wide.astype(BF16)

    @pl.loop(0, steps)
    def _(step):
        part = pl.ds(pl.multiple_of(step * step_rows, step_rows), step_rows)
        returned = ret_s[:, 0].reshape(wide, width)
        grad_mixed = ret_s[:, 1].reshape(wide, width)
        low = low_s[part, :]
        weight = weight_s[part, :]
        mixer = mixer_s[part, :]
        out_ref[part, :] = (res_s[part, :] + dotf(low, returned)).astype(BF16)
        grad_weight = dotf(gmix_s[part, :], returned, ((1,), (1,)))
        grad_weight = grad_weight + dotf(mixer, grad_mixed, ((1,), (1,)))
        inner = jnp.sum(weight * grad_weight, axis=0, keepdims=True)
        grad_logits = (weight * (grad_weight - inner)).astype(BF16)
        glog_s[part, :] = dotf(grad_logits, from_wide).astype(BF16)
        grad_mixer = dotf(low, grad_mixed) + dotf(grad_logits, wide_router[...], ((1,), (1,)))
        scaled = scaled_s[part, :]
        dgain_ref[...] += jnp.sum(grad_mixer * scaled, axis=0, keepdims=True)
        grad_scaled = grad_mixer * gain_ref[...]
        centered = grad_scaled - jnp.mean(grad_scaled, axis=1, keepdims=True)
        along = jnp.mean(grad_scaled * scaled, axis=1, keepdims=True)
        grad_res = cot_ref[part, :] + spread_s[part, 0:1] * (centered - scaled * along)
        gres_ref[part, :] = grad_res
        grad_att = grad_res.astype(BF16)
        gatt_s[part, :] = grad_att
        grad_ctx = dotf(grad_att, wo_ref[...], ((1,), (1,))).astype(BF16)
        for at in range(TENSOR):
            gctx_s[at, part, :] = grad_ctx[:, at * hcols : (at + 1) * hcols]

    def back_copy(off):
        to = lax.rem(place + off, TENSOR)
        block = gctx_ref.at[pl.ds(pl.multiple_of(place * rows, rows), rows), :]
        return remote(
            gctx_s.at[to], block, back_sems.at[0, off], back_sems.at[1, off], "tensor", to
        )

    back_copies = [back_copy(off) for off in (2, 1, 3)]
    for copy in back_copies:
        copy.start()
    gctx_ref[pl.ds(pl.multiple_of(place * rows, rows), rows), :] = gctx_s[place]
    for at in range(TENSOR):
        dwo_ref[at] = dotf(ctx_s[at], gatt_s[...], ((0,), (0,))).astype(BF16)
    drouter_ref[...] = dotf(glog_s[...], mixer_s[...], ((0,), (0,)))

    def wait_sent(off, _):
        mix_copy(off).wait_send()
        ret_copy(off).wait_send()
        return 0

    lax.fori_loop(1, peers, wait_sent, 0)
    for copy in back_copies:
        copy.wait_recv()
    for copy in ctx_copies + back_copies:
        copy.wait_send()


def middle(ctx, tokens, gain, wo, router, kept, cot, win, wout):
    rows, width = tokens.shape
    experts = router.shape[1]
    groups = rows // GROUP
    wide = experts * groups
    slices, _, fcols = win.shape
    hcols = ctx.shape[1]

    def dev(shape, kind):
        return jax.ShapeDtypeStruct(shape, kind)

    return pl.pallas_call(
        functools.partial(middle_kernel, experts=experts),
        out_shape=(
            dev((rows, width), BF16),
            dev((rows, width), F32),
            dev(ctx.shape, BF16),
            dev((slices, width, fcols), BF16),
            dev((slices, fcols, width), BF16),
            dev((TENSOR, hcols, width), BF16),
            dev((experts, width), F32),
            dev((1, width), F32),
        ),
        in_specs=[VM] * 9,
        out_specs=(VM,) * 8,
        scratch_shapes=[
            pltpu.VMEM((TENSOR, rows, hcols), BF16),
            pltpu.VMEM((width, wide), BF16),
            pltpu.VMEM((rows, width), F32),
            pltpu.VMEM((rows, width), F32),
            pltpu.VMEM((rows, 128), F32),
            pltpu.VMEM((rows, width), BF16),
            pltpu.VMEM((rows, width), BF16),
            pltpu.VMEM((rows, wide), F32),
            pltpu.VMEM((rows, wide), BF16),
            pltpu.VMEM((experts, 2, groups, width), BF16),
            pltpu.VMEM((experts, 2, groups, width), BF16),
            pltpu.VMEM((experts, 2, groups, width), BF16),
            pltpu.VMEM((experts, 2, groups, width), BF16),
            pltpu.VMEM((slices, wide, fcols), BF16),
            pltpu.VMEM((slices, wide, fcols), BF16),
            pltpu.VMEM((TENSOR, rows, hcols), BF16),
            pltpu.VMEM((rows, experts), BF16),
            pltpu.VMEM((rows, width), BF16),
            pltpu.SemaphoreType.DMA((2, TENSOR)),
            pltpu.SemaphoreType.DMA((2, experts)),
            pltpu.SemaphoreType.DMA((2, experts)),
            pltpu.SemaphoreType.DMA((2, TENSOR)),
        ],
        compiler_params=pltpu.CompilerParams(
            collective_id=1, has_side_effects=True, vmem_limit_bytes=VMEM_BYTES
        ),
        name="middle",
    )(ctx, tokens, gain, wo, router, kept, cot, win, wout)


def last_kernel(
    seq_ref,
    dq_ref,
    dk_ref,
    dv_ref,
    wq_ref,
    wk_ref,
    wv_ref,
    tok_ref,
    gain_ref,
    gres_ref,
    dwo_ref,
    drouter_ref,
    dgain_ref,
    gtok_ref,
    gq_ref,
    gk_ref,
    gv_ref,
    go_ref,
    small_ref,
    w_s,
    part_s,
    land_s,
    low_s,
    piece_s,
    gather_s,
    sum_s,
    all_s,
    small_s,
    row_sems,
    piece_sems,
    sum_sems,
    small_sems,
):
    rows, width = tok_ref.shape
    half = rows // 2
    hcols = wq_ref.shape[1]
    place = lax.axis_index("tensor")
    me = lax.axis_index("expert")
    peers = gather_s.shape[0]
    right, left = lax.rem(place + 1, TENSOR), lax.rem(place + TENSOR - 1, TENSOR)
    far = lax.rem(place + 2, TENSOR)
    barrier = pltpu.get_barrier_semaphore()
    greet("tensor", TENSOR)
    greet("expert", peers)
    w_s[:, 0:hcols] = wq_ref[...]
    w_s[:, hcols : 2 * hcols] = wk_ref[...]
    w_s[:, 2 * hcols : 3 * hcols] = wv_ref[...]

    def heads_grad(start, count):
        part = pl.ds(pl.multiple_of(start, count), count)
        return jnp.concatenate([dq_ref[part, :], dk_ref[part, :], dv_ref[part, :]], axis=1)

    def partial_rows(owner, piece):
        return dotf(heads_grad(owner * rows + piece * half, half), w_s[...], ((1,), (1,)))

    low, high = pl.ds(0, half), pl.ds(half, half)
    low_s[0, low, :] = partial_rows(far, 0).astype(BF16)
    low_s[1, high, :] = partial_rows(far, 1).astype(BF16)
    pl.semaphore_wait(barrier, TENSOR - 1 + peers - 1)

    def row_copy(slot, src, part, to):
        return remote(
            low_s.at[src, part, :],
            land_s.at[slot // 2, part, :],
            row_sems.at[0, slot],
            row_sems.at[1, slot],
            "tensor",
            to,
        )

    far_low = row_copy(0, 0, low, right)
    far_high = row_copy(1, 1, high, left)
    far_low.start()
    far_high.start()
    low_s[2, high, :] = partial_rows(right, 1).astype(BF16)
    right_high = row_copy(2, 2, high, right)
    right_high.start()
    low_s[3, low, :] = partial_rows(left, 0).astype(BF16)
    left_low = row_copy(4, 3, low, left)
    left_low.start()
    part_s[low, :] = partial_rows(right, 0)
    part_s[high, :] = partial_rows(left, 1)

    def grads_of(at, acc):
        part = pl.ds(pl.multiple_of(at * rows, rows), rows)
        return acc + dotf(seq_ref[part, :], heads_grad(at * rows, rows), ((0,), (0,)))

    grads = lax.fori_loop(0, TENSOR, grads_of, jnp.zeros((width, 3 * hcols), F32))
    for at in range(3):
        piece_s[:, at] = (
            grads[:, at * hcols : (at + 1) * hcols].astype(BF16).reshape(peers, width // peers, hcols)
        )
    blocks = width // hcols
    dwo = dwo_ref[...]
    piece_s[:, 3] = jnp.concatenate(
        [dwo[:, at * hcols : (at + 1) * hcols] for at in range(blocks)], axis=0
    ).reshape(peers, width // peers, hcols)
    ones = jnp.ones((8, 3 * hcols), F32)
    dfirst = dotf(ones, grads * w_s[...].astype(F32), ((1,), (1,)), lax.Precision.HIGHEST)
    dfirst = dfirst[0:1] / gain_ref[...]
    experts = drouter_ref.shape[0]
    small_rows = jnp.concatenate(
        [drouter_ref[...], dfirst, dgain_ref[...], jnp.zeros((width // blocks - experts - 2, width), F32)],
        axis=0,
    ).astype(BF16)
    piece_s[:, 4] = jnp.concatenate(
        [small_rows[:, at * hcols : (at + 1) * hcols] for at in range(blocks)], axis=0
    ).reshape(peers, width // peers, hcols)

    def piece_copy(off):
        to = lax.rem(me + off, peers)
        return remote(
            piece_s.at[to], gather_s.at[off], piece_sems.at[0, off], piece_sems.at[1, off], "expert", to
        )

    def start_piece(off, _):
        piece_copy(off).start()
        return 0

    lax.fori_loop(1, peers, start_piece, 0)
    gather_s[0] = piece_s[me]

    far_low.wait_recv()
    low_s[2, low, :] = (part_s[low, :] + land_s[0, low, :].astype(F32)).astype(BF16)
    right_low = row_copy(3, 2, low, right)
    right_low.start()
    far_high.wait_recv()
    low_s[3, high, :] = (part_s[high, :] + land_s[0, high, :].astype(F32)).astype(BF16)
    left_high = row_copy(5, 3, high, left)
    left_high.start()
    part_s[low, :] = partial_rows(place, 0)
    part_s[high, :] = partial_rows(place, 1)

    def wait_piece(off, _):
        piece_copy(off).wait_recv()
        return 0

    lax.fori_loop(1, peers, wait_piece, 0)

    def add_up(off, acc):
        return acc + gather_s[off].astype(F32)

    sum_s[...] = lax.fori_loop(0, peers, add_up, jnp.zeros(sum_s.shape, F32)).astype(BF16)

    def sum_copy(off):
        to = lax.rem(me + off, peers)
        return remote(sum_s, all_s.at[me], sum_sems.at[0, off], sum_sems.at[1, off], "expert", to)

    def start_sum(off, _):
        sum_copy(off).start()
        return 0

    lax.fori_loop(1, peers, start_sum, 0)
    all_s[me] = sum_s[...]

    for copy in (right_high, right_low, left_low, left_high):
        copy.wait_recv()
    for part in (low, high):
        grad_normed = part_s[part, :] + land_s[1, part, :].astype(F32) + land_s[2, part, :].astype(F32)
        scaled, spread = norm_parts(tok_ref[part, :].astype(F32))
        grad_scaled = grad_normed * gain_ref[...]
        centered = grad_scaled - jnp.mean(grad_scaled, axis=1, keepdims=True)
        along = jnp.mean(grad_scaled * scaled, axis=1, keepdims=True)
        gtok_ref[part, :] = gres_ref[part, :] + spread * (centered - scaled * along)

    def wait_sum(off, _):
        sum_copy(off).wait_recv()
        return 0

    lax.fori_loop(1, peers, wait_sum, 0)
    small = all_s[:, 4].reshape(width, hcols)
    each = width // blocks
    small_s[place] = jnp.concatenate(
        [small[at * each : at * each + small_s.shape[1]] for at in range(blocks)], axis=1
    ).astype(F32)

    def small_copy(off):
        to = lax.rem(place + off, TENSOR)
        return remote(
            small_s.at[place], small_s.at[place], small_sems.at[0, off], small_sems.at[1, off], "tensor", to
        )

    small_copies = [small_copy(off) for off in (2, 1, 3)]
    for copy in small_copies:
        copy.start()
    for at, out_ref in enumerate((gq_ref, gk_ref, gv_ref)):
        out_ref[...] = all_s[:, at].reshape(width, hcols).astype(F32)
    out_grad = all_s[:, 3].reshape(width, hcols).astype(F32)
    for at in range(blocks):
        go_ref[:, at * hcols : (at + 1) * hcols] = out_grad[at * each : (at + 1) * each]
    for copy in (far_low, far_high, right_high, right_low, left_low, left_high):
        copy.wait_send()

    def wait_sent(off, _):
        piece_copy(off).wait_send()
        sum_copy(off).wait_send()
        return 0

    lax.fori_loop(1, peers, wait_sent, 0)
    for copy in small_copies:
        copy.wait_recv()
    small_ref[...] = small_s[0] + small_s[1] + small_s[2] + small_s[3]
    for copy in small_copies:
        copy.wait_send()


def last(seq, dq, dk, dv, wq, wk, wv, tokens, gain, gres, dwo, drouter, dgain, peers):
    rows, width = tokens.shape
    hcols = wq.shape[1]
    experts = drouter.shape[0]
    small_rows = (experts + 2 + 15) // 16 * 16

    def dev(shape, kind):
        return jax.ShapeDtypeStruct(shape, kind)

    piece = (5, width // peers, hcols)
    return pl.pallas_call(
        last_kernel,
        out_shape=(
            dev((rows, width), F32),
            dev(wq.shape, F32),
            dev(wq.shape, F32),
            dev(wq.shape, F32),
            dev((hcols, width), F32),
            dev((small_rows, width), F32),
        ),
        in_specs=[VM] * 13,
        out_specs=(VM,) * 6,
        scratch_shapes=[
            pltpu.VMEM((width, 3 * hcols), BF16),
            pltpu.VMEM((rows, width), F32),
            pltpu.VMEM((3, rows, width), BF16),
            pltpu.VMEM((4, rows, width), BF16),
            pltpu.VMEM((peers,) + piece, BF16),
            pltpu.VMEM((peers,) + piece, BF16),
            pltpu.VMEM(piece, BF16),
            pltpu.VMEM((peers,) + piece, BF16),
            pltpu.VMEM((TENSOR, small_rows, width), F32),
            pltpu.SemaphoreType.DMA((2, 6)),
            pltpu.SemaphoreType.DMA((2, peers)),
            pltpu.SemaphoreType.DMA((2, peers)),
            pltpu.SemaphoreType.DMA((2, TENSOR)),
        ],
        compiler_params=pltpu.CompilerParams(
            collective_id=2, has_side_effects=True, vmem_limit_bytes=VMEM_BYTES
        ),
        name="last",
    )(seq, dq, dk, dv, wq, wk, wv, tokens, gain, gres, dwo, drouter, dgain)


def body(
    tokens,
    first_gain,
    second_gain,
    query_weight,
    key_weight,
    value_weight,
    output_weight,
    router_weight,
    expert_in,
    expert_out,
    cotangent,
    routes,
    priority,
    prefix_len,
):
    rows, width = tokens.shape
    experts = router_weight.shape[1]
    peers = lax.axis_size("expert")
    capacity = (5 * GROUP * TOP + 4 * experts - 1) // (4 * experts)
    gain_one = first_gain.reshape(1, width)
    gain_two = second_gain.reshape(1, width)
    seq, q, k, v, kept = project_rows(
        tokens, gain_one, query_weight, key_weight, value_weight, routes, priority, experts, capacity
    )
    wo = lax.all_gather(output_weight, "tensor", axis=0, tiled=True)
    win = lax.all_gather(expert_in, "tensor", axis=0, tiled=True)
    wout = lax.all_gather(expert_out, "tensor", axis=0, tiled=True)
    ctx, lse = attend(q, k, v, prefix_len)
    out, gres, gctx, dwin, dwout, dwo, drouter, dgain = middle(
        ctx, tokens, gain_two, wo, router_weight, kept, cotangent, win, wout
    )
    dwo = lax.psum_scatter(dwo, "tensor", scatter_dimension=0, tiled=True)
    dwin = lax.psum_scatter(dwin, "tensor", scatter_dimension=0, tiled=True)
    dwout = lax.psum_scatter(dwout, "tensor", scatter_dimension=0, tiled=True)
    dq, dk, dv = attend_back(q, k, v, gctx, ctx, lse, prefix_len)
    gtok, gq, gk, gv, go, small = last(
        seq,
        dq,
        dk,
        dv,
        query_weight,
        key_weight,
        value_weight,
        tokens,
        gain_one,
        gres,
        dwo[0],
        drouter,
        dgain,
        peers,
    )
    return (
        out,
        gtok,
        small[experts],
        small[experts + 1],
        gq,
        gk,
        gv,
        go,
        small[:experts].T,
        dwin.astype(F32),
        dwout.astype(F32),
    )


def solution(mesh):
    in_specs = (
        P(("expert", "tensor"), None),
        P(),
        P(),
        P(None, "tensor"),
        P(None, "tensor"),
        P(None, "tensor"),
        P("tensor", None),
        P(),
        P("expert", None, "tensor"),
        P("expert", "tensor", None),
        P(("expert", "tensor"), None),
        P(("expert", "tensor"), None),
        P(("expert", "tensor"), None),
        P("expert"),
    )
    out_specs = (
        P(("expert", "tensor"), None),
        P(("expert", "tensor"), None),
        P(),
        P(),
        P(None, "tensor"),
        P(None, "tensor"),
        P(None, "tensor"),
        P("tensor", None),
        P(),
        P("expert", None, "tensor"),
        P("expert", "tensor", None),
    )
    return jax.shard_map(body, mesh=mesh, in_specs=in_specs, out_specs=out_specs, check_vma=False)
```

time: 788 us -> 285 us (0.36); the launches traced: 777 us -> 284 us
  waiting for transfers between devices: 381 us -> 29.2 us
  Pallas kernels: 0 us -> 189 us
  matrix products: 132 us -> 0 us
  blocking collectives: 129 us -> 14.4 us
  other arithmetic: 62.2 us -> 4.29 us
  loops' own time: 16.4 us -> 0 us
  starting transfers between devices: 13.6 us -> 0.37 us
    pallas_call x0 -> x5, Pallas kernels: none -> 189 us  [the longest x1 70.7 us: middle(): pl.pallas_call(functools.partial(middle_kernel, experts=experts), out_sha...]
    psum x2 -> x0, waiting for transfers between devices: 163 us -> none  [the longest x1 88.3 us: body(): lax.psum(query_part.astype(jnp.bfloat16), 'expert').astype(jnp.float32)]
    dot_general x56 -> x0, matrix products: 132 us -> none  [the longest x8 21.8 us: block_scores(): jnp.einsum('qhd,khd->hqk', query_blk, key_rows, preferred_element_type=jn...]
    all_gather x4 -> x2, waiting for transfers between devices: 114 us -> 8.78 us  [the longest x1 8.78 us: body(): wout = lax.all_gather(expert_out, 'tensor', axis=0, tiled=True)]
    psum x1 -> x0, blocking collectives: 64.7 us -> none  [body(): lax.psum((first_part, second_part, router_part), ('expert', 'tensor'))]
    all_to_all x2 -> x0, blocking collectives: 64.6 us -> none  [the longest x1 32.6 us: body(): lax.all_to_all(to_homes(grad_part, expert_size).astype(jnp.bfloat16), 'ex...]
    reduce_scatter x4 -> x3, waiting for transfers between devices: 79.3 us -> 18.2 us  [the longest x1 18.2 us: body(): dwin = lax.psum_scatter(dwin, 'tensor', scatter_dimension=0, tiled=True)]
    unnamed x79 -> x78, local copies, waits for them, and re-layouts: 4 us -> 31 us
  transfers between devices with their start and end apart: 12 -> 5, of which waited for: 11 -> 2; matrix products, arithmetic and copies ran while one was open for 6% -> 2% of each run, Pallas kernels for 0% -> 42%
where the time goes in v1:
time: 285 us; the launch traced here: 284 us
  Pallas kernels  189 us (66%)
  local copies, waits for them, and re-layouts  32.2 us (11%)
  waiting for transfers between devices  29.2 us (10%)
  between operations  14.6 us (5%)
  blocking collectives  14.4 us (5%)
  other arithmetic  4.29 us (2%)
    pallas_call x1, Pallas kernels, middle(): pl.pallas_call(functools.partial(middle_kernel, experts=experts), out_sha...  70.7 us
    pallas_call x1, Pallas kernels, last(): pl.pallas_call(last_kernel, out_shape=(dev((rows, width), F32), dev(wq.sh...  45.8 us
    pallas_call x1, Pallas kernels, project_rows(): pl.pallas_call(functools.partial(project_kernel, experts=experts, capacit...  34.6 us
    unnamed x78, local copies, waits for them, and re-layouts  31 us
    pallas_call x1, Pallas kernels, attend_back(): pl.pallas_call(functools.partial(attend_back_kernel, block, block), out_s...  20.3 us
    reduce_scatter x1, waiting for transfers between devices, body(): dwin = lax.psum_scatter(dwin, 'tensor', scatter_dimension=0, tiled=True)  18.2 us
    pallas_call x1, Pallas kernels, attend(): pl.pallas_call(functools.partial(attend_kernel, block, block), out_shape=...  17.3 us
    all_gather x1, blocking collectives, body(): wo = lax.all_gather(output_weight, 'tensor', axis=0, tiled=True)  14.4 us
  transfers between devices with their start and end apart: 5, of which 2 were waited for; matrix products, arithmetic and copies ran while one was open for 2% of the time, Pallas kernels for 42%

profile of v1, /device:TPU:1, one launch (start us, length us, event | category | flops | bytes accessed | tf_op | source)
XLA Modules:
  0.0 283.8 jit_solution(16384355157113251525)
XLA Ops:
  7.2 0.0 all-gather.3.cloned.1.call-start
  7.2 0.7 all-gather.3.cloned.1.call-update
  7.9 0.0 copy-start.1
  7.9 0.0 all-gather.5.cloned.1.call-start
  8.0 0.7 all-gather.5.cloned.1.call-update
  8.7 0.0 reduce-scatter.4.cloned.1.call-start
  9.4 0.9 copy.28.router_ref
  10.3 0.8 copy.27.routes_ref
  11.1 0.0 copy-start
  11.1 1.0 copy-done
  12.2 0.9 copy-done.14
  13.1 0.9 copy-done.16
  14.0 0.9 copy-done.18
  14.9 0.7 copy-done.30
  15.6 0.7 copy-done.32
  16.3 34.6 %project.1 = (bf16[2048,512]{1,0:T(8,128)(2,1)S(1)}, bf16[2048,128]{1,0:T(8,128)(2,1)S(1)}, bf16[2048,128]{1,0:T(8,128)(2,1)S(1)}, bf16[2048,128]{1,0:T(8,128)(2,1)S(1)}, bf16[512,512]{1,0:T(8,128)(2,1)S(1)}) custom-call(bf16[512,512]{1,0:T(8,128)(2,1)S(1)} %copy-done, f32[1,512]{1,0:T(1,128)S(1)} %bitcast.8, bf16[512,128]{1,0:T(8,128)(2,1)S(1)} %copy-done.14, ...), custom_call_target="tpu_custom_call" | custom-call | tf_op jit(solution)/shard_map/project/pallas_call | solution.py:174
  50.9 1.4 copy-done.2
  52.2 0.8 copy-done.6
  53.0 17.3 %attend.1 = (bf16[2048,128]{1,0:T(8,128)(2,1)S(1)}, f32[16,2048]{1,0:T(8,128)S(1)}) custom-call(s32[1]{0:T(128)S(6)} %copy.35.prefix_ref, bf16[2048,128]{1,0:T(8,128)(2,1)S(1)} %get-tuple-element.35.q_ref, bf16[2048,128]{1,0:T(8,128)(2,1)S(1)} %get-tuple-element.36.k_ref, bf16[2048,128]{1,0:T(8,128)(2,1)S(1)} %get-tuple-element.37.v_ref), custom_call_target="tpu_custom_call" | custom-call | tf_op jit(solution)/shard_map/attend/pallas_call | solution.py:260
  70.3 0.0 copy-start.25
  70.4 0.6 copy-done.25
  71.0 14.4 %all_gather.9.wo_ref = bf16[512,512]{1,0:T(8,128)(2,1)S(1)} all-gather(bf16[128,512]{1,0:T(8,128)(2,1)S(1)} %copy-done.34), channel_id=1, replica_groups=mesh['expert'=32,'tensor'=4] {'tensor'}, dimensions={0}, use_global_device_ids=true | all-gather | bytes 655360 | tf_op jit(solution)/shard_map/all_gather | solution.py:947
  85.4 8.8 %all-gather.5.cloned.1.call-done.wout_ref = bf16[4,512,512]{2,1,0:T(8,128)(2,1)} async-done(((bf16[1,512,512]{2,1,0:T(8,128)(2,1)}), bf16[4,512,512]{2,1,0:T(8,128)(2,1)}) %all-gather.5.cloned.1.call-update) | async-done | bytes 2097168 | tf_op jit(solution)/shard_map/all_gather | solution.py:949
  94.2 1.2 copy-done.5
  95.4 1.0 copy-done.7
  96.4 70.7 %middle.1 = (bf16[512,512]{1,0:T(8,128)(2,1)S(1)}, f32[512,512]{1,0:T(8,128)S(1)}, bf16[2048,128]{1,0:T(8,128)(2,1)S(1)}, bf16[4,512,512]{2,1,0:T(8,128)(2,1)}, ...) custom-call(bf16[2048,128]{1,0:T(8,128)(2,1)S(1)} %get-tuple-element, ...), custom_call_target="tpu_custom_call" | custom-call | tf_op jit(solution)/shard_map/middle/pallas_call | solution.py:626
  167.2 1.0 copy-done.3
  168.1 0.8 copy-done.20
  168.9 0.8 copy-done.22
  169.8 0.8 copy-done.23
  170.6 0.6 copy-done.28
  171.2 0.0 reduce-scatter.4.cloned.1.call-update
  171.2 0.0 reduce-scatter.8.cloned.1.call-start
  171.3 0.5 reduce-scatter.8.cloned.1.call-update
  171.8 0.2 reduce-scatter.6.cloned.1.call-start
  172.1 0.0 copy-start.19
  172.1 0.0 copy-start.31
  172.1 0.3 reduce-scatter.6.cloned.1.call-update
  172.4 1.0 copy-done.24
  173.4 0.9 copy-done.26
  174.3 20.3 %attend_back.1 = (bf16[2048,128]{1,0:T(8,128)(2,1)S(1)}, bf16[2048,128]{1,0:T(8,128)(2,1)S(1)}, bf16[2048,128]{1,0:T(8,128)(2,1)S(1)}) custom-call(s32[1]{0:T(128)S(6)} %copy.35.prefix_ref, bf16[2048,128]{1,0:T(8,128)(2,1)S(1)} %get-tuple-element.35.q_ref, bf16[2048,128]{1,0:T(8,128)(2,1)S(1)} %get-tuple-element.36.k_ref, ...), custom_call_target="tpu_custom_call" | custom-call | tf_op jit(solution)/shard_map/attend_back/pallas_call | solution.py:360
  194.6 0.0 copy-start.8
  194.6 0.8 copy-done.8
  195.4 0.8 copy-done.10
  196.2 0.8 copy-done.12
  197.1 1.2 copy-done.4
  198.3 1.0 copy-done.9
  199.4 1.0 copy-done.11
  200.4 1.0 copy-done.13
  201.4 0.9 copy-done.27
  202.3 0.8 copy-done.29
  203.2 45.8 %last.1 = (f32[512,512]{1,0:T(8,128)S(1)}, f32[512,128]{1,0:T(8,128)S(1)}, f32[512,128]{1,0:T(8,128)S(1)}, f32[512,128]{1,0:T(8,128)S(1)}, f32[128,512]{1,0:T(8,128)S(1)}, /*index=5*/f32[48,512]{1,0:T(8,128)S(1)}) custom-call(bf16[2048,512]{1,0:T(8,128)(2,1)} %copy-done.2, bf16[2048,128]{1,0:T(8,128)(2,1)S(1)} %copy-done.9, ...), custom_call_target="tpu_custom_call" | custom-call | tf_op jit(solution)/shard_map/last/pallas_call | solution.py:888
  249.0 0.0 copy-start.21
  249.0 0.6 fusion
  249.6 0.6 slice_bitcast_fusion
  250.2 2.1 convert_element_type.7
  252.4 18.2 %reduce-scatter.6.cloned.1.call-done = bf16[1,512,512]{2,1,0:T(8,128)(2,1)} async-done(((bf16[4,512,512]{2,1,0:T(8,128)(2,1)}), bf16[1,512,512]{2,1,0:T(8,128)(2,1)}) %reduce-scatter.6.cloned.1.call-update) | async-done | bytes 524304 | tf_op jit(solution)/shard_map/reduce_scatter | solution.py:955
  270.5 2.1 convert_element_type.6
  272.7 0.8 copy.36
  273.5 1.0 copy.37
  274.4 0.7 copy.38
  275.2 0.7 copy.39
  275.9 0.7 copy.40
  276.6 0.7 copy.41
  (39 shorter events, 0.1 us)
Async XLA Ops:
  7.2 63.8 %copy-start.34 = (bf16[128,512]{1,0:T(8,128)(2,1)S(1)}, bf16[128,512]{1,0:T(8,128)(2,1)}, u32[]{:S(2)}) copy-start(bf16[128,512]{1,0:T(8,128)(2,1)} %param.20) | copy-start | bytes 393220
  7.2 78.2 %all-gather.3.cloned.1.call-start = ((), (), s32[]{:S(2)}) async-start(), calls=%async_computation.3 | async-start | bytes 2621440 | tf_op jit(solution)/shard_map/all_gather | solution.py:948
  7.9 86.2 %copy-start.1 = (bf16[512,512]{1,0:T(8,128)(2,1)S(1)}, bf16[512,512]{1,0:T(8,128)(2,1)}, u32[]{:S(2)}) copy-start(bf16[512,512]{1,0:T(8,128)(2,1)} %tok_ref.5) | copy-start | bytes 1572868
  7.9 86.2 %copy-start.33 = (f32[512]{0:T(512)S(1)}, f32[512]{0:T(512)}, u32[]{:S(2)}) copy-start(f32[512]{0:T(512)} %param.16) | copy-start | bytes 6148
  7.9 86.2 %all-gather.5.cloned.1.call-start = ((), (), s32[]{:S(2)}) async-start(), calls=%async_computation.4 | async-start | bytes 2621440 | tf_op jit(solution)/shard_map/all_gather | solution.py:949
  8.7 188.4 %reduce-scatter.4.cloned.1.call-start = ((), (), s32[]{:S(2)}) async-start(), calls=%async_computation.5 | async-start | bytes 655360 | tf_op jit(solution)/shard_map/reduce_scatter | solution.py:954
  11.1 1.0 copy-start
  12.2 0.9 copy-start.14
  13.1 0.9 copy-start.16
  14.0 0.9 copy-start.18
  14.9 0.7 copy-start.30
  15.6 0.7 copy-start.32
  50.9 1.4 copy-start.2
  52.2 0.8 copy-start.6
  70.3 0.7 copy-start.25
  94.2 1.2 copy-start.5
  95.4 1.0 copy-start.7
  167.2 1.0 copy-start.3
  168.1 0.8 copy-start.20
  168.9 0.8 copy-start.22
  169.8 0.8 copy-start.23
  170.6 0.6 copy-start.28
  171.2 79.0 %reduce-scatter.8.cloned.1.call-start = ((), (), s32[]{:S(2)}) async-start(), calls=%async_computation.7 | async-start | bytes 2621440 | tf_op jit(solution)/shard_map/reduce_scatter | solution.py:956
  171.8 98.7 %reduce-scatter.6.cloned.1.call-start = ((), (), s32[]{:S(2)}) async-start(), calls=%async_computation.6 | async-start | bytes 2621440 | tf_op jit(solution)/shard_map/reduce_scatter | solution.py:955
  172.0 25.0 %copy-start.15 = (bf16[512,128]{1,0:T(8,128)(2,1)S(1)}, bf16[512,128]{1,0:T(8,128)(2,1)}, u32[]{:S(2)}) copy-start(bf16[512,128]{1,0:T(8,128)(2,1)} %wq_ref.3) | copy-start | bytes 393220
  172.0 25.0 %copy-start.17 = (bf16[512,128]{1,0:T(8,128)(2,1)S(1)}, bf16[512,128]{1,0:T(8,128)(2,1)}, u32[]{:S(2)}) copy-start(bf16[512,128]{1,0:T(8,128)(2,1)} %wk_ref.3) | copy-start | bytes 393220
  172.1 25.0 %copy-start.19 = (bf16[512,128]{1,0:T(8,128)(2,1)S(1)}, bf16[512,128]{1,0:T(8,128)(2,1)}, u32[]{:S(2)}) copy-start(bf16[512,128]{1,0:T(8,128)(2,1)} %wv_ref.3) | copy-start | bytes 393220
  172.1 25.0 %copy-start.31 = (f32[512]{0:T(512)S(1)}, f32[512]{0:T(512)}, u32[]{:S(2)}) copy-start(f32[512]{0:T(512)} %param.15) | copy-start | bytes 6148
  172.4 1.0 copy-start.24
  173.4 0.9 copy-start.26
  194.6 0.8 copy-start.8
  195.4 0.8 copy-start.10
  196.2 0.8 copy-start.12
  197.1 1.2 copy-start.4
  198.3 1.0 copy-start.9
  199.4 1.0 copy-start.11
  200.4 1.0 copy-start.13
  201.4 0.9 copy-start.27
  202.3 0.8 copy-start.29
  249.0 23.7 %copy-start.21 = (bf16[512,512]{1,0:T(8,128)(2,1)S(1)}, bf16[512,512]{1,0:T(8,128)(2,1)}, u32[]{:S(2)}) copy-start(bf16[512,512]{1,0:T(8,128)(2,1)} %copy-done.20) | copy-start | bytes 1572868
Sparse Core Ops, SparseCore 0:
  9.7 46.7 all-gather.2
  58.1 36.0 all-gather.4
  171.3 20.5 reduce-scatter.3
  194.2 42.1 reduce-scatter.7
  238.7 31.7 reduce-scatter.5

commit v2 on v0

v2 whole, which is shorter than its diff:
```python
import functools

import jax
import jax.numpy as jnp
from jax import lax
from jax.experimental import pallas as pl
from jax.experimental.pallas import tpu as pltpu
from jax.sharding import PartitionSpec as P

HEAD_DIM = 64
GROUP = 32
TOP = 4
EPS = 1e-05
NEG = -1e30
SCORE_SCALE = HEAD_DIM**-0.5
PREFIX_MOST = 1024
MESH = pl.DeviceIdType.MESH
VM = pl.BlockSpec(memory_space=pltpu.VMEM)
SM = pl.BlockSpec(memory_space=pltpu.SMEM)
HB = pl.BlockSpec(memory_space=pltpu.HBM)
TENSOR = 4
VMEM_BYTES = 58 << 20
BF16 = jnp.bfloat16
F32 = jnp.float32


def dotf(left, right, dims=((1,), (0,)), precision=None):
    return lax.dot_general(
        left, right, (dims, ((), ())), preferred_element_type=F32, precision=precision
    )


def iota(shape, axis):
    return lax.broadcasted_iota(jnp.int32, shape, axis)


def one_hot(test):
    return jnp.where(test, 1.0, 0.0).astype(BF16)


def norm_parts(values):
    center = values - jnp.mean(values, axis=1, keepdims=True)
    spread = lax.rsqrt(jnp.mean(center * center, axis=1, keepdims=True) + EPS)
    return center * spread, spread


def remote(src, dst, sems, slot, axis, to):
    return pltpu.make_async_remote_copy(
        src_ref=src,
        dst_ref=dst,
        send_sem=sems.at[0, slot],
        recv_sem=sems.at[1, slot],
        device_id={axis: to},
        device_id_type=MESH,
    )


def greet(axis, size):
    barrier = pltpu.get_barrier_semaphore()
    me = lax.axis_index(axis)

    def one(off, _):
        pl.semaphore_signal(
            barrier, inc=1, device_id={axis: lax.rem(me + off, size)}, device_id_type=MESH
        )
        return 0

    lax.fori_loop(1, size, one, 0)


def each(first, last, act):
    def one(at, _):
        act(at)
        return 0

    lax.fori_loop(first, last, one, 0)


def block_of(start, size):
    return pl.ds(pl.multiple_of(start, size), size)


def pick_head(values, head, other=0.0):
    lane = iota(values.shape, 1)
    inside = (lane >= head * HEAD_DIM) & (lane < (head + 1) * HEAD_DIM)
    return jnp.where(inside, values, jnp.full_like(values, other))


class Gather:
    def __init__(self, buf, sems, place):
        self.buf, self.sems, self.place = buf, sems, place
        self.right, self.left = lax.rem(place + 1, TENSOR), lax.rem(place + TENSOR - 1, TENSOR)
        half = buf.shape[1] // 2
        self.low, self.high = pl.ds(0, half), pl.ds(half, half)

    def copy(self, slot):
        owner, part, to = (
            (self.place, self.low, self.right),
            (self.place, self.high, self.left),
            (self.place, self.high, self.right),
            (self.place, self.low, self.left),
            (self.left, self.low, self.right),
            (self.right, self.high, self.left),
        )[slot]
        block = self.buf.at[owner, part]
        return remote(block, block, self.sems, slot, "tensor", to)

    def start(self):
        for slot in range(4):
            self.copy(slot).start()

    def forward(self):
        self.copy(0).wait_recv()
        self.copy(4).start()
        self.copy(1).wait_recv()
        self.copy(5).start()

    def wait_near(self):
        self.copy(2).wait_recv()
        self.copy(3).wait_recv()

    def wait_far(self):
        self.copy(4).wait_recv()
        self.copy(5).wait_recv()

    def drain(self):
        for slot in range(6):
            self.copy(slot).wait_send()


class Scatter:
    def __init__(self, part, via, land, sems, place):
        self.part, self.via, self.land, self.sems, self.place = part, via, land, sems, place
        self.right, self.left = lax.rem(place + 1, TENSOR), lax.rem(place + TENSOR - 1, TENSOR)
        self.far = lax.rem(place + 2, TENSOR)
        half = part.shape[1] // 2
        self.low, self.high = pl.ds(0, half), pl.ds(half, half)

    def copy(self, slot):
        block, half, to, dst = (
            (self.far, self.low, self.right, self.via),
            (self.far, self.high, self.left, self.via),
            (self.right, self.high, self.right, self.land.at[0]),
            (self.left, self.low, self.left, self.land.at[1]),
            (self.right, self.low, self.right, self.land.at[0]),
            (self.left, self.high, self.left, self.land.at[1]),
        )[slot]
        return remote(self.part.at[block, half], dst.at[half], self.sems, slot, "tensor", to)

    def start_far(self):
        self.copy(0).start()
        self.copy(1).start()

    def start_own(self):
        self.copy(2).start()
        self.copy(3).start()

    def add_far(self):
        self.copy(0).wait_recv()
        self.part[self.right, self.low] = (
            self.part[self.right, self.low].astype(F32) + self.via[self.low].astype(F32)
        ).astype(BF16)
        self.copy(1).wait_recv()
        self.part[self.left, self.high] = (
            self.part[self.left, self.high].astype(F32) + self.via[self.high].astype(F32)
        ).astype(BF16)

    def start_sums(self):
        self.copy(4).start()
        self.copy(5).start()

    def wait(self):
        for slot in range(2, 6):
            self.copy(slot).wait_recv()

    def landed(self, rows):
        return self.land[0, rows].astype(F32) + self.land[1, rows].astype(F32)

    def drain(self):
        for slot in range(6):
            self.copy(slot).wait_send()


def layer_kernel(
    prefix_ref,
    tok_hbm,
    gain_one_hbm,
    gain_two_hbm,
    wq_hbm,
    wk_hbm,
    wv_hbm,
    wo_hbm,
    router_hbm,
    win_hbm,
    wout_hbm,
    cot_hbm,
    routes_hbm,
    prio_hbm,
    out_ref,
    gtok_ref,
    gq_ref,
    gk_ref,
    gv_ref,
    go_ref,
    small_ref,
    dfirst_ref,
    dwin_ref,
    dwout_ref,
    tok_s,
    gain_one,
    gain_two,
    w_s,
    wo_s,
    router_s,
    win_s,
    wout_s,
    cot_s,
    routes_s,
    prio_s,
    seq_s,
    q_s,
    k_s,
    v_s,
    kept_s,
    ctx_s,
    lse_s,
    ctx_all,
    wide_router,
    res_s,
    scaled_s,
    spread_s,
    pair_s,
    weight_s,
    low_s,
    out_s,
    in_s,
    done_s,
    ret_s,
    acc_s,
    hidden_s,
    gpre_s,
    gctx_s,
    gctx_all,
    gatt_s,
    glog_s,
    dgain_s,
    dwin_s,
    dwout_s,
    via_win,
    via_wout,
    land_win,
    land_wout,
    wop_s,
    wop_in,
    wop_sum,
    wop_all,
    dq_acc,
    dk_acc,
    dv_acc,
    inner_s,
    grads_s,
    rows_s,
    via_rows,
    land_rows,
    mine_s,
    piece_s,
    piece_in,
    sum_s,
    sum_all,
    first_s,
    local_sems,
    store_sems,
    tok_sems,
    win_sems,
    wout_sems,
    wo_sems,
    ctx_sems,
    mix_sems,
    ret_sems,
    back_sems,
    dwin_sems,
    dwout_sems,
    wop_sems,
    wopz_sems,
    wopb_sems,
    row_sems,
    piece_sems,
    sum_sems,
    first_sems,
    *,
    experts,
    capacity,
):
    place = lax.axis_index("tensor")
    me = lax.axis_index("expert")
    right, left = lax.rem(place + 1, TENSOR), lax.rem(place + TENSOR - 1, TENSOR)
    far = lax.rem(place + 2, TENSOR)
    _, rows, width = tok_s.shape
    length, hcols = q_s.shape
    heads = hcols // HEAD_DIM
    groups = rows // GROUP
    wide = experts * groups
    peers = experts
    barrier = pltpu.get_barrier_semaphore()
    greet("tensor", TENSOR)
    greet("expert", peers)

    loads = [
        (tok_hbm, tok_s.at[place]),
        (gain_one_hbm, gain_one),
        (wq_hbm, w_s.at[:, pl.ds(0, hcols)]),
        (wk_hbm, w_s.at[:, pl.ds(hcols, hcols)]),
        (wv_hbm, w_s.at[:, pl.ds(2 * hcols, hcols)]),
        (routes_hbm, routes_s),
        (prio_hbm, prio_s),
        (wo_hbm, wo_s.at[place]),
        (win_hbm, win_s.at[place]),
        (wout_hbm, wout_s.at[place]),
        (gain_two_hbm, gain_two),
        (router_hbm, router_s),
        (cot_hbm, cot_s),
    ]
    loads = [
        pltpu.make_async_copy(src, dst, local_sems.at[at]) for at, (src, dst) in enumerate(loads)
    ]
    for load in loads:
        load.start()

    tok_ring = Gather(tok_s, tok_sems, place)
    win_ring = Gather(win_s, win_sems, place)
    wout_ring = Gather(wout_s, wout_sems, place)
    wo_ring = Gather(wo_s, wo_sems, place)
    loads[0].wait()
    pl.semaphore_wait(barrier, TENSOR - 1 + peers - 1)
    tok_ring.start()
    for load in loads[1:5]:
        load.wait()

    half = rows // 2

    def project(owner, part):
        @pl.loop(0, 2)
        def _(at):
            count = half // 2
            start = part * half + at * count
            scaled, _ = norm_parts(tok_s[owner, block_of(start, count)].astype(F32))
            normed = (scaled * gain_one[...]).astype(BF16)
            to = block_of(owner * rows + start, count)
            seq_s[to, :] = normed
            out = dotf(normed, w_s[...]).astype(BF16)
            q_s[to, :] = out[:, 0:hcols] * SCORE_SCALE
            k_s[to, :] = out[:, hcols : 2 * hcols]
            v_s[to, :] = out[:, 2 * hcols : 3 * hcols]

    project(place, 0)
    project(place, 1)
    tok_ring.forward()

    loads[5].wait()
    loads[6].wait()
    size = GROUP
    to_wide = one_hot(iota((experts, wide), 0) == iota((experts, wide), 1) // groups)
    prio = prio_s[...].astype(F32).astype(BF16)
    spread_rows = dotf(one_hot((iota((rows, groups), 0) // size) == iota((rows, groups), 1)), prio)
    at_col = (iota((rows, size), 0) % size) == iota((rows, size), 1)
    prio_col = jnp.sum(jnp.where(at_col, spread_rows, 0.0), axis=1, keepdims=True)
    group_tok = one_hot((iota((groups, rows), 1) // size) == iota((groups, rows), 0))
    spread_cols = dotf(prio, group_tok, ((0,), (0,)))
    at_row = (iota((size, rows), 1) % size) == iota((size, rows), 0)
    prio_row = jnp.sum(jnp.where(at_row, spread_cols, 0.0), axis=0, keepdims=True)
    named = routes_s[0:1, :] == iota((experts, rows), 0)
    for pick in range(1, TOP):
        named = named | (routes_s[pick : pick + 1, :] == iota((experts, rows), 0))
    own_group = (iota((rows, wide), 0) // size) == (iota((rows, wide), 1) % groups)
    member = jnp.where(own_group, dotf(one_hot(named), to_wide, ((0,), (0,))), 0.0)
    rank = dotf(one_hot(prio_row < prio_col), member.astype(BF16))
    kept_s[...] = jnp.where(rank < capacity, member, 0.0).astype(BF16)

    tok_ring.copy(2).wait_recv()
    project(left, 0)
    project(left, 1)
    tok_ring.copy(3).wait_recv()
    project(right, 0)
    project(right, 1)
    for load in loads[7:10]:
        load.wait()
    tok_ring.copy(4).wait_recv()
    project(far, 0)
    tok_ring.copy(5).wait_recv()
    wo_ring.start()
    win_ring.start()
    project(far, 1)

    prefix = prefix_ref[0]
    block = rows

    @pl.loop(0, length // block)
    def _(blk):
        row0 = pl.multiple_of(blk * block, block)
        q = q_s[pl.ds(row0, block), :]
        q_heads = [pick_head(q, head) for head in range(heads)]

        def step(kb, carry, masked):
            col0 = pl.multiple_of(kb * block, block)
            keys = k_s[pl.ds(col0, block), :]
            vals = v_s[pl.ds(col0, block), :]
            out = []
            if masked:
                row_ids = iota((block, block), 0) + row0
                col_ids = iota((block, block), 1) + col0
                seen = (col_ids <= row_ids) | (col_ids < prefix)
            for head in range(heads):
                peak, acc = carry[2 * head : 2 * head + 2]
                scores = dotf(q_heads[head], keys, ((1,), (1,)))
                if masked:
                    scores = jnp.where(seen, scores, NEG)
                new_peak = jnp.maximum(peak, jnp.max(scores, axis=1, keepdims=True))
                soft = jnp.exp(scores - new_peak).astype(BF16)
                acc = jnp.exp(peak - new_peak) * acc + dotf(soft, pick_head(vals, head, 1.0))
                out += [new_peak, acc]
            return tuple(out)

        init = (jnp.full((block, 1), NEG, F32), jnp.zeros((block, hcols), F32)) * heads
        carry = lax.fori_loop(0, blk, functools.partial(step, masked=False), init)
        seen_blocks = jnp.maximum(blk + 1, PREFIX_MOST // block)
        carry = lax.fori_loop(blk, seen_blocks, functools.partial(step, masked=True), carry)
        merged = jnp.zeros((block, hcols), F32)
        for head in range(heads):
            peak, acc = carry[2 * head : 2 * head + 2]
            lane = HEAD_DIM if head == 0 else 0
            total = acc[:, lane : lane + 1]
            merged = merged + pick_head(acc * (1.0 / total), head)
            lse = jnp.broadcast_to(peak + jnp.log(total), (block, 128))
            lse_s[pl.ds(8 * head, 8), pl.ds(row0, block)] = jnp.transpose(lse)[:8]
        ctx_s[pl.ds(row0, block), :] = merged.astype(BF16)

        @pl.when(blk == 2)
        def _():
            wo_ring.forward()

    def ctx_copy(off):
        to = lax.rem(place + off, TENSOR)
        src = ctx_s.at[block_of(to * rows, rows), :]
        return remote(src, ctx_all.at[place], ctx_sems, off, "tensor", to)

    for off in (2, 1, 3):
        ctx_copy(off).start()
    ctx_all[place] = ctx_s[block_of(place * rows, rows), :]
    for load in loads[10:]:
        load.wait()
    wide_router[...] = dotf(to_wide, router_s[...], ((0,), (0,))).astype(BF16)
    pair_s[:, 0:width] = cot_s[...].astype(BF16)
    wo_ring.wait_near()
    wo_ring.wait_far()
    wo_full = wo_s.reshape(TENSOR * hcols, width)
    for off in (2, 1, 3):
        ctx_copy(off).wait_recv()
    wout_ring.start()
    win_ring.forward()

    step_rows = 128

    @pl.loop(0, rows // step_rows)
    def _(step):
        part = block_of(step * step_rows, step_rows)
        ctx = jnp.concatenate([ctx_all[at, part, :] for at in range(TENSOR)], axis=1)
        residual = tok_s[place, part].astype(F32) + dotf(ctx, wo_full[...])
        res_s[part, :] = residual
        scaled, spread = norm_parts(residual)
        scaled_s[part, :] = scaled
        spread_s[part, :] = jnp.broadcast_to(spread, (step_rows, 128))
        mixer = (scaled * gain_two[...]).astype(BF16)
        pair_s[part, width : 2 * width] = mixer
        logits = dotf(mixer, wide_router[...], ((1,), (1,)))
        kept = kept_s[part, :].astype(F32)
        terms = jnp.where(kept > 0.0, jnp.exp(logits), 0.0)
        total = jnp.sum(terms, axis=0, keepdims=True)
        count = jnp.sum(kept, axis=0, keepdims=True)
        weight = terms / jnp.where(count > 0.0, total, 1.0)
        weight_s[part, :] = weight
        low_s[part, :] = weight.astype(BF16)

    @pl.loop(0, wide // 128)
    def _(blk):
        mixed = dotf(low_s[:, block_of(blk * 128, 128)], pair_s[...], ((0,), (0,))).astype(BF16)
        count = 128 // groups
        out_s[pl.ds(blk * count, count)] = mixed.reshape(count, groups, 2 * width)

    def mix_copy(off):
        to = lax.rem(me + off, peers)
        return remote(out_s.at[to], in_s.at[off], mix_sems, off, "expert", to)

    each(1, peers, lambda off: mix_copy(off).start())
    in_s[0] = out_s[me]

    def ret_copy(off):
        to = lax.rem(me + peers - off, peers)
        return remote(done_s.at[off], ret_s.at[me], ret_sems, off, "expert", to)

    batch = 128 // groups

    def expert_part(chunk, slices, start):
        part = block_of(chunk * 128, 128)
        rows_in = in_s[pl.ds(chunk * batch, batch)].reshape(128, 2 * width)
        grad = rows_in[:, 0:width]
        mixed = rows_in[:, width : 2 * width]
        for at in slices:
            pre = dotf(mixed, win_s[at])
            sigma = 1.0 / (1.0 + jnp.exp(-pre))
            hidden = (pre * sigma).astype(BF16)
            grad_hidden = dotf(grad, wout_s[at], ((1,), (1,)))
            grad_pre = (grad_hidden * (sigma * (1.0 + pre * (1.0 - sigma)))).astype(BF16)
            hidden_s[at, part, :] = hidden
            gpre_s[at, part, :] = grad_pre
            returned = dotf(hidden, wout_s[at])
            grad_mixed = dotf(grad_pre, win_s[at], ((1,), (1,)))
            if start:
                acc_s[0, part, :] = returned
                acc_s[1, part, :] = grad_mixed
                start = False
            else:
                acc_s[0, part, :] += returned
                acc_s[1, part, :] += grad_mixed

    win_ring.wait_near()

    @pl.loop(0, peers // batch)
    def _(chunk):
        begin = chunk * batch
        each(jnp.maximum(begin, 1), begin + batch, lambda off: mix_copy(off).wait_recv())
        expert_part(chunk, (place,), True)

        @pl.when(chunk == 1)
        def _():
            wout_ring.forward()

    wout_ring.wait_near()

    @pl.loop(0, peers // batch)
    def _(chunk):
        expert_part(chunk, (left, right), False)

    win_ring.wait_far()
    wout_ring.wait_far()

    @pl.loop(0, peers // batch)
    def _(chunk):
        expert_part(chunk, (far,), False)
        part = block_of(chunk * 128, 128)
        begin = chunk * batch
        done = jnp.concatenate([acc_s[0, part, :], acc_s[1, part, :]], axis=1).astype(BF16)
        done_s[pl.ds(begin, batch)] = done.reshape(batch, groups, 2 * width)
        each(jnp.maximum(begin, 1), begin + batch, lambda off: ret_copy(off).start())

    ret_s[me] = done_s[0]

    dwin_ring = Scatter(dwin_s, via_win, land_win, dwin_sems, place)
    dwout_ring = Scatter(dwout_s, via_wout, land_wout, dwout_sems, place)

    def expert_grads(off):
        at = lax.rem(place + off, TENSOR)
        rows_in = in_s[...].reshape(wide, 2 * width)
        dwin_s[at] = dotf(rows_in[:, width : 2 * width], gpre_s[at], ((0,), (0,))).astype(BF16)
        dwout_s[at] = dotf(hidden_s[at], rows_in[:, 0:width], ((0,), (0,))).astype(BF16)

    @pl.loop(0, TENSOR)
    def _(turn):
        expert_grads(lax.rem(turn + 2, TENSOR))

        @pl.when(turn == 0)
        def _():
            dwin_ring.start_far()
            dwout_ring.start_far()

    dwin_ring.start_own()
    each(1, peers, lambda off: ret_copy(off).wait_recv())

    dgain_s[...] = jnp.zeros_like(dgain_s)
    from_wide = one_hot(iota((wide, experts), 0) // groups == iota((wide, experts), 1))

    @pl.loop(0, rows // step_rows)
    def _(step):
        part = block_of(step * step_rows, step_rows)
        came = ret_s[...].reshape(wide, 2 * width)
        low = low_s[part, :]
        weight = weight_s[part, :]
        back = dotf(low, came)
        kept_s[part, :] = (res_s[part, :] + back[:, 0:width]).astype(BF16)
        grad_weight = dotf(pair_s[part, :], came, ((1,), (1,)))
        inner = jnp.sum(weight * grad_weight, axis=0, keepdims=True)
        grad_logits = (weight * (grad_weight - inner)).astype(BF16)
        glog_s[part, :] = dotf(grad_logits, from_wide).astype(BF16)
        grad_mixer = back[:, width : 2 * width] + dotf(grad_logits, wide_router[...])
        scaled = scaled_s[part, :]
        dgain_s[...] += jnp.sum(grad_mixer * scaled, axis=0, keepdims=True)
        grad_scaled = grad_mixer * gain_two[...]
        centered = grad_scaled - jnp.mean(grad_scaled, axis=1, keepdims=True)
        along = jnp.mean(grad_scaled * scaled, axis=1, keepdims=True)
        grad_res = cot_s[part, :] + spread_s[part, 0:1] * (centered - scaled * along)
        res_s[part, :] = grad_res
        grad_att = grad_res.astype(BF16)
        gatt_s[part, :] = grad_att
        grad_ctx = dotf(grad_att, wo_full[...], ((1,), (1,))).astype(BF16)
        for at in range(TENSOR):
            gctx_s[at, part, :] = grad_ctx[:, at * hcols : (at + 1) * hcols]

    def back_copy(off):
        to = lax.rem(place + off, TENSOR)
        dst = gctx_all.at[block_of(place * rows, rows), :]
        return remote(gctx_s.at[to], dst, back_sems, off, "tensor", to)

    for off in (2, 1, 3):
        back_copy(off).start()
    out_store = pltpu.make_async_copy(kept_s, out_ref, store_sems.at[0])
    out_store.start()
    gctx_all[block_of(place * rows, rows), :] = gctx_s[place]

    each_rows = width // peers
    for at in range(TENSOR):
        grad_wo = dotf(ctx_all[at], gatt_s[...], ((0,), (0,))).astype(BF16)
        count = peers // TENSOR
        wop_s[at * count : (at + 1) * count, :, 0:width] = grad_wo.reshape(count, each_rows, width)
    grad_router = dotf(glog_s[...], pair_s[:, width : 2 * width], ((0,), (0,)))
    blocks = width // hcols
    small_rows = jnp.concatenate(
        [grad_router, dgain_s[...], jnp.zeros((width // blocks - experts - 1, width), F32)], axis=0
    ).astype(BF16)
    small_tall = jnp.concatenate(
        [small_rows[:, at * hcols : (at + 1) * hcols] for at in range(blocks)], axis=0
    )
    wop_s[:, :, width : width + hcols] = small_tall.reshape(peers, each_rows, hcols)

    def wop_copy(off):
        to = lax.rem(me + off, peers)
        return remote(wop_s.at[to], wop_in.at[off], wop_sems, off, "expert", to)

    each(1, peers, lambda off: wop_copy(off).start())
    wop_in[0] = wop_s[me]
    dwin_ring.add_far()
    dwout_ring.add_far()
    for off in (2, 1, 3):
        back_copy(off).wait_recv()
    dwin_ring.start_sums()
    dwout_ring.start_own()
    dwout_ring.start_sums()

    dq_acc[...] = jnp.zeros_like(dq_acc)
    ones = [pick_head(jnp.ones((8, hcols), F32), head) for head in range(heads)]

    @pl.loop(0, length // block)
    def _(blk):
        part = block_of(blk * block, block)
        product = gctx_all[part, :].astype(F32) * ctx_s[part, :].astype(F32)
        for head in range(heads):
            inner_s[pl.ds(8 * head, 8), part] = dotf(
                ones[head], product, ((1,), (1,)), lax.Precision.HIGHEST
            )

    def wopz_copy(off):
        to = lax.rem(place + off, TENSOR)
        return remote(wop_sum.at[place], wop_sum.at[place], wopz_sems, off, "tensor", to)

    def wopb_copy(off):
        to = lax.rem(me + off, peers)
        return remote(wop_all.at[me], wop_all.at[me], wopb_sems, off, "expert", to)

    @pl.loop(0, length // block)
    def _(kb):
        col0 = pl.multiple_of(kb * block, block)
        keys = k_s[pl.ds(col0, block), :]
        vals = v_s[pl.ds(col0, block), :]
        key_heads = [pick_head(keys, head) for head in range(heads)]
        dk_acc[...] = jnp.zeros_like(dk_acc)
        dv_acc[...] = jnp.zeros_like(dv_acc)

        def step(blk, masked):
            row0 = pl.multiple_of(blk * block, block)
            part = pl.ds(row0, block)
            q = q_s[part, :]
            grad = gctx_all[part, :]
            if masked:
                key_ids = iota((block, block), 0) + col0
                row_ids = iota((block, block), 1) + row0
                seen = (key_ids <= row_ids) | (key_ids < prefix)
            dq = dq_acc[part, :]
            dk = dk_acc[...]
            dv = dv_acc[...]
            for head in range(heads):
                q_head = pick_head(q, head)
                grad_head = pick_head(grad, head)
                scores = dotf(keys, q_head, ((1,), (1,)))
                if masked:
                    scores = jnp.where(seen, scores, NEG)
                soft = jnp.exp(scores - lse_s[pl.ds(8 * head, 1), part])
                grad_soft = dotf(vals, grad_head, ((1,), (1,)))
                grad_scores = (soft * (grad_soft - inner_s[pl.ds(8 * head, 1), part])).astype(BF16)
                dv += dotf(soft.astype(BF16), grad_head)
                dk += dotf(grad_scores, q_head)
                dq += dotf(grad_scores, key_heads[head], ((0,), (0,)))
            dq_acc[part, :] = dq
            dk_acc[...] = dk
            dv_acc[...] = dv

        first = jnp.where(kb < PREFIX_MOST // block, 0, kb)
        each(first, kb + 1, functools.partial(step, masked=True))
        each(kb + 1, length // block, functools.partial(step, masked=False))
        grads_s[pl.ds(col0, block), hcols : 2 * hcols] = dk_acc[...].astype(BF16)
        grads_s[pl.ds(col0, block), 2 * hcols : 3 * hcols] = dv_acc[...].astype(BF16)

        @pl.when(kb == 0)
        def _():
            each(1, peers, lambda off: wop_copy(off).wait_recv())
            total = jnp.zeros(wop_sum.shape[1:], F32)
            total = lax.fori_loop(0, peers, lambda off, acc: acc + wop_in[off].astype(F32), total)
            wop_sum[place] = total.astype(BF16)
            for off in (2, 1, 3):
                wopz_copy(off).start()

        @pl.when(kb == 1)
        def _():
            for off in (2, 1, 3):
                wopz_copy(off).wait_recv()
            total = jnp.zeros(wop_sum.shape[1:], F32)
            for at in range(TENSOR):
                total = total + wop_sum[at].astype(F32)
            wop_all[me] = total.astype(BF16)
            each(1, peers, lambda off: wopb_copy(off).start())

    grads_s[:, 0:hcols] = (dq_acc[...] * SCORE_SCALE).astype(BF16)

    def partial_rows(owner, part):
        start = owner * rows + part * half
        return dotf(grads_s[block_of(start, half), :], w_s[...], ((1,), (1,)))

    row_ring = Scatter(rows_s, via_rows, land_rows, row_sems, place)
    low, high = row_ring.low, row_ring.high
    rows_s[far, low] = partial_rows(far, 0).astype(BF16)
    rows_s[far, high] = partial_rows(far, 1).astype(BF16)
    row_ring.start_far()
    rows_s[right, high] = partial_rows(right, 1).astype(BF16)
    rows_s[left, low] = partial_rows(left, 0).astype(BF16)
    row_ring.start_own()

    @pl.loop(0, 3)
    def _(at):
        cols = block_of(at * hcols, hcols)
        grad = dotf(seq_s[...], grads_s[:, cols], ((0,), (0,)))
        piece_s[at] = grad.astype(BF16).reshape(peers, each_rows, hcols)

    def piece_copy(off):
        to = lax.rem(me + off, peers)
        return remote(piece_s.at[:, to], piece_in.at[off], piece_sems, off, "expert", to)

    each(1, peers, lambda off: piece_copy(off).start())
    for at in range(3):
        piece_in[0, at] = piece_s[at, me]
    rows_s[right, low] = partial_rows(right, 0).astype(BF16)
    rows_s[left, high] = partial_rows(left, 1).astype(BF16)
    row_ring.add_far()
    row_ring.start_sums()
    mine_s[low, :] = partial_rows(place, 0)
    mine_s[high, :] = partial_rows(place, 1)

    each(1, peers, lambda off: piece_copy(off).wait_recv())
    total = jnp.zeros(sum_s.shape, F32)
    total = lax.fori_loop(0, peers, lambda off, acc: acc + piece_in[off].astype(F32), total)
    sum_s[...] = total.astype(BF16)

    def sum_copy(off):
        to = lax.rem(me + off, peers)
        return remote(sum_s, sum_all.at[:, me], sum_sems, off, "expert", to)

    each(1, peers, lambda off: sum_copy(off).start())
    for at in range(3):
        sum_all[at, me] = sum_s[at]

    dwin_ring.wait()
    dwout_ring.wait()
    for at, (ring, part_s) in enumerate(((dwin_ring, dwin_s), (dwout_ring, dwout_s))):
        for part in (low, high):
            acc_s[at, part, :] = part_s[place, part].astype(F32) + ring.landed(part)
    win_store = pltpu.make_async_copy(acc_s.at[0], dwin_ref, store_sems.at[1])
    wout_store = pltpu.make_async_copy(acc_s.at[1], dwout_ref, store_sems.at[2])
    win_store.start()
    wout_store.start()
    each(1, peers, lambda off: wopb_copy(off).wait_recv())
    count = peers // TENSOR
    go_ref[...] = wop_all[pl.ds(place * count, count), :, 0:width].reshape(hcols, width).astype(F32)
    small = wop_all[:, :, width : width + hcols].reshape(width, hcols)
    tall = width // blocks
    kept_rows = small_ref.shape[0]
    small_ref[...] = jnp.concatenate(
        [small[at * tall : at * tall + kept_rows] for at in range(blocks)], axis=1
    ).astype(F32)

    row_ring.wait()
    for part in (low, high):
        grad_normed = mine_s[part, :] + row_ring.landed(part)
        scaled, spread = norm_parts(tok_s[place, part].astype(F32))
        grad_scaled = grad_normed * gain_one[...]
        centered = grad_scaled - jnp.mean(grad_scaled, axis=1, keepdims=True)
        along = jnp.mean(grad_scaled * scaled, axis=1, keepdims=True)
        scaled_s[part, :] = res_s[part, :] + spread * (centered - scaled * along)
    tok_store = pltpu.make_async_copy(scaled_s, gtok_ref, store_sems.at[3])
    tok_store.start()

    each(1, peers, lambda off: sum_copy(off).wait_recv())
    dfirst = jnp.zeros((8, width), F32)
    for at, grad_ref in enumerate((gq_ref, gk_ref, gv_ref)):
        grad = sum_all[at].reshape(width, hcols).astype(F32)
        grad_ref[...] = grad
        product = grad * w_s[:, at * hcols : (at + 1) * hcols].astype(F32)
        dfirst = dfirst + dotf(
            jnp.ones((8, hcols), F32), product, ((1,), (1,)), lax.Precision.HIGHEST
        )
    first_s[place] = dfirst / gain_one[...]

    def first_copy(off):
        to = lax.rem(place + off, TENSOR)
        return remote(first_s.at[place], first_s.at[place], first_sems, off, "tensor", to)

    for off in (2, 1, 3):
        first_copy(off).start()

    for ring in (tok_ring, win_ring, wout_ring, wo_ring, dwin_ring, dwout_ring, row_ring):
        ring.drain()
    for off in (2, 1, 3):
        ctx_copy(off).wait_send()
        back_copy(off).wait_send()
        wopz_copy(off).wait_send()

    def drain(off):
        for copy in (mix_copy, ret_copy, wop_copy, wopb_copy, piece_copy, sum_copy):
            copy(off).wait_send()

    each(1, peers, drain)
    for off in (2, 1, 3):
        first_copy(off).wait_recv()
    dfirst_ref[...] = first_s[0] + first_s[1] + first_s[2] + first_s[3]
    for off in (2, 1, 3):
        first_copy(off).wait_send()
    for store in (out_store, win_store, wout_store, tok_store):
        store.wait()


def layer(prefix, tokens, gain_one, gain_two, wq, wk, wv, wo, router, win, wout, cot, routes, prio):
    rows, width = tokens.shape
    experts = router.shape[0]
    hcols = wq.shape[1]
    fcols = win.shape[1]
    groups = rows // GROUP
    wide = experts * groups
    length = TENSOR * rows
    heads = hcols // HEAD_DIM
    peers = experts
    each_rows = width // peers
    capacity = (5 * GROUP * TOP + 4 * experts - 1) // (4 * experts)

    def dev(shape, kind):
        return jax.ShapeDtypeStruct(shape, kind)

    def low(*shape):
        return pltpu.VMEM(shape, BF16)

    def full(*shape):
        return pltpu.VMEM(shape, F32)

    def sems(count):
        return pltpu.SemaphoreType.DMA((2, count))

    small_rows = (experts + 1 + 15) // 16 * 16
    return pl.pallas_call(
        functools.partial(layer_kernel, experts=experts, capacity=float(capacity)),
        out_shape=(
            dev((rows, width), BF16),
            dev((rows, width), F32),
            dev(wq.shape, F32),
            dev(wq.shape, F32),
            dev(wq.shape, F32),
            dev(wo.shape, F32),
            dev((small_rows, width), F32),
            dev((8, width), F32),
            dev(win.shape, F32),
            dev(wout.shape, F32),
        ),
        in_specs=[SM] + [HB] * 13,
        out_specs=(HB,) * 2 + (VM,) * 6 + (HB,) * 2,
        scratch_shapes=[
            low(TENSOR, rows, width),
            full(1, width),
            full(1, width),
            low(width, 3 * hcols),
            low(TENSOR, hcols, width),
            low(experts, width),
            low(TENSOR, width, fcols),
            low(TENSOR, fcols, width),
            full(rows, width),
            pltpu.VMEM(routes.shape, jnp.int32),
            pltpu.VMEM(prio.shape, jnp.int32),
            low(length, width),
            low(length, hcols),
            low(length, hcols),
            low(length, hcols),
            low(rows, wide),
            low(length, hcols),
            full(8 * heads, length),
            low(TENSOR, rows, hcols),
            low(wide, width),
            full(rows, width),
            full(rows, width),
            full(rows, 128),
            low(rows, 2 * width),
            full(rows, wide),
            low(rows, wide),
            low(experts, groups, 2 * width),
            low(experts, groups, 2 * width),
            low(experts, groups, 2 * width),
            low(experts, groups, 2 * width),
            full(2, wide, width),
            low(TENSOR, wide, fcols),
            low(TENSOR, wide, fcols),
            low(TENSOR, rows, hcols),
            low(length, hcols),
            low(rows, width),
            low(rows, experts),
            full(1, width),
            low(TENSOR, width, fcols),
            low(TENSOR, fcols, width),
            low(width, fcols),
            low(fcols, width),
            low(2, width, fcols),
            low(2, fcols, width),
            low(peers, each_rows, width + hcols),
            low(peers, each_rows, width + hcols),
            low(TENSOR, each_rows, width + hcols),
            low(peers, each_rows, width + hcols),
            full(length, hcols),
            full(rows, hcols),
            full(rows, hcols),
            full(8 * heads, length),
            low(length, 3 * hcols),
            low(TENSOR, rows, width),
            low(rows, width),
            low(2, rows, width),
            full(rows, width),
            low(3, peers, each_rows, hcols),
            low(peers, 3, each_rows, hcols),
            low(3, each_rows, hcols),
            low(3, peers, each_rows, hcols),
            full(TENSOR, 8, width),
            pltpu.SemaphoreType.DMA((13,)),
            pltpu.SemaphoreType.DMA((4,)),
            sems(6),
            sems(6),
            sems(6),
            sems(6),
            sems(TENSOR),
            sems(peers),
            sems(peers),
            sems(TENSOR),
            sems(6),
            sems(6),
            sems(peers),
            sems(TENSOR),
            sems(peers),
            sems(6),
            sems(peers),
            sems(peers),
            sems(TENSOR),
        ],
        compiler_params=pltpu.CompilerParams(
            collective_id=0, has_side_effects=True, vmem_limit_bytes=VMEM_BYTES
        ),
        name="layer",
    )(prefix, tokens, gain_one, gain_two, wq, wk, wv, wo, router, win, wout, cot, routes, prio)


def body(
    tokens,
    first_gain,
    second_gain,
    query_weight,
    key_weight,
    value_weight,
    output_weight,
    router_weight,
    expert_in,
    expert_out,
    cotangent,
    routes,
    priority,
    prefix_len,
):
    width = tokens.shape[1]
    experts = router_weight.shape[1]
    out, gtok, gq, gk, gv, go, small, dfirst, dwin, dwout = layer(
        prefix_len,
        tokens,
        first_gain.reshape(1, width),
        second_gain.reshape(1, width),
        query_weight,
        key_weight,
        value_weight,
        output_weight,
        router_weight.T,
        expert_in[0],
        expert_out[0],
        cotangent,
        routes.T,
        priority,
    )
    return (
        out,
        gtok,
        dfirst[0],
        small[experts],
        gq,
        gk,
        gv,
        go,
        small[:experts].T,
        dwin[None],
        dwout[None],
    )


def solution(mesh):
    in_specs = (
        P(("expert", "tensor"), None),
        P(),
        P(),
        P(None, "tensor"),
        P(None, "tensor"),
        P(None, "tensor"),
        P("tensor", None),
        P(),
        P("expert", None, "tensor"),
        P("expert", "tensor", None),
        P(("expert", "tensor"), None),
        P(("expert", "tensor"), None),
        P(("expert", "tensor"), None),
        P("expert"),
    )
    out_specs = (
        P(("expert", "tensor"), None),
        P(("expert", "tensor"), None),
        P(),
        P(),
        P(None, "tensor"),
        P(None, "tensor"),
        P(None, "tensor"),
        P("tensor", None),
        P(),
        P("expert", None, "tensor"),
        P("expert", "tensor", None),
    )
    return jax.shard_map(body, mesh=mesh, in_specs=in_specs, out_specs=out_specs, check_vma=False)
```

time: 788 us -> 181 us (0.23)
  waiting for transfers between devices: 381 us -> 0 us
  Pallas kernels: 0 us -> 164 us
  matrix products: 132 us -> 0 us
  blocking collectives: 129 us -> 0 us
  other arithmetic: 62.2 us -> 0 us
  loops' own time: 16.4 us -> 0 us
  local copies, waits for them, and re-layouts: 27.2 us -> 12.8 us
  between operations: 15.3 us -> 1.33 us
  starting transfers between devices: 13.6 us -> 0 us
    pallas_call x0 -> x1, Pallas kernels: none -> 164 us  [layer(): pl.pallas_call(functools.partial(layer_kernel, experts=experts, capacity=...]
    psum x2 -> x0, waiting for transfers between devices: 163 us -> none  [the longest x1 88.3 us: body(): lax.psum(query_part.astype(jnp.bfloat16), 'expert').astype(jnp.float32)]
    dot_general x56 -> x0, matrix products: 132 us -> none  [the longest x8 21.8 us: block_scores(): jnp.einsum('qhd,khd->hqk', query_blk, key_rows, preferred_element_type=jn...]
    all_gather x4 -> x0, waiting for transfers between devices: 114 us -> none  [the longest x1 33.8 us: body(): lax.all_gather(normed_one.astype(jnp.bfloat16), 'tensor', axis=0, tiled=T...]
    reduce_scatter x4 -> x0, waiting for transfers between devices: 79.3 us -> none  [the longest x1 29.8 us: body(): lax.psum_scatter(jnp.dot(context, output_weight, preferred_element_type=j...]
    psum x1 -> x0, blocking collectives: 64.7 us -> none  [body(): lax.psum((first_part, second_part, router_part), ('expert', 'tensor'))]
    all_to_all x2 -> x0, blocking collectives: 64.6 us -> none  [the longest x1 32.6 us: body(): lax.all_to_all(to_homes(grad_part, expert_size).astype(jnp.bfloat16), 'ex...]
    all_to_all x2 -> x0, waiting for transfers between devices: 25.4 us -> none  [the longest x1 22.4 us: body(): lax.all_to_all(sequence_grad, 'expert', split_axis=0, concat_axis=1, tile...]
  transfers between devices with their start and end apart: 12 -> 0, of which waited for: 11 -> 0; matrix products, arithmetic and copies ran while one was open for 6% -> 0% of each run, Pallas kernels for 0% -> 0%
where the time goes in v2:
time: 181 us; the launch traced here: 178 us
  Pallas kernels  164 us (91%)
  local copies, waits for them, and re-layouts  12.8 us (7%)
    pallas_call x1, Pallas kernels, layer(): pl.pallas_call(functools.partial(layer_kernel, experts=experts, capacity=...  164 us
    unnamed x22, local copies, waits for them, and re-layouts  8.67 us

profile of v2, /device:TPU:1, one launch (start us, length us, event | category | flops | bytes accessed | tf_op | source)
XLA Modules:
  0.0 178.0 jit_solution(14159530587134707427)
XLA Ops:
  1.3 163.8 %layer.1 = (bf16[512,512]{1,0:T(8,128)(2,1)}, f32[512,512]{1,0:T(8,128)}, f32[512,128]{1,0:T(8,128)}, f32[512,128]{1,0:T(8,128)}, f32[512,128]{1,0:T(8,128)}, /*...) custom-call(s32[1]{0:T(128)S(6)} %copy.33.prefix_ref, ...), custom_call_target="tpu_custom_call" | custom-call | tf_op jit(solution)/shard_map/layer/pallas_call | solution.py:872
  165.1 0.0 copy-start.2
  165.1 1.4 slice.9
  166.5 1.3 slice.10
  167.8 1.5 slice_bitcast_fusion
  169.3 1.9 %copy.34 = bf16[512,512]{1,0:T(8,128)(2,1)} copy(bf16[512,512]{1,0:T(8,128)(2,1)} %get-tuple-element.42) | data formatting | bytes 1048576
  171.1 0.0 copy-done.2
  171.1 0.0 copy-start.6
  171.2 0.0 copy-start.5
  171.2 0.0 copy-start.4
  171.2 1.0 copy.35
  172.1 0.1 copy-done.6
  172.2 0.0 copy-start.1
  172.2 0.7 copy.36
  172.9 0.0 copy-done.5
  172.9 0.7 copy.37
  173.6 0.0 copy-done.4
  173.6 0.0 copy-start.3
  173.6 0.7 copy.38
  174.3 0.3 copy-done.3
  174.7 0.7 copy.39
  175.4 0.0 copy-done.1
  175.4 0.0 copy-start
  175.4 1.0 copy.40
  176.4 0.6 copy-done
  177.0 1.0 copy.41
Async XLA Ops:
  165.1 6.0 %copy-start.2 = (f32[512,512]{1,0:T(8,128)S(1)}, f32[512,512]{1,0:T(8,128)}, u32[]{:S(2)}) copy-start(f32[512,512]{1,0:T(8,128)} %get-tuple-element.43) | copy-start | bytes 3145732
  171.1 1.1 copy-start.6
  171.2 1.8 copy-start.5
  171.2 2.5 %copy-start.4 = (f32[512,128]{1,0:T(8,128)S(1)}, f32[512,128]{1,0:T(8,128)}, u32[]{:S(2)}) copy-start(f32[512,128]{1,0:T(8,128)} %get-tuple-element.48) | copy-start | bytes 786436
  172.2 3.2 %copy-start.1 = (f32[512,512]{1,0:T(8,128)S(1)}, f32[512,512]{1,0:T(8,128)}, u32[]{:S(2)}) copy-start(f32[512,512]{1,0:T(8,128)} %get-tuple-element.29) | copy-start | bytes 3145732
  173.6 1.0 copy-start.3
  175.4 1.6 copy-start

commit v3 on v2

--- a/solution.py
+++ b/solution.py
@@ -14,6 +14,7 @@
 NEG = -1e30
 SCORE_SCALE = HEAD_DIM**-0.5
 PREFIX_MOST = 1024
+ROW = 8
 MESH = pl.DeviceIdType.MESH
 VM = pl.BlockSpec(memory_space=pltpu.VMEM)
 SM = pl.BlockSpec(memory_space=pltpu.SMEM)
@@ -55,17 +56,32 @@
     )
 
 
-def greet(axis, size):
+def fan(src, dst, sems, to, lane=0):
+    return pltpu.make_async_remote_copy(
+        src_ref=src,
+        dst_ref=dst,
+        send_sem=sems.at[0],
+        recv_sem=sems.at[1 + lane],
+        device_id={"expert": to},
+        device_id_type=MESH,
+    )
+
+
+def greet(peers):
     barrier = pltpu.get_barrier_semaphore()
-    me = lax.axis_index(axis)
-
-    def one(off, _):
-        pl.semaphore_signal(
-            barrier, inc=1, device_id={axis: lax.rem(me + off, size)}, device_id_type=MESH
-        )
-        return 0
-
-    lax.fori_loop(1, size, one, 0)
+    place = lax.axis_index("tensor")
+    me = lax.axis_index("expert")
+
+    def signal(axis, to):
+        pl.semaphore_signal(barrier, inc=1, device_id={axis: to}, device_id_type=MESH)
+
+    for off in range(1, TENSOR):
+        signal("tensor", lax.rem(place + off, TENSOR))
+    for off in range(1, ROW):
+        signal("expert", me // ROW * ROW + lax.rem(me + off, ROW))
+    for off in range(ROW, peers, ROW):
+        signal("expert", lax.rem(me + off, peers))
+    return TENSOR - 1 + ROW - 1 + peers // ROW - 1
 
 
 def each(first, last, act):
@@ -105,8 +121,8 @@
         block = self.buf.at[owner, part]
         return remote(block, block, self.sems, slot, "tensor", to)
 
-    def start(self):
-        for slot in range(4):
+    def start(self, slots=range(4)):
+        for slot in slots:
             self.copy(slot).start()
 
     def forward(self):
@@ -202,7 +218,8 @@
     gk_ref,
     gv_ref,
     go_ref,
-    small_ref,
+    router_ref,
+    dsecond_ref,
     dfirst_ref,
     dwin_ref,
     dwout_ref,
@@ -217,9 +234,10 @@
     cot_s,
     routes_s,
     prio_s,
-    seq_s,
+    seqt_s,
     q_s,
     k_s,
+    kt_s,
     v_s,
     kept_s,
     ctx_s,
@@ -254,10 +272,8 @@
     wop_in,
     wop_sum,
     wop_all,
-    dq_acc,
     dk_acc,
     dv_acc,
-    inner_s,
     grads_s,
     rows_s,
     via_rows,
@@ -265,11 +281,12 @@
     mine_s,
     piece_s,
     piece_in,
-    sum_s,
     sum_all,
     first_s,
+    gain_all,
     local_sems,
     store_sems,
+    plane_sem,
     tok_sems,
     win_sems,
     wout_sems,
@@ -287,6 +304,7 @@
     piece_sems,
     sum_sems,
     first_sems,
+    gain_sems,
     *,
     experts,
     capacity,
@@ -301,9 +319,7 @@
     groups = rows // GROUP
     wide = experts * groups
     peers = experts
-    barrier = pltpu.get_barrier_semaphore()
-    greet("tensor", TENSOR)
-    greet("expert", peers)
+    greeted = greet(peers)
 
     loads = [
         (tok_hbm, tok_s.at[place]),
@@ -326,34 +342,42 @@
     for load in loads:
         load.start()
 
+    def all_of(buf, sems):
+        most = buf.at[pl.ds(1, peers - 1)]
+        return fan(most, most, sems, lax.rem(me + 1, peers))
+
+    batch = 128 // groups
+
     tok_ring = Gather(tok_s, tok_sems, place)
     win_ring = Gather(win_s, win_sems, place)
     wout_ring = Gather(wout_s, wout_sems, place)
     wo_ring = Gather(wo_s, wo_sems, place)
     loads[0].wait()
-    pl.semaphore_wait(barrier, TENSOR - 1 + peers - 1)
+    pl.semaphore_wait(pltpu.get_barrier_semaphore(), greeted)
     tok_ring.start()
+    for off in range(ROW, peers, ROW):
+        to = lax.rem(me + off, peers)
+        pl.semaphore_signal(plane_sem, inc=1, device_id={"expert": to}, device_id_type=MESH)
     for load in loads[1:5]:
         load.wait()
 
     half = rows // 2
 
-    def project(owner, part):
-        @pl.loop(0, 2)
+    def project(owner):
+        @pl.loop(0, rows // 128)
         def _(at):
-            count = half // 2
-            start = part * half + at * count
-            scaled, _ = norm_parts(tok_s[owner, block_of(start, count)].astype(F32))
+            start = at * 128
+            scaled, _ = norm_parts(tok_s[owner, block_of(start, 128)].astype(F32))
             normed = (scaled * gain_one[...]).astype(BF16)
-            to = block_of(owner * rows + start, count)
-            seq_s[to, :] = normed
+            to = block_of(owner * rows + start, 128)
+            seqt_s[:, to] = jnp.transpose(normed)
             out = dotf(normed, w_s[...]).astype(BF16)
             q_s[to, :] = out[:, 0:hcols] * SCORE_SCALE
             k_s[to, :] = out[:, hcols : 2 * hcols]
+            kt_s[:, to] = jnp.transpose(out[:, hcols : 2 * hcols])
             v_s[to, :] = out[:, 2 * hcols : 3 * hcols]
 
-    project(place, 0)
-    project(place, 1)
+    project(place)
     tok_ring.forward()
 
     loads[5].wait()
@@ -377,74 +401,81 @@
     kept_s[...] = jnp.where(rank < capacity, member, 0.0).astype(BF16)
 
     tok_ring.copy(2).wait_recv()
-    project(left, 0)
-    project(left, 1)
+    project(left)
     tok_ring.copy(3).wait_recv()
-    project(right, 0)
-    project(right, 1)
+    project(right)
     for load in loads[7:10]:
         load.wait()
-    tok_ring.copy(4).wait_recv()
-    project(far, 0)
-    tok_ring.copy(5).wait_recv()
+    tok_ring.wait_far()
     wo_ring.start()
-    win_ring.start()
-    project(far, 1)
+    win_ring.start((0, 1))
+    project(far)
 
     prefix = prefix_ref[0]
     block = rows
 
-    @pl.loop(0, length // block)
-    def _(blk):
-        row0 = pl.multiple_of(blk * block, block)
-        q = q_s[pl.ds(row0, block), :]
-        q_heads = [pick_head(q, head) for head in range(heads)]
-
-        def step(kb, carry, masked):
-            col0 = pl.multiple_of(kb * block, block)
-            keys = k_s[pl.ds(col0, block), :]
-            vals = v_s[pl.ds(col0, block), :]
-            out = []
-            if masked:
-                row_ids = iota((block, block), 0) + row0
-                col_ids = iota((block, block), 1) + col0
-                seen = (col_ids <= row_ids) | (col_ids < prefix)
-            for head in range(heads):
-                peak, acc = carry[2 * head : 2 * head + 2]
-                scores = dotf(q_heads[head], keys, ((1,), (1,)))
-                if masked:
-                    scores = jnp.where(seen, scores, NEG)
-                new_peak = jnp.maximum(peak, jnp.max(scores, axis=1, keepdims=True))
-                soft = jnp.exp(scores - new_peak).astype(BF16)
-                acc = jnp.exp(peak - new_peak) * acc + dotf(soft, pick_head(vals, head, 1.0))
-                out += [new_peak, acc]
-            return tuple(out)
-
-        init = (jnp.full((block, 1), NEG, F32), jnp.zeros((block, hcols), F32)) * heads
-        carry = lax.fori_loop(0, blk, functools.partial(step, masked=False), init)
-        seen_blocks = jnp.maximum(blk + 1, PREFIX_MOST // block)
-        carry = lax.fori_loop(blk, seen_blocks, functools.partial(step, masked=True), carry)
+    def hidden_keys(scores, row0, col0, row_axis):
+        if isinstance(row0, int) and col0 + block - 1 <= row0:
+            return scores
+        row_ids = iota((block, block), row_axis) + row0
+        col_ids = iota((block, block), 1 - row_axis) + col0
+        seen = col_ids <= row_ids
+        if col0 < PREFIX_MOST:
+            seen = seen | (col_ids < prefix)
+        return jnp.where(seen, scores, NEG)
+
+    def ctx_copy(off):
+        to = lax.rem(place + off, TENSOR)
+        src = ctx_s.at[block_of(to * rows, rows), :]
+        return remote(src, ctx_all.at[place], ctx_sems, off, "tensor", to)
+
+    def attend(row0, seen_rows):
+        part_rows = pl.ds(row0, block)
+        q = q_s[part_rows, :]
+        starts = range(0, seen_rows, block)
         merged = jnp.zeros((block, hcols), F32)
         for head in range(heads):
-            peak, acc = carry[2 * head : 2 * head + 2]
+            q_head = pick_head(q, head)
+            scores = []
+            for col0 in starts:
+                part = dotf(q_head, k_s[col0 : col0 + block, :], ((1,), (1,)))
+                scores.append(hidden_keys(part, row0, col0, 0))
+            peak = functools.reduce(
+                jnp.maximum, [jnp.max(part, axis=1, keepdims=True) for part in scores]
+            )
+            acc = jnp.zeros((block, hcols), F32)
+            for part, col0 in zip(scores, starts):
+                soft = jnp.exp(part - peak).astype(BF16)
+                acc = acc + dotf(soft, pick_head(v_s[col0 : col0 + block, :], head, 1.0))
             lane = HEAD_DIM if head == 0 else 0
             total = acc[:, lane : lane + 1]
             merged = merged + pick_head(acc * (1.0 / total), head)
             lse = jnp.broadcast_to(peak + jnp.log(total), (block, 128))
-            lse_s[pl.ds(8 * head, 8), pl.ds(row0, block)] = jnp.transpose(lse)[:8]
-        ctx_s[pl.ds(row0, block), :] = merged.astype(BF16)
-
-        @pl.when(blk == 2)
+            lse_s[8 * head : 8 * head + 8, part_rows] = jnp.transpose(lse)[:8]
+        ctx_s[part_rows, :] = merged.astype(BF16)
+
+    def by_length(act, blk):
+        short = PREFIX_MOST // block
+        pl.when(blk < short)(lambda: act(pl.multiple_of(blk * block, block), PREFIX_MOST))
+        for at in range(short, TENSOR):
+            pl.when(blk == at)(functools.partial(act, at * block, (at + 1) * block))
+
+    @pl.loop(0, TENSOR)
+    def _(turn):
+        blk = lax.rem(place + 1 + turn, TENSOR)
+        by_length(attend, blk)
+
+        @pl.when(turn < TENSOR - 1)
+        def _():
+            ctx_copy(turn + 1).start()
+
+        @pl.when(turn == 1)
         def _():
             wo_ring.forward()
 
-    def ctx_copy(off):
-        to = lax.rem(place + off, TENSOR)
-        src = ctx_s.at[block_of(to * rows, rows), :]
-        return remote(src, ctx_all.at[place], ctx_sems, off, "tensor", to)
-
-    for off in (2, 1, 3):
-        ctx_copy(off).start()
+    win_ring.start((2, 3))
+    win_ring.forward()
+    wout_ring.start()
     ctx_all[place] = ctx_s[block_of(place * rows, rows), :]
     for load in loads[10:]:
         load.wait()
@@ -455,8 +486,6 @@
     wo_full = wo_s.reshape(TENSOR * hcols, width)
     for off in (2, 1, 3):
         ctx_copy(off).wait_recv()
-    wout_ring.start()
-    win_ring.forward()
 
     step_rows = 128
 
@@ -488,16 +517,15 @@
 
     def mix_copy(off):
         to = lax.rem(me + off, peers)
-        return remote(out_s.at[to], in_s.at[off], mix_sems, off, "expert", to)
-
+        return fan(out_s.at[to], in_s.at[off], mix_sems, to, off // batch)
+
+    pl.semaphore_wait(plane_sem, peers // ROW - 1)
     each(1, peers, lambda off: mix_copy(off).start())
     in_s[0] = out_s[me]
 
     def ret_copy(off):
         to = lax.rem(me + peers - off, peers)
-        return remote(done_s.at[off], ret_s.at[me], ret_sems, off, "expert", to)
-
-    batch = 128 // groups
+        return fan(done_s.at[off], ret_s.at[me], ret_sems, to)
 
     def expert_part(chunk, slices, start):
         part = block_of(chunk * 128, 128)
@@ -505,6 +533,7 @@
         grad = rows_in[:, 0:width]
         mixed = rows_in[:, width : 2 * width]
         for at in slices:
+            at = lax.rem(place + at, TENSOR)
             pre = dotf(mixed, win_s[at])
             sigma = 1.0 / (1.0 + jnp.exp(-pre))
             hidden = (pre * sigma).astype(BF16)
@@ -526,26 +555,35 @@
 
     @pl.loop(0, peers // batch)
     def _(chunk):
-        begin = chunk * batch
-        each(jnp.maximum(begin, 1), begin + batch, lambda off: mix_copy(off).wait_recv())
-        expert_part(chunk, (place,), True)
-
-        @pl.when(chunk == 1)
+
+        @pl.when(chunk == 0)
+        def _():
+            came = in_s.at[pl.ds(1, batch - 1)]
+            fan(came, came, mix_sems, lax.rem(me + 1, peers), 0).wait_recv()
+
+        @pl.when(chunk > 0)
+        def _():
+            came = in_s.at[pl.ds(chunk * batch, batch)]
+            fan(came, came, mix_sems, lax.rem(me + 1, peers), chunk).wait_recv()
+
+        expert_part(chunk, (0,), True)
+
+        @pl.when(chunk == 2)
         def _():
             wout_ring.forward()
 
     wout_ring.wait_near()
 
+    @pl.loop(0, 2 * peers // batch)
+    def _(turn):
+        expert_part(turn // 2, (3 - 2 * lax.rem(turn, 2),), False)
+
+    win_ring.wait_far()
+    wout_ring.wait_far()
+
     @pl.loop(0, peers // batch)
     def _(chunk):
-        expert_part(chunk, (left, right), False)
-
-    win_ring.wait_far()
-    wout_ring.wait_far()
-
-    @pl.loop(0, peers // batch)
-    def _(chunk):
-        expert_part(chunk, (far,), False)
+        expert_part(chunk, (2,), False)
         part = block_of(chunk * 128, 128)
         begin = chunk * batch
         done = jnp.concatenate([acc_s[0, part, :], acc_s[1, part, :]], axis=1).astype(BF16)
@@ -573,7 +611,7 @@
             dwout_ring.start_far()
 
     dwin_ring.start_own()
-    each(1, peers, lambda off: ret_copy(off).wait_recv())
+    all_of(ret_s, ret_sems).wait_recv()
 
     dgain_s[...] = jnp.zeros_like(dgain_s)
     from_wide = one_hot(iota((wide, experts), 0) // groups == iota((wide, experts), 1))
@@ -632,29 +670,16 @@
 
     def wop_copy(off):
         to = lax.rem(me + off, peers)
-        return remote(wop_s.at[to], wop_in.at[off], wop_sems, off, "expert", to)
+        return fan(wop_s.at[to], wop_in.at[off], wop_sems, to)
 
     each(1, peers, lambda off: wop_copy(off).start())
     wop_in[0] = wop_s[me]
     dwin_ring.add_far()
     dwout_ring.add_far()
-    for off in (2, 1, 3):
-        back_copy(off).wait_recv()
-    dwin_ring.start_sums()
-    dwout_ring.start_own()
-    dwout_ring.start_sums()
-
-    dq_acc[...] = jnp.zeros_like(dq_acc)
+
+    dk_acc[...] = jnp.zeros_like(dk_acc)
+    dv_acc[...] = jnp.zeros_like(dv_acc)
     ones = [pick_head(jnp.ones((8, hcols), F32), head) for head in range(heads)]
-
-    @pl.loop(0, length // block)
-    def _(blk):
-        part = block_of(blk * block, block)
-        product = gctx_all[part, :].astype(F32) * ctx_s[part, :].astype(F32)
-        for head in range(heads):
-            inner_s[pl.ds(8 * head, 8), part] = dotf(
-                ones[head], product, ((1,), (1,)), lax.Precision.HIGHEST
-            )
 
     def wopz_copy(off):
         to = lax.rem(place + off, TENSOR)
@@ -662,61 +687,56 @@
 
     def wopb_copy(off):
         to = lax.rem(me + off, peers)
-        return remote(wop_all.at[me], wop_all.at[me], wopb_sems, off, "expert", to)
-
-    @pl.loop(0, length // block)
-    def _(kb):
-        col0 = pl.multiple_of(kb * block, block)
-        keys = k_s[pl.ds(col0, block), :]
-        vals = v_s[pl.ds(col0, block), :]
-        key_heads = [pick_head(keys, head) for head in range(heads)]
-        dk_acc[...] = jnp.zeros_like(dk_acc)
-        dv_acc[...] = jnp.zeros_like(dv_acc)
-
-        def step(blk, masked):
-            row0 = pl.multiple_of(blk * block, block)
-            part = pl.ds(row0, block)
-            q = q_s[part, :]
-            grad = gctx_all[part, :]
-            if masked:
-                key_ids = iota((block, block), 0) + col0
-                row_ids = iota((block, block), 1) + row0
-                seen = (key_ids <= row_ids) | (key_ids < prefix)
-            dq = dq_acc[part, :]
-            dk = dk_acc[...]
-            dv = dv_acc[...]
-            for head in range(heads):
-                q_head = pick_head(q, head)
-                grad_head = pick_head(grad, head)
-                scores = dotf(keys, q_head, ((1,), (1,)))
-                if masked:
-                    scores = jnp.where(seen, scores, NEG)
-                soft = jnp.exp(scores - lse_s[pl.ds(8 * head, 1), part])
-                grad_soft = dotf(vals, grad_head, ((1,), (1,)))
-                grad_scores = (soft * (grad_soft - inner_s[pl.ds(8 * head, 1), part])).astype(BF16)
-                dv += dotf(soft.astype(BF16), grad_head)
-                dk += dotf(grad_scores, q_head)
-                dq += dotf(grad_scores, key_heads[head], ((0,), (0,)))
-            dq_acc[part, :] = dq
-            dk_acc[...] = dk
-            dv_acc[...] = dv
-
-        first = jnp.where(kb < PREFIX_MOST // block, 0, kb)
-        each(first, kb + 1, functools.partial(step, masked=True))
-        each(kb + 1, length // block, functools.partial(step, masked=False))
-        grads_s[pl.ds(col0, block), hcols : 2 * hcols] = dk_acc[...].astype(BF16)
-        grads_s[pl.ds(col0, block), 2 * hcols : 3 * hcols] = dv_acc[...].astype(BF16)
-
-        @pl.when(kb == 0)
+        return fan(wop_all.at[me], wop_all.at[me], wopb_sems, to)
+
+    def attend_back(row0, seen_rows):
+        part = pl.ds(row0, block)
+        q = q_s[part, :]
+        grad = gctx_all[part, :]
+        product = grad.astype(F32) * ctx_s[part, :].astype(F32)
+        dq = []
+        for head in range(heads):
+            inner = dotf(ones[head], product, ((1,), (1,)), lax.Precision.HIGHEST)[0:1]
+            lse = lse_s[8 * head : 8 * head + 1, part]
+            q_head = pick_head(q, head)
+            grad_head = pick_head(grad, head)
+            dq_head = jnp.zeros((HEAD_DIM, block), F32)
+            for col0 in range(0, seen_rows, block):
+                keys = pl.ds(col0, block)
+                scores = dotf(k_s[keys, :], q_head, ((1,), (1,)))
+                soft = jnp.exp(hidden_keys(scores, row0, col0, 1) - lse)
+                grad_soft = dotf(v_s[keys, :], grad_head, ((1,), (1,)))
+                grad_scores = (soft * (grad_soft - inner)).astype(BF16)
+                dv_acc[keys, :] += dotf(soft.astype(BF16), grad_head)
+                dk_acc[keys, :] += dotf(grad_scores, q_head)
+                dq_head += dotf(kt_s[head * HEAD_DIM : (head + 1) * HEAD_DIM, keys], grad_scores)
+            dq.append(dq_head)
+        dq = jnp.transpose(jnp.concatenate(dq, axis=0))
+        grads_s[part, 0:hcols] = (dq * SCORE_SCALE).astype(BF16)
+
+    @pl.loop(0, TENSOR)
+    def _(turn):
+        blk = lax.rem(place + turn, TENSOR)
+
+        @pl.when(turn > 0)
         def _():
-            each(1, peers, lambda off: wop_copy(off).wait_recv())
+            back_copy(TENSOR - turn).wait_recv()
+
+        by_length(attend_back, blk)
+
+        @pl.when(turn == 1)
+        def _():
+            dwin_ring.start_sums()
+            dwout_ring.start_own()
+            dwout_ring.start_sums()
+            all_of(wop_in, wop_sems).wait_recv()
             total = jnp.zeros(wop_sum.shape[1:], F32)
             total = lax.fori_loop(0, peers, lambda off, acc: acc + wop_in[off].astype(F32), total)
             wop_sum[place] = total.astype(BF16)
             for off in (2, 1, 3):
                 wopz_copy(off).start()
 
-        @pl.when(kb == 1)
+        @pl.when(turn == 2)
         def _():
             for off in (2, 1, 3):
                 wopz_copy(off).wait_recv()
@@ -726,7 +746,8 @@
             wop_all[me] = total.astype(BF16)
             each(1, peers, lambda off: wopb_copy(off).start())
 
-    grads_s[:, 0:hcols] = (dq_acc[...] * SCORE_SCALE).astype(BF16)
+    grads_s[:, hcols : 2 * hcols] = dk_acc[...].astype(BF16)
+    grads_s[:, 2 * hcols : 3 * hcols] = dv_acc[...].astype(BF16)
 
     def partial_rows(owner, part):
         start = owner * rows + part * half
@@ -737,23 +758,32 @@
     rows_s[far, low] = partial_rows(far, 0).astype(BF16)
     rows_s[far, high] = partial_rows(far, 1).astype(BF16)
     row_ring.start_far()
+
+    def piece_copy(off):
+        to = lax.rem(me + off, peers)
+        return fan(piece_s.at[to], piece_in.at[off], piece_sems, to)
+
+    tall = width // ROW
+    count = tall // each_rows
+
+    @pl.loop(0, ROW)
+    def _(turn):
+        at = lax.rem(me // count + turn, ROW)
+        grads = dotf(seqt_s[block_of(at * tall, tall), :], grads_s[...]).astype(BF16)
+        for kind in range(3):
+            piece = grads[:, kind * hcols : (kind + 1) * hcols].reshape(count, each_rows, hcols)
+            piece_s[pl.ds(at * count, count), kind] = piece
+
+        def send(to):
+            off = lax.rem(to + peers - me, peers)
+            pl.when(off > 0)(lambda: piece_copy(off).start())
+
+        each(at * count, (at + 1) * count, send)
+
+    piece_in[0] = piece_s[me]
     rows_s[right, high] = partial_rows(right, 1).astype(BF16)
     rows_s[left, low] = partial_rows(left, 0).astype(BF16)
     row_ring.start_own()
-
-    @pl.loop(0, 3)
-    def _(at):
-        cols = block_of(at * hcols, hcols)
-        grad = dotf(seq_s[...], grads_s[:, cols], ((0,), (0,)))
-        piece_s[at] = grad.astype(BF16).reshape(peers, each_rows, hcols)
-
-    def piece_copy(off):
-        to = lax.rem(me + off, peers)
-        return remote(piece_s.at[:, to], piece_in.at[off], piece_sems, off, "expert", to)
-
-    each(1, peers, lambda off: piece_copy(off).start())
-    for at in range(3):
-        piece_in[0, at] = piece_s[at, me]
     rows_s[right, low] = partial_rows(right, 0).astype(BF16)
     rows_s[left, high] = partial_rows(left, 1).astype(BF16)
     row_ring.add_far()
@@ -761,18 +791,43 @@
     mine_s[low, :] = partial_rows(place, 0)
     mine_s[high, :] = partial_rows(place, 1)
 
-    each(1, peers, lambda off: piece_copy(off).wait_recv())
-    total = jnp.zeros(sum_s.shape, F32)
+    for ring in (tok_ring, win_ring, wout_ring, wo_ring, dwin_ring):
+        ring.drain()
+    for off in (2, 1, 3):
+        ctx_copy(off).wait_send()
+        back_copy(off).wait_send()
+        wopz_copy(off).wait_send()
+    all_of(out_s, mix_sems).wait_send()
+    all_of(done_s, ret_sems).wait_send()
+    all_of(wop_s, wop_sems).wait_send()
+    all_of(piece_in, piece_sems).wait_recv()
+    total = jnp.zeros(piece_in.shape[1:], F32)
     total = lax.fori_loop(0, peers, lambda off, acc: acc + piece_in[off].astype(F32), total)
-    sum_s[...] = total.astype(BF16)
+    sum_all[me] = total.astype(BF16)
 
     def sum_copy(off):
         to = lax.rem(me + off, peers)
-        return remote(sum_s, sum_all.at[:, me], sum_sems, off, "expert", to)
+        return fan(sum_all.at[me], sum_all.at[me], sum_sems, to)
 
     each(1, peers, lambda off: sum_copy(off).start())
-    for at in range(3):
-        sum_all[at, me] = sum_s[at]
+
+    cols = block_of(me * each_rows, each_rows)
+    along = jnp.zeros((each_rows, 1), F32)
+    for kind in range(3):
+        weight = w_s[cols, kind * hcols : (kind + 1) * hcols].astype(F32)
+        along = along + jnp.sum(total[kind] * weight, axis=1, keepdims=True)
+    first_s[place] = jnp.broadcast_to(along, (each_rows, 128))
+
+    def first_copy(off):
+        to = lax.rem(place + off, TENSOR)
+        return remote(first_s.at[place], first_s.at[place], first_sems, off, "tensor", to)
+
+    for off in (2, 1, 3):
+        first_copy(off).start()
+
+    def gain_copy(off):
+        to = lax.rem(me + off, peers)
+        return fan(gain_all.at[me], gain_all.at[me], gain_sems, to)
 
     dwin_ring.wait()
     dwout_ring.wait()
@@ -783,15 +838,23 @@
     wout_store = pltpu.make_async_copy(acc_s.at[1], dwout_ref, store_sems.at[2])
     win_store.start()
     wout_store.start()
-    each(1, peers, lambda off: wopb_copy(off).wait_recv())
+    all_of(wop_all, wopb_sems).wait_recv()
+    all_of(wop_all, wopb_sems).wait_send()
     count = peers // TENSOR
     go_ref[...] = wop_all[pl.ds(place * count, count), :, 0:width].reshape(hcols, width).astype(F32)
     small = wop_all[:, :, width : width + hcols].reshape(width, hcols)
     tall = width // blocks
-    kept_rows = small_ref.shape[0]
-    small_ref[...] = jnp.concatenate(
+    kept_rows = (experts + 1 + 15) // 16 * 16
+    sums = jnp.concatenate(
         [small[at * tall : at * tall + kept_rows] for at in range(blocks)], axis=1
     ).astype(F32)
+    router_ref[...] = sums[0:experts]
+    dsecond_ref[...] = sums[experts : experts + 1]
+
+    for off in (2, 1, 3):
+        first_copy(off).wait_recv()
+    gain_all[me] = first_s[0] + first_s[1] + first_s[2] + first_s[3]
+    each(1, peers, lambda off: gain_copy(off).start())
 
     row_ring.wait()
     for part in (low, high):
@@ -804,41 +867,19 @@
     tok_store = pltpu.make_async_copy(scaled_s, gtok_ref, store_sems.at[3])
     tok_store.start()
 
-    each(1, peers, lambda off: sum_copy(off).wait_recv())
-    dfirst = jnp.zeros((8, width), F32)
-    for at, grad_ref in enumerate((gq_ref, gk_ref, gv_ref)):
-        grad = sum_all[at].reshape(width, hcols).astype(F32)
-        grad_ref[...] = grad
-        product = grad * w_s[:, at * hcols : (at + 1) * hcols].astype(F32)
-        dfirst = dfirst + dotf(
-            jnp.ones((8, hcols), F32), product, ((1,), (1,)), lax.Precision.HIGHEST
-        )
-    first_s[place] = dfirst / gain_one[...]
-
-    def first_copy(off):
-        to = lax.rem(place + off, TENSOR)
-        return remote(first_s.at[place], first_s.at[place], first_sems, off, "tensor", to)
-
-    for off in (2, 1, 3):
-        first_copy(off).start()
-
-    for ring in (tok_ring, win_ring, wout_ring, wo_ring, dwin_ring, dwout_ring, row_ring):
-        ring.drain()
-    for off in (2, 1, 3):
-        ctx_copy(off).wait_send()
-        back_copy(off).wait_send()
-        wopz_copy(off).wait_send()
-
-    def drain(off):
-        for copy in (mix_copy, ret_copy, wop_copy, wopb_copy, piece_copy, sum_copy):
-            copy(off).wait_send()
-
-    each(1, peers, drain)
-    for off in (2, 1, 3):
-        first_copy(off).wait_recv()
-    dfirst_ref[...] = first_s[0] + first_s[1] + first_s[2] + first_s[3]
+    all_of(piece_s, piece_sems).wait_send()
     for off in (2, 1, 3):
         first_copy(off).wait_send()
+    dwout_ring.drain()
+    row_ring.drain()
+    all_of(sum_all, sum_sems).wait_recv()
+    for at, grad_ref in enumerate((gq_ref, gk_ref, gv_ref)):
+        grad_ref[...] = sum_all[:, at].reshape(width, hcols).astype(F32)
+    all_of(gain_all, gain_sems).wait_recv()
+    dfirst_ref[...] = jnp.transpose(gain_all[...].reshape(width, 128))[0:1] / gain_one[...]
+
+    all_of(sum_all, sum_sems).wait_send()
+    all_of(gain_all, gain_sems).wait_send()
     for store in (out_store, win_store, wout_store, tok_store):
         store.wait()
 
@@ -868,7 +909,6 @@
     def sems(count):
         return pltpu.SemaphoreType.DMA((2, count))
 
-    small_rows = (experts + 1 + 15) // 16 * 16
     return pl.pallas_call(
         functools.partial(layer_kernel, experts=experts, capacity=float(capacity)),
         out_shape=(
@@ -878,13 +918,14 @@
             dev(wq.shape, F32),
             dev(wq.shape, F32),
             dev(wo.shape, F32),
-            dev((small_rows, width), F32),
-            dev((8, width), F32),
+            dev((experts, width), F32),
+            dev((1, width), F32),
+            dev((1, width), F32),
             dev(win.shape, F32),
             dev(wout.shape, F32),
         ),
         in_specs=[SM] + [HB] * 13,
-        out_specs=(HB,) * 2 + (VM,) * 6 + (HB,) * 2,
+        out_specs=(HB,) * 2 + (VM,) * 7 + (HB,) * 2,
         scratch_shapes=[
             low(TENSOR, rows, width),
             full(1, width),
@@ -897,9 +938,10 @@
             full(rows, width),
             pltpu.VMEM(routes.shape, jnp.int32),
             pltpu.VMEM(prio.shape, jnp.int32),
-            low(length, width),
+            low(width, length),
             low(length, hcols),
             low(length, hcols),
+            low(hcols, length),
             low(length, hcols),
             low(rows, wide),
             low(length, hcols),
@@ -935,44 +977,77 @@
             low(TENSOR, each_rows, width + hcols),
             low(peers, each_rows, width + hcols),
             full(length, hcols),
-            full(rows, hcols),
-            full(rows, hcols),
-            full(8 * heads, length),
+            full(length, hcols),
             low(length, 3 * hcols),
             low(TENSOR, rows, width),
             low(rows, width),
             low(2, rows, width),
             full(rows, width),
-            low(3, peers, each_rows, hcols),
             low(peers, 3, each_rows, hcols),
-            low(3, each_rows, hcols),
-            low(3, peers, each_rows, hcols),
-            full(TENSOR, 8, width),
+            low(peers, 3, each_rows, hcols),
+            low(peers, 3, each_rows, hcols),
+            full(TENSOR, each_rows, 128),
+            full(peers, each_rows, 128),
             pltpu.SemaphoreType.DMA((13,)),
             pltpu.SemaphoreType.DMA((4,)),
+            pltpu.SemaphoreType.REGULAR,
             sems(6),
             sems(6),
             sems(6),
             sems(6),
             sems(TENSOR),
-            sems(peers),
-            sems(peers),
+            pltpu.SemaphoreType.DMA((1 + wide // 128,)),
+            pltpu.SemaphoreType.DMA((2,)),
             sems(TENSOR),
             sems(6),
             sems(6),
-            sems(peers),
+            pltpu.SemaphoreType.DMA((2,)),
             sems(TENSOR),
-            sems(peers),
+            pltpu.SemaphoreType.DMA((2,)),
             sems(6),
-            sems(peers),
-            sems(peers),
+            pltpu.SemaphoreType.DMA((2,)),
+            pltpu.SemaphoreType.DMA((2,)),
             sems(TENSOR),
+            pltpu.SemaphoreType.DMA((2,)),
         ],
         compiler_params=pltpu.CompilerParams(
             collective_id=0, has_side_effects=True, vmem_limit_bytes=VMEM_BYTES
         ),
         name="layer",
     )(prefix, tokens, gain_one, gain_two, wq, wk, wv, wo, router, win, wout, cot, routes, prio)
+
+
+def write_kernel(*refs):
+    count = (len(refs) - 2) // 3
+    in_sems, out_sems = refs[-2:]
+    loads = [
+        pltpu.make_async_copy(refs[at], refs[2 * count + at], in_sems.at[at]) for at in range(count)
+    ]
+    stores = [
+        pltpu.make_async_copy(refs[2 * count + at], refs[count + at], out_sems.at[at])
+        for at in range(count)
+    ]
+    for load in loads:
+        load.start()
+    for load, store in zip(loads, stores):
+        load.wait()
+        store.start()
+    for store in stores:
+        store.wait()
+
+
+def write_out(results):
+    count = len(results)
+    return pl.pallas_call(
+        write_kernel,
+        out_shape=tuple(jax.ShapeDtypeStruct(x.shape, x.dtype) for x in results),
+        in_specs=[HB] * count,
+        out_specs=(HB,) * count,
+        scratch_shapes=[pltpu.VMEM(x.shape, x.dtype) for x in results]
+        + [pltpu.SemaphoreType.DMA((count,)), pltpu.SemaphoreType.DMA((count,))],
+        compiler_params=pltpu.CompilerParams(vmem_limit_bytes=VMEM_BYTES),
+        name="write_out",
+    )(*results)
 
 
 def body(
@@ -992,8 +1067,7 @@
     prefix_len,
 ):
     width = tokens.shape[1]
-    experts = router_weight.shape[1]
-    out, gtok, gq, gk, gv, go, small, dfirst, dwin, dwout = layer(
+    results = layer(
         prefix_len,
         tokens,
         first_gain.reshape(1, width),
@@ -1009,16 +1083,17 @@
         routes.T,
         priority,
     )
+    out, gtok, gq, gk, gv, go, grouter, dsecond, dfirst, dwin, dwout = write_out(results)
     return (
         out,
         gtok,
-        dfirst[0],
-        small[experts],
+        dfirst.reshape(width),
+        dsecond.reshape(width),
         gq,
         gk,
         gv,
         go,
-        small[:experts].T,
+        grouter.T,
         dwin[None],
         dwout[None],
     )

time: 181 us -> 163 us (0.901); the launches traced: 178 us -> 163 us
  local copies, waits for them, and re-layouts: 12.8 us -> 0 us
  Pallas kernels: 164 us -> 162 us
    unnamed x22 -> x0, local copies, waits for them, and re-layouts: 8.67 us -> none
    pallas_call x1, Pallas kernels: 164 us -> 157 us  [layer(): pl.pallas_call(functools.partial(layer_kernel, experts=experts, capacity=...]
    pallas_call x0 -> x1, Pallas kernels: none -> 4.29 us  [write_out(): pl.pallas_call(write_kernel, out_shape=tuple((jax.ShapeDtypeStruct(x.shap...]
    slice x2 -> x0, local copies, waits for them, and re-layouts: 2.68 us -> none  [the longest x1 1.38 us: body(): dfirst[0]]
where the time goes in v3:
time: 163 us
  Pallas kernels  162 us (99%)
    pallas_call x1, Pallas kernels, layer(): pl.pallas_call(functools.partial(layer_kernel, experts=experts, capacity=...  157 us
    pallas_call x1, Pallas kernels, write_out(): pl.pallas_call(write_kernel, out_shape=tuple((jax.ShapeDtypeStruct(x.shap...  4.29 us

profile of v3, /device:TPU:1, one launch (start us, length us, event | category | flops | bytes accessed | tf_op | source)
XLA Modules:
  0.0 163.0 jit_solution(18087449127482127512)
XLA Ops:
  1.3 157.2 %layer.1 = (bf16[512,512]{1,0:T(8,128)(2,1)}, f32[512,512]{1,0:T(8,128)}, f32[512,128]{1,0:T(8,128)}, f32[512,128]{1,0:T(8,128)}, f32[512,128]{1,0:T(8,128)}, /*...) custom-call(s32[1]{0:T(128)S(6)} %copy.25.prefix_ref, ...), custom_call_target="tpu_custom_call" | custom-call | tf_op jit(solution)/shard_map/layer/pallas_call | solution.py:912
  158.5 4.3 %write_out.1 = (bf16[512,512]{1,0:T(8,128)(2,1)}, f32[512,512]{1,0:T(8,128)}, f32[512,128]{1,0:T(8,128)}, f32[512,128]{1,0:T(8,128)}, f32[512,128]{1,0:T(8,128)}...) custom-call(bf16[512,512]{1,0:T(8,128)(2,1)} %get-tuple-element.33.r, ...), custom_call_target="tpu_custom_call" | custom-call | tf_op jit(solution)/shard_map/write_out/pallas_call | solution.py:1041

commit v4 on v3

--- a/solution.py
+++ b/solution.py
@@ -103,11 +103,12 @@
 
 
 class Gather:
-    def __init__(self, buf, sems, place):
+    def __init__(self, buf, sems, place, eighths=4):
         self.buf, self.sems, self.place = buf, sems, place
         self.right, self.left = lax.rem(place + 1, TENSOR), lax.rem(place + TENSOR - 1, TENSOR)
-        half = buf.shape[1] // 2
-        self.low, self.high = pl.ds(0, half), pl.ds(half, half)
+        size = buf.shape[1]
+        cut = size * eighths // 8
+        self.low, self.high = pl.ds(0, cut), pl.ds(cut, size - cut)
 
     def copy(self, slot):
         owner, part, to = (
@@ -269,8 +270,11 @@
     land_win,
     land_wout,
     wop_s,
-    wop_in,
+    wop_row,
+    col_s,
+    wop_col,
     wop_sum,
+    col_all,
     wop_all,
     dk_acc,
     dv_acc,
@@ -298,6 +302,8 @@
     dwin_sems,
     dwout_sems,
     wop_sems,
+    col_sems,
+    colb_sems,
     wopz_sems,
     wopb_sems,
     row_sems,
@@ -343,14 +349,14 @@
         load.start()
 
     def all_of(buf, sems):
-        most = buf.at[pl.ds(1, peers - 1)]
+        most = buf.at[pl.ds(1, buf.shape[0] - 1)]
         return fan(most, most, sems, lax.rem(me + 1, peers))
 
     batch = 128 // groups
 
     tok_ring = Gather(tok_s, tok_sems, place)
-    win_ring = Gather(win_s, win_sems, place)
-    wout_ring = Gather(wout_s, wout_sems, place)
+    win_ring = Gather(win_s, win_sems, place, 4)
+    wout_ring = Gather(wout_s, wout_sems, place, 4)
     wo_ring = Gather(wo_s, wo_sems, place)
     loads[0].wait()
     pl.semaphore_wait(pltpu.get_barrier_semaphore(), greeted)
@@ -527,9 +533,10 @@
         to = lax.rem(me + peers - off, peers)
         return fan(done_s.at[off], ret_s.at[me], ret_sems, to)
 
-    def expert_part(chunk, slices, start):
-        part = block_of(chunk * 128, 128)
-        rows_in = in_s[pl.ds(chunk * batch, batch)].reshape(128, 2 * width)
+    def expert_part(chunk, slices, start, count=128):
+        part = block_of(chunk * count, count)
+        sources = count // groups
+        rows_in = in_s[pl.ds(chunk * sources, sources)].reshape(count, 2 * width)
         grad = rows_in[:, 0:width]
         mixed = rows_in[:, width : 2 * width]
         for at in slices:
@@ -574,21 +581,21 @@
 
     wout_ring.wait_near()
 
-    @pl.loop(0, 2 * peers // batch)
+    @pl.loop(0, peers // batch)
     def _(turn):
-        expert_part(turn // 2, (3 - 2 * lax.rem(turn, 2),), False)
+        expert_part(turn // 2, (3 - 2 * lax.rem(turn, 2),), False, 256)
 
     win_ring.wait_far()
     wout_ring.wait_far()
 
-    @pl.loop(0, peers // batch)
+    @pl.loop(0, peers // (2 * batch))
     def _(chunk):
-        expert_part(chunk, (2,), False)
-        part = block_of(chunk * 128, 128)
-        begin = chunk * batch
+        expert_part(chunk, (2,), False, 256)
+        part = block_of(chunk * 256, 256)
+        begin = chunk * 2 * batch
         done = jnp.concatenate([acc_s[0, part, :], acc_s[1, part, :]], axis=1).astype(BF16)
-        done_s[pl.ds(begin, batch)] = done.reshape(batch, groups, 2 * width)
-        each(jnp.maximum(begin, 1), begin + batch, lambda off: ret_copy(off).start())
+        done_s[pl.ds(begin, 2 * batch)] = done.reshape(2 * batch, groups, 2 * width)
+        each(jnp.maximum(begin, 1), begin + 2 * batch, lambda off: ret_copy(off).start())
 
     ret_s[me] = done_s[0]
 
@@ -615,6 +622,8 @@
 
     dgain_s[...] = jnp.zeros_like(dgain_s)
     from_wide = one_hot(iota((wide, experts), 0) // groups == iota((wide, experts), 1))
+
+    step_rows = 256
 
     @pl.loop(0, rows // step_rows)
     def _(step):
@@ -647,8 +656,10 @@
         dst = gctx_all.at[block_of(place * rows, rows), :]
         return remote(gctx_s.at[to], dst, back_sems, off, "tensor", to)
 
-    for off in (2, 1, 3):
+    for off in (3, 2, 1):
         back_copy(off).start()
+    dwin_ring.add_far()
+    dwin_ring.start_sums()
     out_store = pltpu.make_async_copy(kept_s, out_ref, store_sems.at[0])
     out_store.start()
     gctx_all[block_of(place * rows, rows), :] = gctx_s[place]
@@ -656,25 +667,38 @@
     each_rows = width // peers
     for at in range(TENSOR):
         grad_wo = dotf(ctx_all[at], gatt_s[...], ((0,), (0,))).astype(BF16)
-        count = peers // TENSOR
-        wop_s[at * count : (at + 1) * count, :, 0:width] = grad_wo.reshape(count, each_rows, width)
+        wop_s[:, at, :, 0:width] = grad_wo.reshape(ROW, each_rows, width)
     grad_router = dotf(glog_s[...], pair_s[:, width : 2 * width], ((0,), (0,)))
     blocks = width // hcols
     small_rows = jnp.concatenate(
         [grad_router, dgain_s[...], jnp.zeros((width // blocks - experts - 1, width), F32)], axis=0
     ).astype(BF16)
-    small_tall = jnp.concatenate(
-        [small_rows[:, at * hcols : (at + 1) * hcols] for at in range(blocks)], axis=0
-    )
-    wop_s[:, :, width : width + hcols] = small_tall.reshape(peers, each_rows, hcols)
+    for at in range(blocks):
+        small = small_rows[:, at * hcols : (at + 1) * hcols]
+        wop_s[:, at, :, width : width + hcols] = small.reshape(ROW, each_rows, hcols)
+
+    my_row, my_col = me // ROW, lax.rem(me, ROW)
+
+    def to_row(off, sems, src, dst):
+        return fan(src, dst, sems, my_row * ROW + lax.rem(me + off, ROW))
 
     def wop_copy(off):
-        to = lax.rem(me + off, peers)
-        return fan(wop_s.at[to], wop_in.at[off], wop_sems, to)
-
-    each(1, peers, lambda off: wop_copy(off).start())
-    wop_in[0] = wop_s[me]
-    dwin_ring.add_far()
+        return to_row(off, wop_sems, wop_s.at[lax.rem(me + off, ROW)], wop_row.at[off])
+
+    def col_copy(off):
+        to = lax.rem(me + off * ROW, peers)
+        return fan(col_s.at[to // ROW], wop_col.at[off], col_sems, to)
+
+    def colb_copy(off):
+        to = lax.rem(me + off * ROW, peers)
+        return fan(col_all.at[my_row], col_all.at[my_row], colb_sems, to)
+
+    def wopb_copy(off):
+        return to_row(off, wopb_sems, col_all, wop_all.at[my_col])
+
+    cols = peers // ROW
+    each(1, ROW, lambda off: wop_copy(off).start())
+    wop_row[0] = wop_s[my_col]
     dwout_ring.add_far()
 
     dk_acc[...] = jnp.zeros_like(dk_acc)
@@ -684,10 +708,6 @@
     def wopz_copy(off):
         to = lax.rem(place + off, TENSOR)
         return remote(wop_sum.at[place], wop_sum.at[place], wopz_sems, off, "tensor", to)
-
-    def wopb_copy(off):
-        to = lax.rem(me + off, peers)
-        return fan(wop_all.at[me], wop_all.at[me], wopb_sems, to)
 
     def attend_back(row0, seen_rows):
         part = pl.ds(row0, block)
@@ -724,14 +744,23 @@
 
         by_length(attend_back, blk)
 
+        @pl.when(turn == 0)
+        def _():
+            dwout_ring.start_own()
+            all_of(wop_row, wop_sems).wait_recv()
+            total = jnp.zeros(col_s.shape, F32)
+            total = lax.fori_loop(0, ROW, lambda off, acc: acc + wop_row[off].astype(F32), total)
+            col_s[...] = total.astype(BF16)
+            each(1, cols, lambda off: col_copy(off).start())
+            wop_col[0] = col_s[my_row]
+
         @pl.when(turn == 1)
         def _():
-            dwin_ring.start_sums()
-            dwout_ring.start_own()
             dwout_ring.start_sums()
-            all_of(wop_in, wop_sems).wait_recv()
+            all_of(wop_col, col_sems).wait_recv()
             total = jnp.zeros(wop_sum.shape[1:], F32)
-            total = lax.fori_loop(0, peers, lambda off, acc: acc + wop_in[off].astype(F32), total)
+            for at in range(cols):
+                total = total + wop_col[at].astype(F32)
             wop_sum[place] = total.astype(BF16)
             for off in (2, 1, 3):
                 wopz_copy(off).start()
@@ -743,8 +772,14 @@
             total = jnp.zeros(wop_sum.shape[1:], F32)
             for at in range(TENSOR):
                 total = total + wop_sum[at].astype(F32)
-            wop_all[me] = total.astype(BF16)
-            each(1, peers, lambda off: wopb_copy(off).start())
+            col_all[my_row] = total.astype(BF16)
+            each(1, cols, lambda off: colb_copy(off).start())
+
+        @pl.when(turn == 3)
+        def _():
+            all_of(col_all, colb_sems).wait_recv()
+            each(1, ROW, lambda off: wopb_copy(off).start())
+            wop_all[my_col] = col_all[...]
 
     grads_s[:, hcols : 2 * hcols] = dk_acc[...].astype(BF16)
     grads_s[:, 2 * hcols : 3 * hcols] = dv_acc[...].astype(BF16)
@@ -800,6 +835,8 @@
     all_of(out_s, mix_sems).wait_send()
     all_of(done_s, ret_sems).wait_send()
     all_of(wop_s, wop_sems).wait_send()
+    all_of(wop_col, col_sems).wait_send()
+    all_of(col_all, colb_sems).wait_send()
     all_of(piece_in, piece_sems).wait_recv()
     total = jnp.zeros(piece_in.shape[1:], F32)
     total = lax.fori_loop(0, peers, lambda off, acc: acc + piece_in[off].astype(F32), total)
@@ -840,13 +877,14 @@
     wout_store.start()
     all_of(wop_all, wopb_sems).wait_recv()
     all_of(wop_all, wopb_sems).wait_send()
-    count = peers // TENSOR
-    go_ref[...] = wop_all[pl.ds(place * count, count), :, 0:width].reshape(hcols, width).astype(F32)
-    small = wop_all[:, :, width : width + hcols].reshape(width, hcols)
-    tall = width // blocks
+    go_ref[...] = wop_all[:, place, :, 0:width].reshape(hcols, width).astype(F32)
     kept_rows = (experts + 1 + 15) // 16 * 16
     sums = jnp.concatenate(
-        [small[at * tall : at * tall + kept_rows] for at in range(blocks)], axis=1
+        [
+            wop_all[:, at, :, width : width + hcols].reshape(ROW * each_rows, hcols)[:kept_rows]
+            for at in range(blocks)
+        ],
+        axis=1,
     ).astype(F32)
     router_ref[...] = sums[0:experts]
     dsecond_ref[...] = sums[experts : experts + 1]
@@ -972,10 +1010,13 @@
             low(fcols, width),
             low(2, width, fcols),
             low(2, fcols, width),
-            low(peers, each_rows, width + hcols),
-            low(peers, each_rows, width + hcols),
+            low(ROW, peers // ROW, each_rows, width + hcols),
+            low(ROW, peers // ROW, each_rows, width + hcols),
+            low(peers // ROW, each_rows, width + hcols),
+            low(peers // ROW, each_rows, width + hcols),
             low(TENSOR, each_rows, width + hcols),
-            low(peers, each_rows, width + hcols),
+            low(peers // ROW, each_rows, width + hcols),
+            low(ROW, peers // ROW, each_rows, width + hcols),
             full(length, hcols),
             full(length, hcols),
             low(length, 3 * hcols),
@@ -1001,6 +1042,8 @@
             sems(TENSOR),
             sems(6),
             sems(6),
+            pltpu.SemaphoreType.DMA((2,)),
+            pltpu.SemaphoreType.DMA((2,)),
             pltpu.SemaphoreType.DMA((2,)),
             sems(TENSOR),
             pltpu.SemaphoreType.DMA((2,)),

time: 163 us -> 157 us (0.963)
  Pallas kernels: 162 us -> 155 us
    pallas_call x1, Pallas kernels: 157 us -> 151 us  [layer(): pl.pallas_call(functools.partial(layer_kernel, experts=experts, capacity=...]
where the time goes in v4:
time: 157 us
  Pallas kernels  155 us (99%)
    pallas_call x1, Pallas kernels, layer(): pl.pallas_call(functools.partial(layer_kernel, experts=experts, capacity=...  151 us
    pallas_call x1, Pallas kernels, write_out(): pl.pallas_call(write_kernel, out_shape=tuple((jax.ShapeDtypeStruct(x.shap...  4.29 us

profile of v4, /device:TPU:1, one launch (start us, length us, event | category | flops | bytes accessed | tf_op | source)
XLA Modules:
  0.0 156.6 jit_solution(12345643904893541685)
XLA Ops:
  1.3 150.8 %layer.1 = (bf16[512,512]{1,0:T(8,128)(2,1)}, f32[512,512]{1,0:T(8,128)}, f32[512,128]{1,0:T(8,128)}, f32[512,128]{1,0:T(8,128)}, f32[512,128]{1,0:T(8,128)}, /*...) custom-call(s32[1]{0:T(128)S(6)} %copy.25.prefix_ref, ...), custom_call_target="tpu_custom_call" | custom-call | tf_op jit(solution)/shard_map/layer/pallas_call | solution.py:950
  152.1 4.3 %write_out.1 = (bf16[512,512]{1,0:T(8,128)(2,1)}, f32[512,512]{1,0:T(8,128)}, f32[512,128]{1,0:T(8,128)}, f32[512,128]{1,0:T(8,128)}, f32[512,128]{1,0:T(8,128)}...) custom-call(bf16[512,512]{1,0:T(8,128)(2,1)} %get-tuple-element.33.r, ...), custom_call_target="tpu_custom_call" | custom-call | tf_op jit(solution)/shard_map/write_out/pallas_call | solution.py:1084

commit v5 on v4

--- a/solution.py
+++ b/solution.py
@@ -423,11 +423,11 @@
     def hidden_keys(scores, row0, col0, row_axis):
         if isinstance(row0, int) and col0 + block - 1 <= row0:
             return scores
-        row_ids = iota((block, block), row_axis) + row0
-        col_ids = iota((block, block), 1 - row_axis) + col0
-        seen = col_ids <= row_ids
+        line = (block, 1) if row_axis == 0 else (1, block)
+        until = iota(line, row_axis) + (row0 + 1 - col0)
         if col0 < PREFIX_MOST:
-            seen = seen | (col_ids < prefix)
+            until = jnp.maximum(until, prefix - col0)
+        seen = iota((block, block), 1 - row_axis) < until
         return jnp.where(seen, scores, NEG)
 
     def ctx_copy(off):
@@ -618,6 +618,7 @@
             dwout_ring.start_far()
 
     dwin_ring.start_own()
+    dwout_ring.start_own()
     all_of(ret_s, ret_sems).wait_recv()
 
     dgain_s[...] = jnp.zeros_like(dgain_s)
@@ -714,23 +715,29 @@
         q = q_s[part, :]
         grad = gctx_all[part, :]
         product = grad.astype(F32) * ctx_s[part, :].astype(F32)
-        dq = []
-        for head in range(heads):
-            inner = dotf(ones[head], product, ((1,), (1,)), lax.Precision.HIGHEST)[0:1]
-            lse = lse_s[8 * head : 8 * head + 1, part]
-            q_head = pick_head(q, head)
-            grad_head = pick_head(grad, head)
-            dq_head = jnp.zeros((HEAD_DIM, block), F32)
-            for col0 in range(0, seen_rows, block):
-                keys = pl.ds(col0, block)
-                scores = dotf(k_s[keys, :], q_head, ((1,), (1,)))
-                soft = jnp.exp(hidden_keys(scores, row0, col0, 1) - lse)
-                grad_soft = dotf(v_s[keys, :], grad_head, ((1,), (1,)))
-                grad_scores = (soft * (grad_soft - inner)).astype(BF16)
-                dv_acc[keys, :] += dotf(soft.astype(BF16), grad_head)
-                dk_acc[keys, :] += dotf(grad_scores, q_head)
-                dq_head += dotf(kt_s[head * HEAD_DIM : (head + 1) * HEAD_DIM, keys], grad_scores)
-            dq.append(dq_head)
+        inner = [
+            dotf(ones[head], product, ((1,), (1,)), lax.Precision.HIGHEST)[0:1]
+            for head in range(heads)
+        ]
+        lse = [lse_s[8 * head : 8 * head + 1, part] for head in range(heads)]
+        q_heads = [pick_head(q, head) for head in range(heads)]
+        grad_heads = [pick_head(grad, head) for head in range(heads)]
+        dq = [jnp.zeros((HEAD_DIM, block), F32) for head in range(heads)]
+        for col0 in range(0, seen_rows, block):
+            keys = pl.ds(col0, block)
+            dk = dk_acc[keys, :]
+            dv = dv_acc[keys, :]
+            for head in range(heads):
+                scores = dotf(k_s[keys, :], q_heads[head], ((1,), (1,)))
+                soft = jnp.exp(hidden_keys(scores, row0, col0, 1) - lse[head])
+                grad_soft = dotf(v_s[keys, :], grad_heads[head], ((1,), (1,)))
+                grad_scores = (soft * (grad_soft - inner[head])).astype(BF16)
+                dv += dotf(soft.astype(BF16), grad_heads[head])
+                dk += dotf(grad_scores, q_heads[head])
+                lanes = slice(head * HEAD_DIM, (head + 1) * HEAD_DIM)
+                dq[head] += dotf(kt_s[lanes, keys], grad_scores)
+            dk_acc[keys, :] = dk
+            dv_acc[keys, :] = dv
         dq = jnp.transpose(jnp.concatenate(dq, axis=0))
         grads_s[part, 0:hcols] = (dq * SCORE_SCALE).astype(BF16)
 
@@ -746,7 +753,7 @@
 
         @pl.when(turn == 0)
         def _():
-            dwout_ring.start_own()
+            dwout_ring.start_sums()
             all_of(wop_row, wop_sems).wait_recv()
             total = jnp.zeros(col_s.shape, F32)
             total = lax.fori_loop(0, ROW, lambda off, acc: acc + wop_row[off].astype(F32), total)
@@ -756,7 +763,6 @@
 
         @pl.when(turn == 1)
         def _():
-            dwout_ring.start_sums()
             all_of(wop_col, col_sems).wait_recv()
             total = jnp.zeros(wop_sum.shape[1:], F32)
             for at in range(cols):

time: 157 us -> 156 us (level)
  no operation moved by 1% of the time
where the time goes in v5:
time: 156 us
  Pallas kernels  155 us (99%)
    pallas_call x1, Pallas kernels, layer(): pl.pallas_call(functools.partial(layer_kernel, experts=experts, capacity=...  150 us
    pallas_call x1, Pallas kernels, write_out(): pl.pallas_call(write_kernel, out_shape=tuple((jax.ShapeDtypeStruct(x.shap...  4.29 us

profile of v5, /device:TPU:1, one launch (start us, length us, event | category | flops | bytes accessed | tf_op | source)
XLA Modules:
  0.0 156.1 jit_solution(4648487889475209485)
XLA Ops:
  1.3 150.3 %layer.1 = (bf16[512,512]{1,0:T(8,128)(2,1)}, f32[512,512]{1,0:T(8,128)}, f32[512,128]{1,0:T(8,128)}, f32[512,128]{1,0:T(8,128)}, f32[512,128]{1,0:T(8,128)}, /*...) custom-call(s32[1]{0:T(128)S(6)} %copy.25.prefix_ref, ...), custom_call_target="tpu_custom_call" | custom-call | tf_op jit(solution)/shard_map/layer/pallas_call | solution.py:956
  151.6 4.3 %write_out.1 = (bf16[512,512]{1,0:T(8,128)(2,1)}, f32[512,512]{1,0:T(8,128)}, f32[512,128]{1,0:T(8,128)}, f32[512,128]{1,0:T(8,128)}, f32[512,128]{1,0:T(8,128)}...) custom-call(bf16[512,512]{1,0:T(8,128)(2,1)} %get-tuple-element.33.r, ...), custom_call_target="tpu_custom_call" | custom-call | tf_op jit(solution)/shard_map/write_out/pallas_call | solution.py:1090

commit v6 on v5

--- a/solution.py
+++ b/solution.py
@@ -479,9 +479,9 @@
         def _():
             wo_ring.forward()
 
+    wout_ring.start((0, 1))
+    win_ring.forward()
     win_ring.start((2, 3))
-    win_ring.forward()
-    wout_ring.start()
     ctx_all[place] = ctx_s[block_of(place * rows, rows), :]
     for load in loads[10:]:
         load.wait()
@@ -528,6 +528,7 @@
     pl.semaphore_wait(plane_sem, peers // ROW - 1)
     each(1, peers, lambda off: mix_copy(off).start())
     in_s[0] = out_s[me]
+    wout_ring.start((2, 3))
 
     def ret_copy(off):
         to = lax.rem(me + peers - off, peers)
@@ -575,7 +576,7 @@
 
         expert_part(chunk, (0,), True)
 
-        @pl.when(chunk == 2)
+        @pl.when(chunk == 1)
         def _():
             wout_ring.forward()
 

time: 156 us -> 155 us (level)
  no operation moved by 1% of the time
where the time goes in v6:
time: 155 us
  Pallas kernels  154 us (99%)
    pallas_call x1, Pallas kernels, layer(): pl.pallas_call(functools.partial(layer_kernel, experts=experts, capacity=...  149 us
    pallas_call x1, Pallas kernels, write_out(): pl.pallas_call(write_kernel, out_shape=tuple((jax.ShapeDtypeStruct(x.shap...  4.29 us

profile of v6, /device:TPU:1, one launch (start us, length us, event | category | flops | bytes accessed | tf_op | source)
XLA Modules:
  0.0 155.1 jit_solution(4713487783736276473)
XLA Ops:
  1.3 149.3 %layer.1 = (bf16[512,512]{1,0:T(8,128)(2,1)}, f32[512,512]{1,0:T(8,128)}, f32[512,128]{1,0:T(8,128)}, f32[512,128]{1,0:T(8,128)}, f32[512,128]{1,0:T(8,128)}, /*...) custom-call(s32[1]{0:T(128)S(6)} %copy.25.prefix_ref, ...), custom_call_target="tpu_custom_call" | custom-call | tf_op jit(solution)/shard_map/layer/pallas_call | solution.py:957
  150.6 4.3 %write_out.1 = (bf16[512,512]{1,0:T(8,128)(2,1)}, f32[512,512]{1,0:T(8,128)}, f32[512,128]{1,0:T(8,128)}, f32[512,128]{1,0:T(8,128)}, f32[512,128]{1,0:T(8,128)}...) custom-call(bf16[512,512]{1,0:T(8,128)(2,1)} %get-tuple-element.33.r, ...), custom_call_target="tpu_custom_call" | custom-call | tf_op jit(solution)/shard_map/write_out/pallas_call | solution.py:1091

commit v7 on v6

--- a/solution.py
+++ b/solution.py
@@ -576,7 +576,7 @@
 
         expert_part(chunk, (0,), True)
 
-        @pl.when(chunk == 1)
+        @pl.when(chunk == 0)
         def _():
             wout_ring.forward()
 

time: 155 us -> 155 us (level)
  no operation moved by 1% of the time
where the time goes in v7:
time: 155 us
  Pallas kernels  153 us (99%)
    pallas_call x1, Pallas kernels, layer(): pl.pallas_call(functools.partial(layer_kernel, experts=experts, capacity=...  149 us
    pallas_call x1, Pallas kernels, write_out(): pl.pallas_call(write_kernel, out_shape=tuple((jax.ShapeDtypeStruct(x.shap...  4.29 us

profile of v7, /device:TPU:1, one launch (start us, length us, event | category | flops | bytes accessed | tf_op | source)
XLA Modules:
  0.0 154.9 jit_solution(4476037120634462152)
XLA Ops:
  1.3 149.1 %layer.1 = (bf16[512,512]{1,0:T(8,128)(2,1)}, f32[512,512]{1,0:T(8,128)}, f32[512,128]{1,0:T(8,128)}, f32[512,128]{1,0:T(8,128)}, f32[512,128]{1,0:T(8,128)}, /*...) custom-call(s32[1]{0:T(128)S(6)} %copy.25.prefix_ref, ...), custom_call_target="tpu_custom_call" | custom-call | tf_op jit(solution)/shard_map/layer/pallas_call | solution.py:957
  150.4 4.3 %write_out.1 = (bf16[512,512]{1,0:T(8,128)(2,1)}, f32[512,512]{1,0:T(8,128)}, f32[512,128]{1,0:T(8,128)}, f32[512,128]{1,0:T(8,128)}, f32[512,128]{1,0:T(8,128)}...) custom-call(bf16[512,512]{1,0:T(8,128)(2,1)} %get-tuple-element.33.r, ...), custom_call_target="tpu_custom_call" | custom-call | tf_op jit(solution)/shard_map/write_out/pallas_call | solution.py:1091
